TPU v7x, 128 devices: a whole 4x4x4 slice. The times are simulated.
128 devices in a mesh: dp: 4 (over x), ctx: 32 (over y, z, core).
Axes of the slice: x: 4, y: 4, z: 4, core: 2. Of those that a mesh axis runs over, the one named last changes fastest.
Arguments:
- normed_layer_input: bfloat16 [4, 4096, 8192], P('dp', 'ctx'), may hold values from -6 to 6
- frozen_query_rows: bfloat16 [4, 4096, 8192], P('dp', 'ctx'), may hold values from -160 to 160
- projected_keys: bfloat16 [4, 4096, 1024], P('dp', 'ctx'), may hold values from -7 to 7
- projected_values: bfloat16 [4, 4096, 1024], P('dp', 'ctx'), may hold values from -6 to 6
- output_gradient: bfloat16 [4, 4096, 8192], P('dp', 'ctx'), may hold values from -6 to 6
- adapter_down: bfloat16 [8192, 16], replicated, may hold values from -0.0625 to 0.0625
- adapter_up: bfloat16 [16, 8192], replicated, may hold values from -1.5 to 1.5
- langevin_down_noise: float32 [8192, 16], replicated, may hold values from -1.8 to 1.8
- langevin_up_noise: float32 [16, 8192], replicated, may hold values from -0.6 to 0.6
- listed_key_blocks: int32 [64, 32, 12], replicated, may hold values from 0 to 31, as said below
- head_live_slots: int32 [64], replicated, may hold values from 4 to 12, as said below
Outputs:
- attention: bfloat16 [4, 4096, 8192], P('dp', 'ctx')
- step_down: float32 [8192, 16], replicated
- step_up: float32 [16, 8192], replicated
Inputs may be any that keep to these rules, and one draw needn't show every extreme that they name: `listed_key_blocks`: slot 0 of block b's list is b, slot 1 is b - 1, slot 2 is b + 1 (modulo 32), slot 3 is block 0, for every head; the other slots are any blocks. `head_live_slots`: each count is a multiple of 4.
All inputs are finite; a program needn't handle non-finite values.
Results may differ from a plain program's by a relative error of at most 0.013.
Values may be sent and summed in bfloat16 or wider, within the bound.
No kernel may reach another device: no remote copies, remote signals or barrier semaphores. Data moves between devices by JAX's collectives and lax.ppermute only.
A program may use at most 128 MiB of HBM per device.

v0:
```python
import jax
import jax.numpy as jnp
from jax import lax
from jax.sharding import PartitionSpec as P

HEAD_SIZE = 128
G = 8
HEADS_OWN = 2
BLK = 128
NBMAX = 12


ADAPTER_GAIN = 2.0
MASK_VALUE = -1e30


def attention_weights(queries, key_rows, live_mask):
    scaling = queries.shape[-1] ** (-0.5)
    scores = (
        jnp.einsum("gqd,gkd->gqk", queries, key_rows, preferred_element_type=jnp.float32) * scaling
    )
    scores = jnp.where(live_mask[:, None, :], scores, MASK_VALUE)
    largest = jnp.max(scores, axis=-1, keepdims=True)
    shifted = jnp.exp(scores - largest)
    return shifted / jnp.sum(shifted, axis=-1, keepdims=True)


def forward_part(weights, value_rows):
    weights_low = weights.astype(jnp.bfloat16)
    return jnp.einsum(
        "gqk,gkd->gqd", weights_low, value_rows, preferred_element_type=jnp.float32
    ).astype(jnp.bfloat16)


def backward_part(weights, cotangent, key_rows, value_rows):
    scaling = key_rows.shape[-1] ** (-0.5)
    weight_grad = jnp.einsum(
        "gqd,gkd->gqk", cotangent, value_rows, preferred_element_type=jnp.float32
    )
    row_inner = jnp.sum(weights * weight_grad, axis=-1, keepdims=True)
    score_grad = (weights * (weight_grad - row_inner)).astype(jnp.bfloat16)
    return (
        jnp.einsum("gqk,gkd->gqd", score_grad, key_rows, preferred_element_type=jnp.float32)
        * scaling
    ).astype(jnp.bfloat16)


def both_parts(queries, cotangent, key_rows, value_rows, live_mask):
    weights = attention_weights(queries, key_rows, live_mask)
    return (
        forward_part(weights, value_rows),
        backward_part(weights, cotangent, key_rows, value_rows),
    )


def block_pass(
    work_fn, query_blocks, grad_blocks, key_blocks, value_blocks, slot_lists, live_mask, per_step
):
    block_total = query_blocks.shape[0]
    slot_count = slot_lists.shape[1]

    def grouped(tensor):
        return tensor.reshape((block_total // per_step, per_step) + tensor.shape[1:])

    def step_fn(pieces):
        query_part, grad_part, list_part, mask_part = pieces
        key_rows = key_blocks[list_part].reshape(per_step, slot_count * BLK, HEAD_SIZE)
        value_rows = value_blocks[list_part].reshape(per_step, slot_count * BLK, HEAD_SIZE)
        return work_fn(query_part, grad_part, key_rows, value_rows, mask_part)

    results = lax.map(
        step_fn,
        (grouped(query_blocks), grouped(grad_blocks), grouped(slot_lists), grouped(live_mask)),
    )
    return tuple((result.reshape(query_blocks.shape) for result in results))


def body(
    normed_layer_input,
    frozen_query_rows,
    projected_keys,
    projected_values,
    output_gradient,
    adapter_down,
    adapter_up,
    langevin_down_noise,
    langevin_up_noise,
    listed_key_blocks,
    head_live_slots,
):
    tok_rows = normed_layer_input.shape[1]
    head_total = frozen_query_rows.shape[2] // HEAD_SIZE
    group_total = projected_keys.shape[2] // HEAD_SIZE
    owners = lax.axis_size("ctx")
    reduced_rank_rows = jnp.dot(
        normed_layer_input[0], adapter_down, preferred_element_type=jnp.float32
    ).astype(jnp.bfloat16)
    query_matrix = (
        frozen_query_rows[0].astype(jnp.float32)
        + ADAPTER_GAIN * jnp.dot(reduced_rank_rows, adapter_up, preferred_element_type=jnp.float32)
    ).astype(jnp.bfloat16)
    query_cube = query_matrix.reshape(tok_rows, head_total, HEAD_SIZE)
    grad_cube = output_gradient[0].reshape(tok_rows, head_total, HEAD_SIZE)
    key_cube = projected_keys[0].reshape(tok_rows, group_total, HEAD_SIZE)
    value_cube = projected_values[0].reshape(tok_rows, group_total, HEAD_SIZE)
    my_first = lax.axis_index("ctx") * HEADS_OWN
    query_send = query_cube.reshape(tok_rows, owners, HEADS_OWN, HEAD_SIZE)
    grad_send = grad_cube.reshape(tok_rows, owners, HEADS_OWN, HEAD_SIZE)
    query_recv, grad_recv = (
        lax.all_to_all(query_send, "ctx", split_axis=1, concat_axis=0, tiled=True),
        lax.all_to_all(grad_send, "ctx", split_axis=1, concat_axis=0, tiled=True),
    )
    group_ids = (jnp.arange(head_total, dtype=jnp.int32) // G).reshape(owners, HEADS_OWN)
    key_recv, value_recv = (
        lax.all_to_all(key_cube[:, group_ids], "ctx", split_axis=1, concat_axis=0, tiled=True),
        lax.all_to_all(value_cube[:, group_ids], "ctx", split_axis=1, concat_axis=0, tiled=True),
    )
    group_pick = list(range(HEADS_OWN))
    seq_rows = query_recv.shape[0]
    block_total = listed_key_blocks.shape[1]
    per_step = min(block_total, max(1, 512 // BLK))
    key_held = key_recv[:, 0]
    value_held = value_recv[:, 0]

    def run_slot(slot_number, work_fn):
        head_index = my_first + slot_number
        slot_lists = lax.dynamic_index_in_dim(listed_key_blocks, head_index, 0, keepdims=False)
        live_count = lax.dynamic_index_in_dim(head_live_slots, head_index, 0, keepdims=False)
        live_row = jnp.arange(NBMAX * BLK, dtype=jnp.int32) // BLK < live_count
        live_mask = jnp.broadcast_to(live_row[None, :], (block_total, NBMAX * BLK))
        query_blocks = query_recv[:, 0, slot_number].reshape(block_total, BLK, HEAD_SIZE)
        grad_blocks = grad_recv[:, 0, slot_number].reshape(block_total, BLK, HEAD_SIZE)
        key_blocks = key_held[:, group_pick[slot_number]].reshape(block_total, BLK, HEAD_SIZE)
        value_blocks = value_held[:, group_pick[slot_number]].reshape(block_total, BLK, HEAD_SIZE)
        results = block_pass(
            work_fn,
            query_blocks,
            grad_blocks,
            key_blocks,
            value_blocks,
            slot_lists,
            live_mask,
            per_step,
        )
        return tuple((result.reshape(seq_rows, HEAD_SIZE) for result in results))

    finished = [run_slot(slot_number, both_parts) for slot_number in range(HEADS_OWN)]
    out_slots = jnp.stack([entry[0] for entry in finished], axis=1)[:, None]
    grad_slots = jnp.stack([entry[1] for entry in finished], axis=1)[:, None]
    out_back, grad_back = (
        lax.all_to_all(out_slots, "ctx", split_axis=0, concat_axis=1, tiled=True),
        lax.all_to_all(grad_slots, "ctx", split_axis=0, concat_axis=1, tiled=True),
    )
    attended = out_back.reshape(tok_rows, head_total * HEAD_SIZE)
    query_gradient = grad_back.reshape(tok_rows, head_total * HEAD_SIZE)
    up_gradient = ADAPTER_GAIN * jnp.einsum(
        "tr,tc->rc", reduced_rank_rows, query_gradient, preferred_element_type=jnp.float32
    )
    reduced_gradient = (
        ADAPTER_GAIN
        * jnp.einsum("ns,ws->nw", query_gradient, adapter_up, preferred_element_type=jnp.float32)
    ).astype(jnp.bfloat16)
    grad_down = jnp.einsum(
        "td,tr->dr", normed_layer_input[0], reduced_gradient, preferred_element_type=jnp.float32
    )
    total_down, total_up = lax.psum((grad_down, up_gradient), ("dp", "ctx"))
    token_norm = (tok_rows * owners * lax.axis_size("dp")) ** (-0.5)
    return (
        attended[None],
        total_down * token_norm + langevin_down_noise,
        total_up * token_norm + langevin_up_noise,
    )


def solution(mesh):
    return jax.shard_map(
        body,
        mesh=mesh,
        in_specs=(
            P("dp", "ctx", None),
            P("dp", "ctx", None),
            P("dp", "ctx", None),
            P("dp", "ctx", None),
            P("dp", "ctx", None),
            P(),
            P(),
            P(),
            P(),
            P(),
            P(),
        ),
        out_specs=(P("dp", "ctx", None), P(), P()),
        check_vma=False,
    )
```

profile of v0, /device:TPU:1, one launch (start us, length us, event | category | flops | bytes accessed | tf_op | source)
XLA Modules:
  0.0 675.8 jit_solution(14031596743235958248)
XLA Ops:
  13.0 4.4 reshape_reshape.3
  17.5 5.3 copy.51
  22.8 9.8 %all-to-all-start = ((bf16[128,32,2,128]{3,0,2,1:T(8,128)(2,1)}), bf16[128,32,2,128]{3,0,2,1:T(8,128)(2,1)}, u32[]{:S(2)}, u32[]{:S(2)}) async-start(bf16[128,32,2,128]{3,0,2,1:T(8,128)(2,1)} %copy.51), calls=%async_computation | async-start | bytes 4194304 | tf_op jit(solution)/shard_map/all_to_all | solution.py:110
  35.3 25.7 %all-to-all-done = bf16[128,32,2,128]{3,0,2,1:T(8,128)(2,1)} async-done(((bf16[128,32,2,128]{3,0,2,1:T(8,128)(2,1)}), bf16[128,32,2,128]{3,0,2,1:T(8,128)(2,1)}, u32[]{:S(2)}, u32[]{:S(2)}) %all-to-all-start) | async-done | bytes 2097184 | tf_op jit(solution)/shard_map/all_to_all | solution.py:110
  61.0 5.3 all-to-all-start.1
  68.8 25.9 %all-to-all-done.1 = bf16[128,32,2,128]{3,0,2,1:T(8,128)(2,1)} async-done(((bf16[128,32,2,128]{3,0,2,1:T(8,128)(2,1)}), bf16[128,32,2,128]{3,0,2,1:T(8,128)(2,1)}, u32[]{:S(2)}, u32[]{:S(2)}) %all-to-all-start.1) | async-done | bytes 2097184 | tf_op jit(solution)/shard_map/all_to_all | solution.py:115
  94.8 5.3 all-to-all-start.2
  100.6 4.1 copy.60
  104.7 6.2 copy.61
  116.2 12.4 %all-to-all-done.2 = bf16[128,32,2,128]{3,0,2,1:T(8,128)(2,1)} async-done(((bf16[128,32,2,128]{3,0,2,1:T(8,128)(2,1)}), bf16[128,32,2,128]{3,0,2,1:T(8,128)(2,1)}, u32[]{:S(2)}, u32[]{:S(2)}) %all-to-all-start.2) | async-done | bytes 2097184 | tf_op jit(solution)/shard_map/all_to_all | solution.py:116
  128.6 5.2 all-to-all-start.3
  142.9 19.4 %all-to-all-done.3 = bf16[128,32,2,128]{3,2,0,1:T(2,128)(2,1)} async-done(((bf16[128,32,2,128]{3,2,0,1:T(2,128)(2,1)}), bf16[128,32,2,128]{3,2,0,1:T(2,128)(2,1)}, u32[]{:S(2)}, u32[]{:S(2)}) %all-to-all-start.3) | async-done | bytes 2097184 | tf_op jit(solution)/shard_map/all_to_all | solution.py:111
  168.5 140.6 %while.25 = (s32[]{:T(128)}, bf16[8,4,128,128]{3,2,1,0:T(8,128)(2,1)}, bf16[8,4,128,128]{3,2,1,0:T(8,128)(2,1)}, pred[8,4,1536]{2,1,0:T(4,128)(4,1)S(1)}, bf16[8...) while((s32[]{:T(128)}, ...), condition=%wide.region_9.10_spmd, body=%wide.region_5.9_spmd.sunk | while | flops 815728768 | bytes 57183768 | solution.py:71
  171.8 3.2 gather_fusion.3
  174.9 4.2 fusion.156
  179.2 3.8 fusion.157
  189.3 3.2 gather_fusion.3
  192.5 4.2 fusion.156
  196.8 3.8 fusion.157
  206.9 3.2 gather_fusion.3
  210.1 4.2 fusion.156
  214.3 3.8 fusion.157
  224.5 3.2 gather_fusion.3
  227.7 4.2 fusion.156
  231.9 3.8 fusion.157
  242.1 3.2 gather_fusion.3
  245.2 4.2 fusion.156
  249.5 3.8 fusion.157
  259.6 3.2 gather_fusion.3
  262.8 4.2 fusion.156
  267.1 3.8 fusion.157
  280.4 4.2 fusion.156
  284.6 3.8 fusion.157
  297.9 4.2 fusion.156
  302.2 3.8 fusion.157
  311.5 130.5 %while.24 = (s32[]{:T(128)}, bf16[8,4,128,128]{3,2,1,0:T(8,128)(2,1)}, bf16[8,4,128,128]{3,2,1,0:T(8,128)(2,1)}, pred[8,4,1536]{2,1,0:T(4,128)(4,1)S(1)}, bf16[8...) while((s32[]{:T(128)}, ...), condition=%wide.region_4.5_spmd, body=%wide.region_0.4_spmd.sunk | while | flops 815728768 | bytes 57183768 | solution.py:71
  316.8 4.1 fusion.147
  320.9 3.8 fusion.148
  333.1 4.1 fusion.147
  337.2 3.8 fusion.148
  349.4 4.1 fusion.147
  353.6 3.8 fusion.148
  365.7 4.1 fusion.147
  369.9 3.8 fusion.148
  382.1 4.1 fusion.147
  386.2 3.8 fusion.148
  398.4 4.1 fusion.147
  402.5 3.8 fusion.148
  414.7 4.1 fusion.147
  418.9 3.8 fusion.148
  431.0 4.1 fusion.147
  435.2 3.8 fusion.148
  443.8 18.4 %copy.67 = bf16[4096,1,2,128]{3,2,1,0:T(2,128)(2,1)} copy(bf16[4096,1,2,128]{3,0,2,1:T(8,128)(2,1)S(1)} %maximum_bitcast_fusion.1) | data formatting | bytes 4194304 | tf_op jit(solution)/shard_map/broadcast_in_dim | solution.py:149
  462.2 5.3 all-to-all-start.5
  468.9 18.1 %copy.64 = bf16[4096,1,2,128]{3,2,1,0:T(2,128)(2,1)} copy(bf16[4096,1,2,128]{3,0,2,1:T(8,128)(2,1)S(1)} %maximum_bitcast_fusion) | data formatting | bytes 4194304 | tf_op jit(solution)/shard_map/broadcast_in_dim | solution.py:148
  487.0 8.9 %all-to-all-done.5 = bf16[4096,1,2,128]{3,2,1,0:T(2,128)(2,1)} async-done(((bf16[4096,1,2,128]{3,2,1,0:T(2,128)(2,1)}), bf16[4096,1,2,128]{3,2,1,0:T(2,128)(2,1)}, u32[]{:S(2)}, u32[]{:S(2)}) %all-to-all-start.5) | async-done | bytes 2097184 | tf_op jit(solution)/shard_map/all_to_all | solution.py:152
  496.0 5.2 all-to-all-start.4
  501.2 3.2 copy.68
  504.4 4.1 copy.69
  514.8 14.9 %all-to-all-done.4 = bf16[4096,1,2,128]{3,2,1,0:T(2,128)(2,1)} async-done(((bf16[4096,1,2,128]{3,2,1,0:T(2,128)(2,1)}), bf16[4096,1,2,128]{3,2,1,0:T(2,128)(2,1)}, u32[]{:S(2)}, u32[]{:S(2)}) %all-to-all-start.4) | async-done | bytes 2097184 | tf_op jit(solution)/shard_map/all_to_all | solution.py:151
  529.6 3.2 copy.65
  532.8 4.1 copy.66
  536.9 4.2 copy.70
  541.1 124.1 %all-reduce.3.cloned.1.call-done = (f32[8192,16]{0,1:T(8,128)}, f32[16,8192]{1,0:T(8,128)}) async-done(((f32[8192,16]{0,1:T(8,128)}, f32[16,8192]{1,0:T(8,128)}), (f32[8192,16]{0,1:T(8,128)}, f32[16,8192]{1,0:T(8,128)})) %all-reduce.3.cloned.1.call-update) | async-done | bytes 1048592 | tf_op jit(solution)/shard_map/psum | solution.py:166
  (283 shorter events, 171.9 us)
Async XLA Ops:
  7.2 3.8 copy-start.7
  7.2 3.8 copy-start.6
  22.8 9.8 %copy-start.12 = (bf16[1,128,1024]{2,1,0:T(8,128)(2,1)S(1)}, bf16[1,128,1024]{2,1,0:T(8,128)(2,1)}, u32[]{:S(2)}) copy-start(bf16[1,128,1024]{2,1,0:T(8,128)(2,1)} %param.17) | copy-start | bytes 786436
  22.8 38.2 %all-to-all-start = ((bf16[128,32,2,128]{3,0,2,1:T(8,128)(2,1)}), bf16[128,32,2,128]{3,0,2,1:T(8,128)(2,1)}, u32[]{:S(2)}, u32[]{:S(2)}) async-start(bf16[128,32,2,128]{3,0,2,1:T(8,128)(2,1)} %copy.51), calls=%async_computation | async-start | bytes 4194304 | tf_op jit(solution)/shard_map/all_to_all | solution.py:110
  61.0 5.3 copy-start.13
  61.0 33.8 %all-to-all-start.1 = ((bf16[128,32,2,128]{3,0,2,1:T(8,128)(2,1)}), bf16[128,32,2,128]{3,0,2,1:T(8,128)(2,1)}, u32[]{:S(2)}, u32[]{:S(2)}) async-start(bf16[128,32,2,128]{3,0,2,1:T(8,128)(2,1)} %bitcast.210), calls=%async_computation.1 | async-start | bytes 4194304 | tf_op jit(solution)/shard_map/all_to_all | solution.py:115
  94.8 5.3 copy-start.9
  94.8 33.8 %all-to-all-start.2 = ((bf16[128,32,2,128]{3,0,2,1:T(8,128)(2,1)}), bf16[128,32,2,128]{3,0,2,1:T(8,128)(2,1)}, u32[]{:S(2)}, u32[]{:S(2)}) async-start(bf16[128,32,2,128]{3,0,2,1:T(8,128)(2,1)} %bitcast.209), calls=%async_computation.2 | async-start | bytes 4194304 | tf_op jit(solution)/shard_map/all_to_all | solution.py:116
  104.7 6.5 copy-start.16
  128.6 33.7 %all-to-all-start.3 = ((bf16[128,32,2,128]{3,2,0,1:T(2,128)(2,1)}), bf16[128,32,2,128]{3,2,0,1:T(2,128)(2,1)}, u32[]{:S(2)}, u32[]{:S(2)}) async-start(bf16[128,32,2,128]{3,2,0,1:T(2,128)(2,1)} %copy.61), calls=%async_computation.3 | async-start | bytes 4194304 | tf_op jit(solution)/shard_map/all_to_all | solution.py:111
  179.2 3.8 copy-start.3
  179.2 3.8 copy-start.17
  183.0 1.7 copy-start.1
  196.8 3.8 copy-start.3
  196.8 3.8 copy-start.17
  200.5 1.7 copy-start.1
  214.3 3.8 copy-start.3
  214.3 3.8 copy-start.17
  218.1 1.7 copy-start.1
  231.9 3.8 copy-start.3
  231.9 3.8 copy-start.17
  235.7 1.7 copy-start.1
  249.5 3.8 copy-start.3
  249.5 3.8 copy-start.17
  253.3 1.7 copy-start.1
  267.1 3.8 copy-start.3
  267.1 3.8 copy-start.17
  270.9 1.7 copy-start.1
  284.6 3.8 copy-start.3
  284.6 3.8 copy-start.17
  288.4 1.7 copy-start.1
  302.2 3.8 copy-start.3
  302.2 3.8 copy-start.17
  306.0 1.7 copy-start.1
  320.9 3.8 copy-start.4
  320.9 3.8 copy-start.18
  337.2 3.8 copy-start.4
  337.2 3.8 copy-start.18
  341.1 1.7 copy-start.2
  353.6 3.8 copy-start.4
  353.6 3.8 copy-start.18
  357.4 1.7 copy-start.2
  369.9 3.8 copy-start.4
  369.9 3.8 copy-start.18
  373.7 1.7 copy-start.2
  386.2 3.8 copy-start.4
  386.2 3.8 copy-start.18
  390.0 1.7 copy-start.2
  402.5 3.8 copy-start.4
  402.5 3.8 copy-start.18
  406.3 1.7 copy-start.2
  418.9 3.8 copy-start.4
  418.9 3.8 copy-start.18
  422.7 1.7 copy-start.2
  435.2 3.8 copy-start.4
  435.2 3.8 copy-start.18
  462.2 5.3 copy-start.5
  462.2 33.8 %all-to-all-start.5 = ((bf16[4096,1,2,128]{3,2,1,0:T(2,128)(2,1)}), bf16[4096,1,2,128]{3,2,1,0:T(2,128)(2,1)}, u32[]{:S(2)}, u32[]{:S(2)}) async-start(bf16[4096,1,2,128]{3,2,1,0:T(2,128)(2,1)} %copy.67), calls=%async_computation.5 | async-start | bytes 4194304 | tf_op jit(solution)/shard_map/all_to_all | solution.py:152
  496.0 33.6 %all-to-all-start.4 = ((bf16[4096,1,2,128]{3,2,1,0:T(2,128)(2,1)}), bf16[4096,1,2,128]{3,2,1,0:T(2,128)(2,1)}, u32[]{:S(2)}, u32[]{:S(2)}) async-start(bf16[4096,1,2,128]{3,2,1,0:T(2,128)(2,1)} %copy.64), calls=%async_computation.4 | async-start | bytes 4194304 | tf_op jit(solution)/shard_map/all_to_all | solution.py:151
  501.1 164.0 %all-reduce.3.cloned.1.call-start = ((), (), s32[]{:S(2)}) async-start(), calls=%async_computation.6 | async-start | bytes 2097152 | tf_op jit(solution)/shard_map/psum | solution.py:166
  504.4 4.1 copy-start.15
  508.5 3.1 copy-start.8
  536.9 128.3 %copy-start.10 = (f32[8192,16]{0,1:T(8,128)S(1)}, f32[8192,16]{0,1:T(8,128)}, u32[]{:S(2)}) copy-start(f32[8192,16]{0,1:T(8,128)} %param.22) | copy-start | bytes 1572868
  536.9 130.1 %copy-start.11 = (f32[16,8192]{1,0:T(8,128)S(1)}, f32[16,8192]{1,0:T(8,128)}, u32[]{:S(2)}) copy-start(f32[16,8192]{1,0:T(8,128)} %param.23) | copy-start | bytes 1572868
  (4 other events, 5.6 us)
Sparse Core Ops, SparseCore 0:
  514.9 150.2 all-reduce.2
where the time goes:
time: 679 us; the launch traced here: 676 us
  waiting for transfers between devices  231 us (34%)
  local copies, waits for them, and re-layouts  199 us (29%)
  matrix products  187 us (28%)
  starting transfers between devices  36.1 us (5%)
  between operations  14.3 us (2%)
  other arithmetic  8.34 us (1%)
    psum x1, waiting for transfers between devices, body(): total_down, total_up = lax.psum((grad_down, up_gradient), ('dp', 'ctx'))  124 us
    sub x16, matrix products, attention_weights(): shifted = jnp.exp(scores - largest)  67 us
    dot_general x16, matrix products, forward_part(): jnp.einsum('gqk,gkd->gqd', weights_low, value_rows, preferred_element_typ...  60.7 us
    gather x16, local copies, waits for them, and re-layouts, step_fn(): value_blocks[list_part].reshape(per_step, slot_count * BLK, HEAD_SIZE)  50.7 us
    gather x16, local copies, waits for them, and re-layouts, step_fn(): key_blocks[list_part].reshape(per_step, slot_count * BLK, HEAD_SIZE)  41.4 us
    dot_general x16, matrix products, backward_part(): jnp.einsum('gqd,gkd->gqk', cotangent, value_rows, preferred_element_type=...  27.4 us
    all_to_all x1, waiting for transfers between devices, body(): lax.all_to_all(key_cube[:, group_ids], 'ctx', split_axis=1, concat_axis=0...  25.9 us
    all_to_all x1, waiting for transfers between devices, body(): lax.all_to_all(query_send, 'ctx', split_axis=1, concat_axis=0, tiled=True)  25.7 us
  transfers between devices with their start and end apart: 7, of which 7 were waited for; matrix products, arithmetic and copies ran while one was open for 11% of the time, Pallas kernels for 0%

commit v1 on v0

v1 whole, which is shorter than its diff:
```python
import functools
import math

import jax
import jax.numpy as jnp
from jax import lax
from jax.experimental import pallas as pl
from jax.experimental.pallas import tpu as pltpu
from jax.sharding import Mesh, PartitionSpec as P

D = 128
HEADS = 32
NBMAX = 12
GAIN = 2.0
SCALE = D**-0.5
EXP2_SCALE = SCALE * math.log2(math.e)
F32, BF16 = jnp.float32, jnp.bfloat16
NT = (((1,), (1,)), ((), ()))
NN = (((1,), (0,)), ((), ()))
TN = (((0,), (0,)), ((), ()))


def attend(quads, base, lists, g, kv, kvt, w_ref, s_ref, q, cot):
    w_ref[0:D, 0:D] = q
    w_ref[D : 2 * D, D : 2 * D] = cot
    w = w_ref[...]

    def block(i, j):
        return lists[base + 4 * i + j]

    def rows(i):
        return pl.ds(512 * i, 512)

    top = jnp.full((8, D), -jnp.inf, F32)
    for i in range(quads):
        tiles = []
        for j in range(4):
            n = block(i, j)
            tiles.append(kv[g, n // 2, pl.ds(pl.multiple_of((n % 2) * D, D), D), :])
        both = lax.dot_general(jnp.concatenate(tiles, axis=0), w, NT, preferred_element_type=F32)
        s_ref[rows(i), :] = both
        top = jnp.maximum(top, both[:, :D].reshape(64, 8, D).max(0))
    largest = jnp.max(top, axis=0, keepdims=True)
    total = jnp.zeros((8, D), F32)
    inner = jnp.zeros((8, D), F32)
    for i in range(quads):
        e = jnp.exp2((s_ref[rows(i), 0:D] - largest) * EXP2_SCALE)
        s_ref[rows(i), 0:D] = e
        total += e.reshape(64, 8, D).sum(0)
        inner += (e * s_ref[rows(i), D : 2 * D]).reshape(64, 8, D).sum(0)
    inverse = 1.0 / jnp.sum(total, axis=0, keepdims=True)
    inner = jnp.sum(inner, axis=0, keepdims=True) * inverse
    out = jnp.zeros((D, D), F32)
    grad = jnp.zeros((D, D), F32)
    for i in range(quads):
        e = s_ref[rows(i), 0:D]
        ds = e * (s_ref[rows(i), D : 2 * D] - inner)
        x = jnp.concatenate([e.astype(BF16), ds.astype(BF16)], axis=1)
        cols = [kvt[g, :, pl.ds(pl.multiple_of(block(i, j) * D, D), D)] for j in range(4)]
        r = lax.dot_general(jnp.concatenate(cols, axis=1), x, NN, preferred_element_type=F32)
        out += r[D : 2 * D, 0:D]
        grad += r[0:D, D : 2 * D]
    return (out * inverse).T.astype(BF16), (grad * (inverse * SCALE)).T.astype(BF16)


def attention_kernel(n_src, copies, lists, live, off, q_own, g_own, qg_far, *rest):
    srcs = rest[:n_src]
    o_own, o_far, d_own, d_far, kv, kvt, w_ref, s_ref, sem = rest[n_src:]
    step = pl.program_id(0)
    del off

    def copy(g, i):
        src, make_src, lo, size, col = copies[g][i]
        return pltpu.make_async_copy(
            make_src(srcs[src]), kv.at[g, lo : lo + size, :, col : col + D], sem.at[g, i]
        )

    @pl.when(step == 0)
    def _():
        for g in range(2):
            for i in range(len(copies[g])):
                copy(g, i).start()
        w_ref[...] = jnp.zeros_like(w_ref)

    for g in range(2):

        @pl.when(step == 8 * g)
        def _():
            for i in range(len(copies[g])):
                copy(g, i).wait()

            def turn(chip, _):
                kvt[g, :, pl.ds(pl.multiple_of(chip * 256, 256), 256)] = kv[g, chip].T
                return 0

            lax.fori_loop(0, 16, turn, 0)

    g = step // 8
    for quads in (1, 2, 3):

        @pl.when(live[step] == 4 * quads)
        def _():
            go = functools.partial(attend, quads)
            out, grad = go(step * 24, lists, g, kv, kvt, w_ref, s_ref, q_own[...], g_own[...])
            o_own[...] = out
            d_own[...] = grad
            out, grad = go(step * 24 + 12, lists, g, kv, kvt, w_ref, s_ref, qg_far[0], qg_far[1])
            o_far[...] = out
            d_far[...] = grad


def attention(chunk, lists, live, off, q_all, g_all, qg_far, srcs, copies):
    whole = pl.BlockSpec((D, D), lambda h, a, b, off: (0, off[0] + h))
    far = pl.BlockSpec((2, D, D), lambda h, a, b, off: (0, 0, 16 * chunk + h))
    res = pl.BlockSpec((D, D), lambda h, a, b, off: (0, h))
    shape = jax.ShapeDtypeStruct((D, 16 * D), BF16)
    n_copies = max(len(c) for c in copies)
    return pl.pallas_call(
        functools.partial(attention_kernel, len(srcs), copies),
        out_shape=(shape,) * 4,
        grid_spec=pltpu.PrefetchScalarGridSpec(
            num_scalar_prefetch=3,
            grid=(16,),
            in_specs=[whole, whole, far] + [pl.BlockSpec(memory_space=pl.ANY)] * len(srcs),
            out_specs=(res,) * 4,
            scratch_shapes=[
                pltpu.VMEM((2, 16, 256, 2 * D), BF16),
                pltpu.VMEM((2, 2 * D, 4096), BF16),
                pltpu.VMEM((2 * D, 2 * D), BF16),
                pltpu.VMEM((NBMAX * D, 2 * D), F32),
                pltpu.SemaphoreType.DMA((2, n_copies)),
            ],
        ),
        compiler_params=pltpu.CompilerParams(
            dimension_semantics=("arbitrary",), vmem_limit_bytes=40 << 20
        ),
        cost_estimate=pl.CostEstimate(
            flops=32 * 8 * 8 * D * D * D, bytes_accessed=8 << 20, transcendentals=32 * 8 * D * D
        ),
        name=f"attend_{chunk}",
    )(lists, live, off, q_all, g_all, qg_far, *srcs)


def hop(x, axis, by):
    return lax.ppermute(x, axis, [(i, (i + by) % 4) for i in range(4)])


def swap(x):
    return lax.ppermute(x, "core", [(0, 1), (1, 0)])


def ring_gather(own, first, second):
    less, more = hop(own, first, 1), hop(own, first, -1)
    k2, v2 = hop(less[0], first, 1), hop(more[1], first, -1)
    line = jnp.stack([own, less, more, jnp.stack([k2, v2])])
    less, more = hop(line, second, 1), hop(line, second, -1)
    k2, v2 = hop(less[:, 0], second, 1), hop(more[:, 1], second, -1)
    return [line, less, more, k2, v2]


def ring_copies(first_src):
    pick = []
    for s in range(3):
        for k in range(2):
            pick.append((first_src + s, lambda r, k=k: r.at[:, k], 4 * s, 4, k * D))
    for k in range(2):
        pick.append((first_src + 3 + k, lambda r: r, 12, 4, k * D))
    return pick


def in_order(own, others, index):
    have = [own, *others]
    out = []
    for j in range(4):
        back = (index - j) % 4
        pick = have[3]
        for d in range(3):
            pick = jnp.where(back == d, have[d], pick)
        out.append(pick)
    return out


def exchange(x, axis):
    return [hop(x, axis, d) for d in (1, 2, 3)]


def all_sum(x, axis):
    low = x.astype(BF16)
    parts = in_order(low, exchange(low, axis), lax.axis_index(axis))
    return sum(p.astype(F32) for p in parts)


def body(x, frozen, keys, values, cot, down, up, noise_down, noise_up, lists, live):
    x, frozen, keys, values, cot = x[0], frozen[0], keys[0], values[0], cot[0]
    core, y, z = lax.axis_index("core"), lax.axis_index("y"), lax.axis_index("z")
    chip = y * 4 + z
    half = HEADS * D

    kv = jnp.stack([keys, values])
    mine = lax.dynamic_slice_in_dim(kv, core * 512, 512, 2)
    far = swap(lax.dynamic_slice_in_dim(kv, (1 - core) * 512, 512, 2))
    kv = jnp.where(core == 0, jnp.concatenate([mine, far], 1), jnp.concatenate([far, mine], 1))
    kv_heads = [kv[:, :, i * D : (i + 1) * D] for i in range(4)]

    late = lax.all_gather(jnp.stack(kv_heads[2:]), ("y", "z"), axis=0, tiled=False)
    ring_a = ring_gather(kv_heads[0], "z", "y")
    ring_b = ring_gather(kv_heads[1], "y", "z")

    low = jnp.dot(x, down, preferred_element_type=F32).astype(BF16)
    query = (frozen.astype(F32) + GAIN * jnp.dot(low, up, preferred_element_type=F32)).astype(BF16)
    away = (1 - core) * half
    qg_far = swap(
        jnp.stack(
            [
                lax.dynamic_slice_in_dim(query, away, half, 1),
                lax.dynamic_slice_in_dim(cot, away, half, 1),
            ]
        )
    )
    low_far = swap(low)

    mylists = lax.dynamic_slice(lists, (core * HEADS, chip * 2, 0), (HEADS, 2, NBMAX))
    mylists = jnp.where(core == 0, mylists, mylists[:, ::-1])
    mylive = lax.dynamic_slice_in_dim(live, core * HEADS, HEADS, 0)
    place = jnp.array([0, 2, 3, 1], jnp.int32)
    at_y = place[(mylists // 8 - y) % 4]
    at_z = place[(mylists // 2 - z) % 4]
    low_bit = mylists % 2
    spot = jnp.concatenate(
        [
            (at_y * 8 + at_z * 2 + low_bit)[:8],
            (at_z * 8 + at_y * 2 + low_bit)[8:16],
            mylists[16:],
        ]
    )

    def run(chunk, srcs, copies):
        return attention(
            chunk,
            spot[16 * chunk : 16 * chunk + 16].reshape(-1),
            mylive[16 * chunk : 16 * chunk + 16],
            jnp.reshape(core * HEADS + 16 * chunk, (1,)),
            query,
            cot,
            qg_far,
            srcs,
            copies,
        )

    early = run(0, ring_a + ring_b, [ring_copies(0), ring_copies(5)])
    gathered = [
        [(0, lambda r, g=g, k=k: r.at[:, g, k], 0, 16, k * D) for k in range(2)] for g in range(2)
    ]
    last = run(1, [late], gathered)

    own_half = jnp.concatenate([early[0], last[0]], axis=1)
    far_half = jnp.concatenate([swap(early[1]), swap(last[1])], axis=1)
    attended = jnp.where(
        core == 0,
        jnp.concatenate([own_half, far_half], 1),
        jnp.concatenate([far_half, own_half], 1),
    )

    d_own = jnp.concatenate([early[2], last[2]], axis=1)
    d_far = jnp.concatenate([early[3], last[3]], axis=1)
    my_up = lax.dynamic_slice_in_dim(up, core * half, half, 1)
    low_grad_far = swap(lax.dot_general(d_far, my_up, NT, preferred_element_type=F32))
    low_grad = lax.dot_general(d_own, my_up, NT, preferred_element_type=F32) + low_grad_far
    low_grad = (GAIN * low_grad).astype(BF16)
    grad_up = GAIN * (
        lax.dot_general(low, d_own, TN, preferred_element_type=F32)
        + lax.dot_general(low_far, d_far, TN, preferred_element_type=F32)
    )
    grad_down = lax.dot_general(low_grad, x, TN, preferred_element_type=F32)
    down_mine = lax.dynamic_slice_in_dim(grad_down, core * half, half, 1)
    down_away = lax.dynamic_slice_in_dim(grad_down, (1 - core) * half, half, 1)
    down_mine = down_mine + swap(down_away.astype(BF16)).astype(F32)

    total = jnp.concatenate([grad_up, down_mine], axis=0)
    quarter = half // 4
    pieces = [
        lax.dynamic_slice_in_dim(total, ((z + d) % 4) * quarter, quarter, 1) for d in range(4)
    ]
    total = pieces[0] + sum(hop(pieces[d].astype(BF16), "z", d).astype(F32) for d in (1, 2, 3))
    total = all_sum(all_sum(total, "y"), "dp").astype(BF16)
    total = jnp.concatenate(in_order(total, exchange(total, "z"), z), axis=1)
    other = swap(total)
    total = jnp.where(
        core == 0, jnp.concatenate([total, other], 1), jnp.concatenate([other, total], 1)
    ).astype(F32)
    norm = (4 * 32 * x.shape[0]) ** -0.5
    step_up = total[:16] * norm + noise_up
    step_down = (total[16:] * norm).T + noise_down
    return attended[None], step_down, step_up


def solution(mesh):
    fine = Mesh(mesh.devices.reshape(4, 4, 4, 2), ("dp", "y", "z", "core"))
    rows = P("dp", ("y", "z", "core"), None)
    return jax.shard_map(
        body,
        mesh=fine,
        in_specs=(rows,) * 5 + (P(),) * 6,
        out_specs=(rows, P(), P()),
        check_vma=False,
    )
```

time: 679 us -> 211 us (0.31)
  waiting for transfers between devices: 231 us -> 21.4 us
  matrix products: 187 us -> 8.15 us
  local copies, waits for them, and re-layouts: 199 us -> 26.8 us
  Pallas kernels: 0 us -> 63.9 us
  starting transfers between devices: 36.1 us -> 64 us
    psum x1 -> x0, waiting for transfers between devices: 124 us -> none  [body(): total_down, total_up = lax.psum((grad_down, up_gradient), ('dp', 'ctx'))]
    dot_general x52 -> x6, matrix products: 120 us -> 8.15 us  [the longest x1 2.82 us: body(): grad_down = lax.dot_general(low_grad, x, TN, preferred_element_type=F32)]
    all_to_all x6 -> x0, waiting for transfers between devices: 107 us -> none  [the longest x1 25.9 us: body(): lax.all_to_all(key_cube[:, group_ids], 'ctx', split_axis=1, concat_axis=0...]
    gather x34 -> x0, local copies, waits for them, and re-layouts: 96.4 us -> none  [the longest x16 50.7 us: step_fn(): value_blocks[list_part].reshape(per_step, slot_count * BLK, HEAD_SIZE)]
    sub x16 -> x0, matrix products: 67 us -> none  [attention_weights(): shifted = jnp.exp(scores - largest)]
    ppermute x0 -> x36, starting transfers between devices: none -> 64 us  [the longest x28 41.1 us: hop(): return lax.ppermute(x, axis, [(i, (i + by) % 4) for i in range(4)])]
    pallas_call x0 -> x2, Pallas kernels: none -> 63.9 us  [attention(): pl.pallas_call(functools.partial(attention_kernel, len(srcs), copies), ou...]
    broadcast_in_dim x18 -> x0, local copies, waits for them, and re-layouts: 36.6 us -> none  [the longest x1 18.4 us: body(): grad_slots = jnp.stack([entry[1] for entry in finished], axis=1)[:, None]]
  transfers between devices with their start and end apart: 7 -> 37, of which waited for: 7 -> 12; matrix products, arithmetic and copies ran while one was open for 11% -> 9% of each run, Pallas kernels for 0% -> 31%
where the time goes in v1:
time: 211 us; the launch traced here: 208 us
  starting transfers between devices  64 us (30%)
  Pallas kernels  63.9 us (30%)
  local copies, waits for them, and re-layouts  26.8 us (13%)
  waiting for transfers between devices  21.4 us (10%)
  between operations  14.6 us (7%)
  other arithmetic  9.19 us (4%)
  matrix products  8.15 us (4%)
    pallas_call x2, Pallas kernels, attention(): pl.pallas_call(functools.partial(attention_kernel, len(srcs), copies), ou...  63.9 us
    ppermute x28, starting transfers between devices, hop(): return lax.ppermute(x, axis, [(i, (i + by) % 4) for i in range(4)])  41.1 us
    ppermute x8, starting transfers between devices, swap(): return lax.ppermute(x, 'core', [(0, 1), (1, 0)])  22.9 us
    ppermute x28, waiting for transfers between devices, hop(): return lax.ppermute(x, axis, [(i, (i + by) % 4) for i in range(4)])  20.2 us
    unnamed x62, local copies, waits for them, and re-layouts  16 us
  transfers between devices with their start and end apart: 37, of which 12 were waited for; matrix products, arithmetic and copies ran while one was open for 9% of the time, Pallas kernels for 31%

profile of v1, /device:TPU:1, one launch (start us, length us, event | category | flops | bytes accessed | tf_op | source)
XLA Modules:
  0.0 208.1 jit_solution(5094862247587189675)
XLA Ops:
  7.2 1.1 constant_dynamic-update-slice_fusion.1
  8.3 1.0 constant_dynamic-update-slice_fusion
  9.4 1.5 collective-permute-start.1
  10.8 1.2 collective-permute-done.1
  12.2 0.8 slice_bitcast_fusion.10
  13.8 1.7 fusion.9
  16.3 0.8 copy-done.4
  17.2 1.2 copy-done.1
  18.6 1.6 pad_maximum_fusion
  20.5 0.9 constant_dynamic-slice_fusion.3
  21.5 3.9 %collective-permute-start.3 = (bf16[2,256,128]{2,1,0:T(8,128)(2,1)}, bf16[2,256,128]{2,1,0:T(8,128)(2,1)S(1)}, u32[]{:S(2)}, u32[]{:S(2)}) collective-permute-start(bf16[2,256,128]{2,1,0:T(8,128)(2,1)} %get-tuple-element.37), channel_id=1, source_target_pairs={{0,6},{2,0},{4,2},{6,4},{1,7},{3,1},{5,3},{7,5},{8,14},{10,8},{12,... | collective-permute-start | bytes 393224 | tf_op jit(solution)/shard_map/ppermute | solution.py:145
  25.5 2.8 %collective-permute-start.11 = (bf16[2,256,128]{2,1,0:T(8,128)(2,1)S(1)}, bf16[2,256,128]{2,1,0:T(8,128)(2,1)S(1)}, u32[]{:S(2)}, u32[]{:S(2)}) collective-permute-start(bf16[2,256,128]{2,1,0:T(8,128)(2,1)S(1)} %get-tuple-element.36), channel_id=1, source_target_pairs={{0,24},{8,0},{16,8},{24,16},{1,25},{9,1},{17,9},{25,17},{2,26},{10... | collective-permute-start | bytes 393224 | tf_op jit(solution)/shard_map/ppermute | solution.py:145
  28.3 1.2 collective-permute-done.3
  29.5 3.4 %collective-permute-start.5 = (bf16[256,128]{1,0:T(8,128)(2,1)S(1)}, bf16[256,128]{1,0:T(8,128)(2,1)S(1)}, u32[]{:S(2)}, u32[]{:S(2)}) collective-permute-start(bf16[256,128]{1,0:T(8,128)(2,1)S(1)} %slice_bitcast_fusion.8), channel_id=1, source_target_pairs={{0,6},{2,0},{4,2},{6,4},{1,7},{3,1},{5,3},{7,5},{8,14},{10,8},{12,... | collective-permute-start | bytes 196616 | tf_op jit(solution)/shard_map/ppermute | solution.py:145
  33.1 3.0 %collective-permute-start.13 = (bf16[256,128]{1,0:T(8,128)(2,1)S(1)}, bf16[256,128]{1,0:T(8,128)(2,1)S(1)}, u32[]{:S(2)}, u32[]{:S(2)}) collective-permute-start(bf16[256,128]{1,0:T(8,128)(2,1)S(1)} %slice_bitcast_fusion.6), channel_id=1, source_target_pairs={{0,24},{8,0},{16,8},{24,16},{1,25},{9,1},{17,9},{25,17},{2,26},{10... | collective-permute-start | bytes 196616 | tf_op jit(solution)/shard_map/ppermute | solution.py:145
  36.1 1.7 collective-permute-done.4
  38.0 1.0 collective-permute-start.6
  39.1 1.8 collective-permute-start.7
  41.3 2.6 %collective-permute-start.15 = (bf16[4,2,256,128]{3,2,0,1:T(8,128)(2,1)S(1)}, bf16[4,2,256,128]{3,2,0,1:T(8,128)(2,1)S(1)}, u32[]{:S(2)}, u32[]{:S(2)}) collective-permute-start(bf16[4,2,256,128]{3,2,0,1:T(8,128)(2,1)S(1)} %pad_maximum_fusion.2), channel_id=1, source_target_pairs={{0,6},{2,0},{4,2},{6,4},{1,7},{3,1},{5,3},{7,5},{8,14},{10,8},{12,... | collective-permute-start | bytes 1572872 | tf_op jit(solution)/shard_map/ppermute | solution.py:145
  43.9 7.3 %collective-permute-done.6.rest_1_ = bf16[4,2,256,128]{3,2,1,0:T(8,128)(2,1)S(1)} collective-permute-done((bf16[4,2,256,128]{3,2,1,0:T(8,128)(2,1)S(1)}, bf16[4,2,256,128]{3,2,1,0:T(8,128)(2,1)S(1)}, u32[]{:S(2)}, u32[]{:S(2)}) %collective-permute-start.6) | collective-permute-done | bytes 524320 | tf_op jit(solution)/shard_map/ppermute | solution.py:145
  53.5 2.7 %collective-permute-start.9 = (bf16[4,256,128]{2,1,0:T(8,128)(2,1)}, bf16[4,256,128]{2,1,0:T(8,128)(2,1)}, u32[]{:S(2)}, u32[]{:S(2)}) collective-permute-start(bf16[4,256,128]{2,1,0:T(8,128)(2,1)} %slice_bitcast_fusion.2), channel_id=1, source_target_pairs={{0,24},{8,0},{16,8},{24,16},{1,25},{9,1},{17,9},{25,17},{2,26},{10... | collective-permute-start | bytes 786440 | tf_op jit(solution)/shard_map/ppermute | solution.py:145
  56.9 0.8 collective-permute-start.16
  58.7 1.8 collective-permute-start.17
  61.0 1.2 copy.34.rest_5_
  62.2 1.1 copy.35.rest_6_
  63.3 1.1 copy.36.rest_7_
  64.4 1.1 collective-permute-done.8.rest_3_
  65.5 12.4 %collective-permute-start.20 = (bf16[128,16]{0,1:T(8,128)(2,1)S(1)}, bf16[128,16]{0,1:T(8,128)(2,1)S(1)}, u32[]{:S(2)}, u32[]{:S(2)}) collective-permute-start(bf16[128,16]{0,1:T(8,128)(2,1)S(1)} %fusion.9), channel_id=1, source_target_pairs={{0,1},{1,0},{2,3},{3,2},{4,5},{5,4},{6,7},{7,6},{8,9},{9,8},{10,11... | collective-permute-start | bytes 12296 | tf_op jit(solution)/shard_map/ppermute | solution.py:149
  77.9 1.6 copy-done.5
  79.5 1.0 copy-done.8
  80.6 31.7 %attend_0.1 = (bf16[128,2048]{1,0:T(8,128)(2,1)S(1)}, bf16[128,2048]{1,0:T(8,128)(2,1)S(1)}, bf16[128,2048]{1,0:T(8,128)(2,1)S(1)}, bf16[128,2048]{1,0:T(8,128)(2,1)S(1)}) custom-call(s32[384]{0:T(512)S(1)} %reshape.129.lists, s32[16]{0:T(128)S(1)} %get-tuple-element.46.live, s32[1]{0:T(128)} %bitcast.off, bf16[128,8192]{1,0:T(8,128)(2,1)S(1)} %copy-done.2, ...), custom_call_target="tpu_custom_call" | custom-call | flops 4294967296 | bytes 8388608 | tf_op jit(solution)/shard_map/attend_0/pallas_call | solution.py:118
  112.3 0.9 constant_dynamic-update-slice_fusion.5
  113.3 0.9 constant_dynamic-update-slice_fusion.3
  114.2 1.6 copy-done.3
  115.7 1.6 copy-done.6
  117.3 2.2 %copy-done.11 = bf16[32,2,256,128]{3,2,1,0:T(8,128)(2,1)S(1)} copy-done((bf16[32,2,256,128]{3,2,1,0:T(8,128)(2,1)S(1)}, bf16[32,2,256,128]{3,2,1,0:T(8,128)(2,1)}, u32[]{:S(2)}) %copy-start.11) | copy-done | bytes 4194328
  119.5 32.2 %attend_1.1 = (bf16[128,2048]{1,0:T(8,128)(2,1)S(1)}, bf16[128,2048]{1,0:T(8,128)(2,1)S(1)}, bf16[128,2048]{1,0:T(8,128)(2,1)S(1)}, bf16[128,2048]{1,0:T(8,128)(2,1)S(1)}) custom-call(s32[384]{0:T(512)S(1)} %reshape.131.lists, s32[16]{0:T(128)S(1)} %get-tuple-element.47.live, s32[1]{0:T(128)} %bitcast.29.off, bf16[128,8192]{1,0:T(8,128)(2,1)S(1)} %copy-done.3, ...), custom_call_target="tpu_custom_call" | custom-call | flops 4294967296 | bytes 8388608 | tf_op jit(solution)/shard_map/attend_1/pallas_call | solution.py:118
  152.2 1.1 collective-permute-start.21
  153.3 1.0 fusion.43
  154.3 1.0 copy-done.16
  155.2 2.8 %fusion.3 = f32[16,8192]{1,0:T(8,128)} fusion(bf16[1,128,8192]{2,1,0:T(8,128)(2,1)S(1)} %copy-done, f32[128,16]{0,1:T(8,128)S(1)} %collective-permute-done.21, bf16[128,4096]{1,0:T(8,128)(2,1)} %copy-done.16, bf16[16,8192]{1,0:T(8,128)(2,1)S(1)} %copy-done.23, s32[]{:T(128)S(6)} %select_n.409), kind=kOutput, calls=%fused_computation.7 | convolution fusion | flops 50337792 | bytes 3809284 | tf_op jit(solution)/shard_map/dot_general | solution.py:274
  158.1 1.0 dynamic-slice_convert_fusion
  159.1 1.5 fusion.2
  160.7 1.1 convert_add_fusion
  162.4 2.7 %collective-permute-start.25 = (bf16[32,1024]{1,0:T(8,128)(2,1)}, bf16[32,1024]{1,0:T(8,128)(2,1)}, u32[]{:S(2)}, u32[]{:S(2)}) collective-permute-start(bf16[32,1024]{1,0:T(8,128)(2,1)} %get-tuple-element.31), channel_id=1, source_target_pairs={{0,6},{2,0},{4,2},{6,4},{1,7},{3,1},{5,3},{7,5},{8,14},{10,8},{12,... | collective-permute-start | bytes 196616 | tf_op jit(solution)/shard_map/ppermute | solution.py:145
  165.7 2.7 %collective-permute-done.25 = bf16[32,1024]{1,0:T(8,128)(2,1)} collective-permute-done((bf16[32,1024]{1,0:T(8,128)(2,1)}, bf16[32,1024]{1,0:T(8,128)(2,1)}, u32[]{:S(2)}, u32[]{:S(2)}) %collective-permute-start.25) | collective-permute-done | bytes 65568 | tf_op jit(solution)/shard_map/ppermute | solution.py:145
  168.4 1.6 collective-permute-done.24
  170.0 0.8 collective-permute-done.23
  170.8 1.0 fusion.19
  171.8 1.7 collective-permute-start.26
  173.5 2.7 %collective-permute-start.28 = (bf16[32,1024]{1,0:T(8,128)(2,1)S(1)}, bf16[32,1024]{1,0:T(8,128)(2,1)S(1)}, u32[]{:S(2)}, u32[]{:S(2)}) collective-permute-start(bf16[32,1024]{1,0:T(8,128)(2,1)S(1)} %fusion.19), channel_id=1, source_target_pairs={{0,24},{8,0},{16,8},{24,16},{1,25},{9,1},{17,9},{25,17},{2,26},{10... | collective-permute-start | bytes 196616 | tf_op jit(solution)/shard_map/ppermute | solution.py:145
  176.5 1.7 collective-permute-done.27
  178.2 2.8 %collective-permute-start.29 = (bf16[32,1024]{1,0:T(8,128)(2,1)S(1)}, bf16[32,1024]{1,0:T(8,128)(2,1)S(1)}, u32[]{:S(2)}, u32[]{:S(2)}) collective-permute-start(bf16[32,1024]{1,0:T(8,128)(2,1)S(1)} %add_convert_fusion.1), channel_id=1, source_target_pairs={{0,64},{32,96},{64,0},{96,32},{1,65},{33,97},{65,1},{97,33},{2,66}... | collective-permute-start | bytes 196616 | tf_op jit(solution)/shard_map/ppermute | solution.py:145
  181.4 2.2 %collective-permute-start.31 = (bf16[32,1024]{1,0:T(8,128)(2,1)S(1)}, bf16[32,1024]{1,0:T(8,128)(2,1)S(1)}, u32[]{:S(2)}, u32[]{:S(2)}) collective-permute-start(bf16[32,1024]{1,0:T(8,128)(2,1)S(1)} %add_convert_fusion.1), channel_id=1, source_target_pairs={{0,96},{32,0},{64,32},{96,64},{1,97},{33,1},{65,33},{97,65},{2,98}... | collective-permute-start | bytes 196616 | tf_op jit(solution)/shard_map/ppermute | solution.py:145
  183.6 1.6 collective-permute-done.30
  185.4 1.1 collective-permute-start.32
  186.5 1.8 collective-permute-start.33
  188.3 0.9 collective-permute-start.34
  189.2 5.2 %collective-permute-start.18 = (bf16[128,2048]{1,0:T(8,128)(2,1)}, bf16[128,2048]{1,0:T(8,128)(2,1)S(1)}, u32[]{:S(2)}, u32[]{:S(2)}) collective-permute-start(bf16[128,2048]{1,0:T(8,128)(2,1)} %copy-done.12), channel_id=1, source_target_pairs={{0,1},{1,0},{2,3},{3,2},{4,5},{5,4},{6,7},{7,6},{8,9},{9,8},{10,11... | collective-permute-start | bytes 1572872 | tf_op jit(solution)/shard_map/ppermute | solution.py:149
  194.6 2.3 %collective-permute-start.35 = (bf16[32,4096]{1,0:T(8,128)(2,1)S(1)}, bf16[32,4096]{1,0:T(8,128)(2,1)S(1)}, u32[]{:S(2)}, u32[]{:S(2)}) collective-permute-start(bf16[32,4096]{1,0:T(8,128)(2,1)S(1)} %pad_maximum_fusion.4), channel_id=1, source_target_pairs={{0,1},{1,0},{2,3},{3,2},{4,5},{5,4},{6,7},{7,6},{8,9},{9,8},{10,11... | collective-permute-start | bytes 786440 | tf_op jit(solution)/shard_map/ppermute | solution.py:149
  196.9 1.6 maximum_select_fusion
  198.7 0.8 copy-done.24
  199.5 0.8 fusion.14
  200.4 0.8 fusion.12
  (134 shorter events, 10.8 us)
Async XLA Ops:
  7.2 6.6 %copy-start = (bf16[1,128,8192]{2,1,0:T(8,128)(2,1)S(1)}, bf16[1,128,8192]{2,1,0:T(8,128)(2,1)}, u32[]{:S(2)}) copy-start(bf16[1,128,8192]{2,1,0:T(8,128)(2,1)} %param.12) | copy-start | bytes 6291460
  7.2 107.0 %all-gather.3.cloned.1.call-start = ((), (), s32[]{:S(2)}) async-start(), calls=%async_computation | async-start | bytes 4456448 | tf_op jit(solution)/shard_map/all_gather | solution.py:205
  9.4 2.6 %collective-permute-start.1 = (bf16[2,128,512]{2,1,0:T(8,128)(2,1)S(1)}, bf16[2,128,512]{2,1,0:T(8,128)(2,1)S(1)}, u32[]{:S(2)}, u32[]{:S(2)}) collective-permute-start(bf16[2,128,512]{2,1,0:T(8,128)(2,1)S(1)} %get-tuple-element.39), channel_id=1, source_target_pairs={{0,1},{1,0},{2,3},{3,2},{4,5},{5,4},{6,7},{7,6},{8,9},{9,8},{10,11... | collective-permute-start | bytes 786440 | tf_op jit(solution)/shard_map/ppermute | solution.py:149
  12.2 3.3 %copy-start.22 = (bf16[16,8192]{1,0:T(8,128)(2,1)S(1)}, bf16[16,8192]{1,0:T(8,128)(2,1)}, u32[]{:S(2)}) copy-start(bf16[16,8192]{1,0:T(8,128)(2,1)} %param.18) | copy-start | bytes 786436
  13.8 1.8 copy-start.18
  15.6 1.6 copy-start.4
  17.2 1.3 copy-start.1
  20.1 57.8 %collective-permute-start = (bf16[2,128,4096]{2,1,0:T(8,128)(2,1)}, bf16[2,128,4096]{2,1,0:T(8,128)(2,1)}, u32[]{:S(2)}, u32[]{:S(2)}) collective-permute-start(bf16[2,128,4096]{2,1,0:T(8,128)(2,1)} %pad_maximum_fusion), channel_id=1, source_target_pairs={{0,1},{1,0},{2,3},{3,2},{4,5},{5,4},{6,7},{7,6},{8,9},{9,8},{10,11... | collective-permute-start | bytes 6291464 | tf_op jit(solution)/shard_map/ppermute | solution.py:149
  21.5 8.1 %collective-permute-start.3 = (bf16[2,256,128]{2,1,0:T(8,128)(2,1)}, bf16[2,256,128]{2,1,0:T(8,128)(2,1)S(1)}, u32[]{:S(2)}, u32[]{:S(2)}) collective-permute-start(bf16[2,256,128]{2,1,0:T(8,128)(2,1)} %get-tuple-element.37), channel_id=1, source_target_pairs={{0,6},{2,0},{4,2},{6,4},{1,7},{3,1},{5,3},{7,5},{8,14},{10,8},{12,... | collective-permute-start | bytes 393224 | tf_op jit(solution)/shard_map/ppermute | solution.py:145
  25.4 7.5 %collective-permute-start.2 = (bf16[2,256,128]{2,1,0:T(8,128)(2,1)}, bf16[2,256,128]{2,1,0:T(8,128)(2,1)S(1)}, u32[]{:S(2)}, u32[]{:S(2)}) collective-permute-start(bf16[2,256,128]{2,1,0:T(8,128)(2,1)} %get-tuple-element.37), channel_id=1, source_target_pairs={{0,2},{2,4},{4,6},{6,0},{1,3},{3,5},{5,7},{7,1},{8,10},{10,12},{12... | collective-permute-start | bytes 393224 | tf_op jit(solution)/shard_map/ppermute | solution.py:145
  25.5 7.6 %collective-permute-start.11 = (bf16[2,256,128]{2,1,0:T(8,128)(2,1)S(1)}, bf16[2,256,128]{2,1,0:T(8,128)(2,1)S(1)}, u32[]{:S(2)}, u32[]{:S(2)}) collective-permute-start(bf16[2,256,128]{2,1,0:T(8,128)(2,1)S(1)} %get-tuple-element.36), channel_id=1, source_target_pairs={{0,24},{8,0},{16,8},{24,16},{1,25},{9,1},{17,9},{25,17},{2,26},{10... | collective-permute-start | bytes 393224 | tf_op jit(solution)/shard_map/ppermute | solution.py:145
  28.3 7.7 %collective-permute-start.10 = (bf16[2,256,128]{2,1,0:T(8,128)(2,1)S(1)}, bf16[2,256,128]{2,1,0:T(8,128)(2,1)S(1)}, u32[]{:S(2)}, u32[]{:S(2)}) collective-permute-start(bf16[2,256,128]{2,1,0:T(8,128)(2,1)S(1)} %get-tuple-element.36), channel_id=1, source_target_pairs={{0,8},{8,16},{16,24},{24,0},{1,9},{9,17},{17,25},{25,1},{2,10},{10... | collective-permute-start | bytes 393224 | tf_op jit(solution)/shard_map/ppermute | solution.py:145
  29.5 6.6 %collective-permute-start.5 = (bf16[256,128]{1,0:T(8,128)(2,1)S(1)}, bf16[256,128]{1,0:T(8,128)(2,1)S(1)}, u32[]{:S(2)}, u32[]{:S(2)}) collective-permute-start(bf16[256,128]{1,0:T(8,128)(2,1)S(1)} %slice_bitcast_fusion.8), channel_id=1, source_target_pairs={{0,6},{2,0},{4,2},{6,4},{1,7},{3,1},{5,3},{7,5},{8,14},{10,8},{12,... | collective-permute-start | bytes 196616 | tf_op jit(solution)/shard_map/ppermute | solution.py:145
  33.0 4.9 %collective-permute-start.4 = (bf16[256,128]{1,0:T(8,128)(2,1)S(1)}, bf16[256,128]{1,0:T(8,128)(2,1)S(1)}, u32[]{:S(2)}, u32[]{:S(2)}) collective-permute-start(bf16[256,128]{1,0:T(8,128)(2,1)S(1)} %slice_bitcast_fusion.9), channel_id=1, source_target_pairs={{0,2},{2,4},{4,6},{6,0},{1,3},{3,5},{5,7},{7,1},{8,10},{10,12},{12... | collective-permute-start | bytes 196616 | tf_op jit(solution)/shard_map/ppermute | solution.py:145
  33.1 7.8 %collective-permute-start.13 = (bf16[256,128]{1,0:T(8,128)(2,1)S(1)}, bf16[256,128]{1,0:T(8,128)(2,1)S(1)}, u32[]{:S(2)}, u32[]{:S(2)}) collective-permute-start(bf16[256,128]{1,0:T(8,128)(2,1)S(1)} %slice_bitcast_fusion.6), channel_id=1, source_target_pairs={{0,24},{8,0},{16,8},{24,16},{1,25},{9,1},{17,9},{25,17},{2,26},{10... | collective-permute-start | bytes 196616 | tf_op jit(solution)/shard_map/ppermute | solution.py:145
  36.0 5.0 %collective-permute-start.12 = (bf16[256,128]{1,0:T(8,128)(2,1)S(1)}, bf16[256,128]{1,0:T(8,128)(2,1)S(1)}, u32[]{:S(2)}, u32[]{:S(2)}) collective-permute-start(bf16[256,128]{1,0:T(8,128)(2,1)S(1)} %slice_bitcast_fusion.7), channel_id=1, source_target_pairs={{0,8},{8,16},{16,24},{24,0},{1,9},{9,17},{17,25},{25,1},{2,10},{10... | collective-permute-start | bytes 196616 | tf_op jit(solution)/shard_map/ppermute | solution.py:145
  38.0 22.7 %copy-start.26 = (s32[64]{0:T(128)S(1)}, s32[64]{0:T(128)}, u32[]{:S(2)}) copy-start(s32[64]{0:T(128)} %param.22) | copy-start | bytes 772
  38.0 13.2 %collective-permute-start.6 = (bf16[4,2,256,128]{3,2,1,0:T(8,128)(2,1)S(1)}, bf16[4,2,256,128]{3,2,1,0:T(8,128)(2,1)S(1)}, u32[]{:S(2)}, u32[]{:S(2)}) collective-permute-start(bf16[4,2,256,128]{3,2,1,0:T(8,128)(2,1)S(1)} %pad_maximum_fusion.1.rest_0_), channel_id=1, source_target_pairs={{0,8},{8,16},{16,24},{24,0},{1,9},{9,17},{17,25},{25,1},{2,10},{10... | collective-permute-start | bytes 1572872 | tf_op jit(solution)/shard_map/ppermute | solution.py:145
  39.1 12.9 %collective-permute-start.7 = (bf16[4,2,256,128]{3,2,1,0:T(8,128)(2,1)S(1)}, bf16[4,2,256,128]{3,2,1,0:T(8,128)(2,1)S(1)}, u32[]{:S(2)}, u32[]{:S(2)}) collective-permute-start(bf16[4,2,256,128]{3,2,1,0:T(8,128)(2,1)S(1)} %pad_maximum_fusion.1.rest_0_), channel_id=1, source_target_pairs={{0,24},{8,0},{16,8},{24,16},{1,25},{9,1},{17,9},{25,17},{2,26},{10... | collective-permute-start | bytes 1572872 | tf_op jit(solution)/shard_map/ppermute | solution.py:145
  41.1 11.6 %copy-start.19 = (bf16[4,2,256,128]{3,2,0,1:T(8,128)(2,1)}, bf16[4,2,256,128]{3,2,0,1:T(8,128)(2,1)S(1)}, u32[]{:S(2)}) copy-start(bf16[4,2,256,128]{3,2,0,1:T(8,128)(2,1)S(1)} %pad_maximum_fusion.2) | copy-start | bytes 1572868
  41.1 15.0 %collective-permute-start.14 = (bf16[4,2,256,128]{3,2,0,1:T(8,128)(2,1)S(1)}, bf16[4,2,256,128]{3,2,0,1:T(8,128)(2,1)S(1)}, u32[]{:S(2)}, u32[]{:S(2)}) collective-permute-start(bf16[4,2,256,128]{3,2,0,1:T(8,128)(2,1)S(1)} %pad_maximum_fusion.2), channel_id=1, source_target_pairs={{0,2},{2,4},{4,6},{6,0},{1,3},{3,5},{5,7},{7,1},{8,10},{10,12},{12... | collective-permute-start | bytes 1572872 | tf_op jit(solution)/shard_map/ppermute | solution.py:145
  41.3 16.5 %collective-permute-start.15 = (bf16[4,2,256,128]{3,2,0,1:T(8,128)(2,1)S(1)}, bf16[4,2,256,128]{3,2,0,1:T(8,128)(2,1)S(1)}, u32[]{:S(2)}, u32[]{:S(2)}) collective-permute-start(bf16[4,2,256,128]{3,2,0,1:T(8,128)(2,1)S(1)} %pad_maximum_fusion.2), channel_id=1, source_target_pairs={{0,6},{2,0},{4,2},{6,4},{1,7},{3,1},{5,3},{7,5},{8,14},{10,8},{12,... | collective-permute-start | bytes 1572872 | tf_op jit(solution)/shard_map/ppermute | solution.py:145
  51.2 12.1 %copy-start.7 = (bf16[4,2,256,128]{3,2,1,0:T(8,128)(2,1)}, bf16[4,2,256,128]{3,2,1,0:T(8,128)(2,1)S(1)}, u32[]{:S(2)}) copy-start(bf16[4,2,256,128]{3,2,1,0:T(8,128)(2,1)S(1)} %collective-permute-done.6.rest_1_) | copy-start | bytes 1572868
  51.9 13.5 %collective-permute-start.8 = (bf16[4,256,128]{2,1,0:T(8,128)(2,1)}, bf16[4,256,128]{2,1,0:T(8,128)(2,1)S(1)}, u32[]{:S(2)}, u32[]{:S(2)}) collective-permute-start(bf16[4,256,128]{2,1,0:T(8,128)(2,1)} %slice_bitcast_fusion.3), channel_id=1, source_target_pairs={{0,8},{8,16},{16,24},{24,0},{1,9},{9,17},{17,25},{25,1},{2,10},{10... | collective-permute-start | bytes 786440 | tf_op jit(solution)/shard_map/ppermute | solution.py:145
  52.7 0.8 copy-start.9
  53.5 24.4 %collective-permute-start.9 = (bf16[4,256,128]{2,1,0:T(8,128)(2,1)}, bf16[4,256,128]{2,1,0:T(8,128)(2,1)}, u32[]{:S(2)}, u32[]{:S(2)}) collective-permute-start(bf16[4,256,128]{2,1,0:T(8,128)(2,1)} %slice_bitcast_fusion.2), channel_id=1, source_target_pairs={{0,24},{8,0},{16,8},{24,16},{1,25},{9,1},{17,9},{25,17},{2,26},{10... | collective-permute-start | bytes 786440 | tf_op jit(solution)/shard_map/ppermute | solution.py:145
  56.2 1.6 copy-start.20
  56.9 21.0 %collective-permute-start.16 = (bf16[4,256,128]{2,1,0:T(8,128)(2,1)}, bf16[4,256,128]{2,1,0:T(8,128)(2,1)}, u32[]{:S(2)}, u32[]{:S(2)}) collective-permute-start(bf16[4,256,128]{2,1,0:T(8,128)(2,1)} %slice_bitcast_fusion.1), channel_id=1, source_target_pairs={{0,2},{2,4},{4,6},{6,0},{1,3},{3,5},{5,7},{7,1},{8,10},{10,12},{12... | collective-permute-start | bytes 786440 | tf_op jit(solution)/shard_map/ppermute | solution.py:145
  57.8 0.9 copy-start.21
  58.7 19.2 %collective-permute-start.17 = (bf16[4,256,128]{2,1,0:T(8,128)(2,1)}, bf16[4,256,128]{2,1,0:T(8,128)(2,1)}, u32[]{:S(2)}, u32[]{:S(2)}) collective-permute-start(bf16[4,256,128]{2,1,0:T(8,128)(2,1)} %slice_bitcast_fusion), channel_id=1, source_target_pairs={{0,6},{2,0},{4,2},{6,4},{1,7},{3,1},{5,3},{7,5},{8,14},{10,8},{12,... | collective-permute-start | bytes 786440 | tf_op jit(solution)/shard_map/ppermute | solution.py:145
  60.9 17.0 %copy-start.2 = (bf16[128,8192]{1,0:T(8,128)(2,1)S(1)}, bf16[128,8192]{1,0:T(8,128)(2,1)}, u32[]{:S(2)}) copy-start(bf16[128,8192]{1,0:T(8,128)(2,1)} %copy-done.1) | copy-start | bytes 6291460
  60.9 17.0 %copy-start.10 = (bf16[4,2,256,128]{3,2,1,0:T(8,128)(2,1)S(1)}, bf16[4,2,256,128]{3,2,1,0:T(8,128)(2,1)}, u32[]{:S(2)}) copy-start(bf16[4,2,256,128]{3,2,1,0:T(8,128)(2,1)} %copy-done.9) | copy-start | bytes 1572868
  65.5 87.8 %collective-permute-start.20 = (bf16[128,16]{0,1:T(8,128)(2,1)S(1)}, bf16[128,16]{0,1:T(8,128)(2,1)S(1)}, u32[]{:S(2)}, u32[]{:S(2)}) collective-permute-start(bf16[128,16]{0,1:T(8,128)(2,1)S(1)} %fusion.9), channel_id=1, source_target_pairs={{0,1},{1,0},{2,3},{3,2},{4,5},{5,4},{6,7},{7,6},{8,9},{9,8},{10,11... | collective-permute-start | bytes 12296 | tf_op jit(solution)/shard_map/ppermute | solution.py:149
  77.9 1.6 copy-start.5
  79.5 1.0 copy-start.8
  112.3 1.0 copy-start.12
  114.2 1.6 copy-start.3
  115.7 1.6 copy-start.6
  117.3 2.2 %copy-start.11 = (bf16[32,2,256,128]{3,2,1,0:T(8,128)(2,1)S(1)}, bf16[32,2,256,128]{3,2,1,0:T(8,128)(2,1)}, u32[]{:S(2)}) copy-start(bf16[32,2,256,128]{3,2,1,0:T(8,128)(2,1)} %all-gather.3.cloned.1.call-done) | copy-start | bytes 12582916
  119.5 32.2 %copy-start.14 = (bf16[128,4096]{1,0:T(8,128)(2,1)S(1)}, bf16[128,4096]{1,0:T(8,128)(2,1)}, u32[]{:S(2)}) copy-start(bf16[128,4096]{1,0:T(8,128)(2,1)} %constant_dynamic-update-slice_fusion.5) | copy-start | bytes 3145732
  119.5 32.3 %copy-start.23 = (bf16[16,8192]{1,0:T(8,128)(2,1)S(1)}, bf16[16,8192]{1,0:T(8,128)(2,1)}, u32[]{:S(2)}) copy-start(bf16[16,8192]{1,0:T(8,128)(2,1)} %param.18) | copy-start | bytes 786436
  151.7 2.5 %copy-start.13 = (bf16[128,2048]{1,0:T(8,128)(2,1)}, bf16[128,2048]{1,0:T(8,128)(2,1)S(1)}, u32[]{:S(2)}) copy-start(bf16[128,2048]{1,0:T(8,128)(2,1)S(1)} %get-tuple-element.14) | copy-start | bytes 1572868
  151.7 2.5 %copy-start.15 = (bf16[128,4096]{1,0:T(8,128)(2,1)S(1)}, bf16[128,4096]{1,0:T(8,128)(2,1)}, u32[]{:S(2)}) copy-start(bf16[128,4096]{1,0:T(8,128)(2,1)} %constant_dynamic-update-slice_fusion.3) | copy-start | bytes 3145732
  152.2 3.1 %collective-permute-start.21 = (f32[128,16]{0,1:T(8,128)S(1)}, f32[128,16]{0,1:T(8,128)S(1)}, u32[]{:S(2)}, u32[]{:S(2)}) collective-permute-start(f32[128,16]{0,1:T(8,128)S(1)} %fusion.24), channel_id=1, source_target_pairs={{0,1},{1,0},{2,3},{3,2},{4,5},{5,4},{6,7},{7,6},{8,9},{9,8},{10,11... | collective-permute-start | bytes 24584 | tf_op jit(solution)/shard_map/ppermute | solution.py:149
  154.3 1.0 copy-start.16
  159.0 1.6 collective-permute-start.22
  160.6 1.1 copy-start.17
  162.4 6.0 %collective-permute-start.25 = (bf16[32,1024]{1,0:T(8,128)(2,1)}, bf16[32,1024]{1,0:T(8,128)(2,1)}, u32[]{:S(2)}, u32[]{:S(2)}) collective-permute-start(bf16[32,1024]{1,0:T(8,128)(2,1)} %get-tuple-element.31), channel_id=1, source_target_pairs={{0,6},{2,0},{4,2},{6,4},{1,7},{3,1},{5,3},{7,5},{8,14},{10,8},{12,... | collective-permute-start | bytes 196616 | tf_op jit(solution)/shard_map/ppermute | solution.py:145
  165.1 4.8 %collective-permute-start.24 = (bf16[32,1024]{1,0:T(8,128)(2,1)S(1)}, bf16[32,1024]{1,0:T(8,128)(2,1)}, u32[]{:S(2)}, u32[]{:S(2)}) collective-permute-start(bf16[32,1024]{1,0:T(8,128)(2,1)S(1)} %get-tuple-element.30), channel_id=1, source_target_pairs={{0,4},{2,6},{4,0},{6,2},{1,5},{3,7},{5,1},{7,3},{8,12},{10,14},{12... | collective-permute-start | bytes 196616 | tf_op jit(solution)/shard_map/ppermute | solution.py:145
  165.1 5.6 %collective-permute-start.23 = (bf16[32,1024]{1,0:T(8,128)(2,1)S(1)}, bf16[32,1024]{1,0:T(8,128)(2,1)}, u32[]{:S(2)}, u32[]{:S(2)}) collective-permute-start(bf16[32,1024]{1,0:T(8,128)(2,1)S(1)} %get-tuple-element.29), channel_id=1, source_target_pairs={{0,2},{2,4},{4,6},{6,0},{1,3},{3,5},{5,7},{7,1},{8,10},{10,12},{12... | collective-permute-start | bytes 196616 | tf_op jit(solution)/shard_map/ppermute | solution.py:145
  171.8 4.7 %collective-permute-start.26 = (bf16[32,1024]{1,0:T(8,128)(2,1)S(1)}, bf16[32,1024]{1,0:T(8,128)(2,1)S(1)}, u32[]{:S(2)}, u32[]{:S(2)}) collective-permute-start(bf16[32,1024]{1,0:T(8,128)(2,1)S(1)} %fusion.19), channel_id=1, source_target_pairs={{0,16},{8,24},{16,0},{24,8},{1,17},{9,25},{17,1},{25,9},{2,18},{10... | collective-permute-start | bytes 196616 | tf_op jit(solution)/shard_map/ppermute | solution.py:145
  173.5 4.6 %collective-permute-start.27 = (bf16[32,1024]{1,0:T(8,128)(2,1)S(1)}, bf16[32,1024]{1,0:T(8,128)(2,1)S(1)}, u32[]{:S(2)}, u32[]{:S(2)}) collective-permute-start(bf16[32,1024]{1,0:T(8,128)(2,1)S(1)} %fusion.19), channel_id=1, source_target_pairs={{0,8},{8,16},{16,24},{24,0},{1,9},{9,17},{17,25},{25,1},{2,10},{10... | collective-permute-start | bytes 196616 | tf_op jit(solution)/shard_map/ppermute | solution.py:145
  173.5 4.6 %collective-permute-start.28 = (bf16[32,1024]{1,0:T(8,128)(2,1)S(1)}, bf16[32,1024]{1,0:T(8,128)(2,1)S(1)}, u32[]{:S(2)}, u32[]{:S(2)}) collective-permute-start(bf16[32,1024]{1,0:T(8,128)(2,1)S(1)} %fusion.19), channel_id=1, source_target_pairs={{0,24},{8,0},{16,8},{24,16},{1,25},{9,1},{17,9},{25,17},{2,26},{10... | collective-permute-start | bytes 196616 | tf_op jit(solution)/shard_map/ppermute | solution.py:145
  178.2 5.5 %collective-permute-start.29 = (bf16[32,1024]{1,0:T(8,128)(2,1)S(1)}, bf16[32,1024]{1,0:T(8,128)(2,1)S(1)}, u32[]{:S(2)}, u32[]{:S(2)}) collective-permute-start(bf16[32,1024]{1,0:T(8,128)(2,1)S(1)} %add_convert_fusion.1), channel_id=1, source_target_pairs={{0,64},{32,96},{64,0},{96,32},{1,65},{33,97},{65,1},{97,33},{2,66}... | collective-permute-start | bytes 196616 | tf_op jit(solution)/shard_map/ppermute | solution.py:145
  181.0 4.3 %collective-permute-start.30 = (bf16[32,1024]{1,0:T(8,128)(2,1)S(1)}, bf16[32,1024]{1,0:T(8,128)(2,1)S(1)}, u32[]{:S(2)}, u32[]{:S(2)}) collective-permute-start(bf16[32,1024]{1,0:T(8,128)(2,1)S(1)} %add_convert_fusion.1), channel_id=1, source_target_pairs={{0,32},{32,64},{64,96},{96,0},{1,33},{33,65},{65,97},{97,1},{2,34}... | collective-permute-start | bytes 196616 | tf_op jit(solution)/shard_map/ppermute | solution.py:145
  181.4 3.9 %collective-permute-start.31 = (bf16[32,1024]{1,0:T(8,128)(2,1)S(1)}, bf16[32,1024]{1,0:T(8,128)(2,1)S(1)}, u32[]{:S(2)}, u32[]{:S(2)}) collective-permute-start(bf16[32,1024]{1,0:T(8,128)(2,1)S(1)} %add_convert_fusion.1), channel_id=1, source_target_pairs={{0,96},{32,0},{64,32},{96,64},{1,97},{33,1},{65,33},{97,65},{2,98}... | collective-permute-start | bytes 196616 | tf_op jit(solution)/shard_map/ppermute | solution.py:145
  185.4 9.0 %collective-permute-start.32 = (bf16[32,1024]{1,0:T(8,128)(2,1)S(1)}, bf16[32,1024]{1,0:T(8,128)(2,1)S(1)}, u32[]{:S(2)}, u32[]{:S(2)}) collective-permute-start(bf16[32,1024]{1,0:T(8,128)(2,1)S(1)} %add_convert_fusion), channel_id=1, source_target_pairs={{0,4},{2,6},{4,0},{6,2},{1,5},{3,7},{5,1},{7,3},{8,12},{10,14},{12... | collective-permute-start | bytes 196616 | tf_op jit(solution)/shard_map/ppermute | solution.py:145
  186.5 7.9 %collective-permute-start.33 = (bf16[32,1024]{1,0:T(8,128)(2,1)S(1)}, bf16[32,1024]{1,0:T(8,128)(2,1)S(1)}, u32[]{:S(2)}, u32[]{:S(2)}) collective-permute-start(bf16[32,1024]{1,0:T(8,128)(2,1)S(1)} %add_convert_fusion), channel_id=1, source_target_pairs={{0,2},{2,4},{4,6},{6,0},{1,3},{3,5},{5,7},{7,1},{8,10},{10,12},{12... | collective-permute-start | bytes 196616 | tf_op jit(solution)/shard_map/ppermute | solution.py:145
  188.3 6.1 %collective-permute-start.34 = (bf16[32,1024]{1,0:T(8,128)(2,1)S(1)}, bf16[32,1024]{1,0:T(8,128)(2,1)S(1)}, u32[]{:S(2)}, u32[]{:S(2)}) collective-permute-start(bf16[32,1024]{1,0:T(8,128)(2,1)S(1)} %add_convert_fusion), channel_id=1, source_target_pairs={{0,6},{2,0},{4,2},{6,4},{1,7},{3,1},{5,3},{7,5},{8,14},{10,8},{12,... | collective-permute-start | bytes 196616 | tf_op jit(solution)/shard_map/ppermute | solution.py:145
  189.2 7.7 %collective-permute-start.18 = (bf16[128,2048]{1,0:T(8,128)(2,1)}, bf16[128,2048]{1,0:T(8,128)(2,1)S(1)}, u32[]{:S(2)}, u32[]{:S(2)}) collective-permute-start(bf16[128,2048]{1,0:T(8,128)(2,1)} %copy-done.12), channel_id=1, source_target_pairs={{0,1},{1,0},{2,3},{3,2},{4,5},{5,4},{6,7},{7,6},{8,9},{9,8},{10,11... | collective-permute-start | bytes 1572872 | tf_op jit(solution)/shard_map/ppermute | solution.py:149
  194.4 2.5 %collective-permute-start.19 = (bf16[128,2048]{1,0:T(8,128)(2,1)}, bf16[128,2048]{1,0:T(8,128)(2,1)S(1)}, u32[]{:S(2)}, u32[]{:S(2)}) collective-permute-start(bf16[128,2048]{1,0:T(8,128)(2,1)} %copy-done.13), channel_id=1, source_target_pairs={{0,1},{1,0},{2,3},{3,2},{4,5},{5,4},{6,7},{7,6},{8,9},{9,8},{10,11... | collective-permute-start | bytes 1572872 | tf_op jit(solution)/shard_map/ppermute | solution.py:149
  194.6 3.9 %collective-permute-start.35 = (bf16[32,4096]{1,0:T(8,128)(2,1)S(1)}, bf16[32,4096]{1,0:T(8,128)(2,1)S(1)}, u32[]{:S(2)}, u32[]{:S(2)}) collective-permute-start(bf16[32,4096]{1,0:T(8,128)(2,1)S(1)} %pad_maximum_fusion.4), channel_id=1, source_target_pairs={{0,1},{1,0},{2,3},{3,2},{4,5},{5,4},{6,7},{7,6},{8,9},{9,8},{10,11... | collective-permute-start | bytes 786440 | tf_op jit(solution)/shard_map/ppermute | solution.py:149
  198.5 1.0 copy-start.24
  198.5 1.8 copy-start.25
Sparse Core Ops, SparseCore 0:
  13.9 64.0 all-gather.2

commit v2 on v1

v2 whole, which is shorter than its diff:
```python
import functools
import math

import jax
import jax.numpy as jnp
from jax import lax
from jax.experimental import pallas as pl
from jax.experimental.pallas import tpu as pltpu
from jax.sharding import Mesh, PartitionSpec as P

D = 128
HEADS = 32
NBMAX = 12
GAIN = 2.0
SCALE = D**-0.5
EXP2_SCALE = SCALE * math.log2(math.e)
F32, BF16 = jnp.float32, jnp.bfloat16
NT = (((1,), (1,)), ((), ()))
NN = (((1,), (0,)), ((), ()))
TN = (((0,), (0,)), ((), ()))


def attend(quads, lists, bases, g, kv, kvt, w_ref, s_ref, queries, cots):
    def rows(i, part=0, parts=1):
        return pl.ds((512 * i) + part * (512 // parts), 512 // parts)

    def fold(x, op):
        return op(x.reshape(x.shape[0] // 8, 8, D), axis=0)

    def scores(t, out):
        w_ref[t, 0:D, 0:D] = queries[t]
        w_ref[t, D : 2 * D, D : 2 * D] = cots[t]
        w = w_ref[t]
        top = jnp.full((8, D), -jnp.inf, F32)
        for i in range(quads):
            tiles = []
            for j in range(4):
                n = lists[bases[t] + 4 * i + j]
                tiles.append(kv[g, n // 2, pl.ds(pl.multiple_of((n % 2) * D, D), D), :])
            both = lax.dot_general(
                jnp.concatenate(tiles, axis=0), w, NT, preferred_element_type=F32
            )
            s_ref[t, rows(i), :] = both
            top = jnp.maximum(top, fold(both[:, :D], jnp.max))
            yield
        out.append(jnp.max(top, axis=0, keepdims=True))

    def weights(t, largest, out):
        total = jnp.zeros((8, D), F32)
        inner = jnp.zeros((8, D), F32)
        for i in range(quads):
            for part in range(4):
                r = rows(i, part, 4)
                e = jnp.exp2((s_ref[t, r, 0:D] - largest) * EXP2_SCALE)
                s_ref[t, r, 0:D] = e
                total += fold(e, jnp.sum)
                inner += fold(e * s_ref[t, r, D : 2 * D], jnp.sum)
            yield
        inverse = 1.0 / jnp.sum(total, axis=0, keepdims=True)
        out.append((inverse, jnp.sum(inner, axis=0, keepdims=True) * inverse))

    def products(t, inverse, inner, res):
        out = jnp.zeros((D, D), F32)
        grad = jnp.zeros((D, D), F32)
        for i in range(quads):
            e = s_ref[t, rows(i), 0:D]
            ds = e * (s_ref[t, rows(i), D : 2 * D] - inner)
            x = jnp.concatenate([e.astype(BF16), ds.astype(BF16)], axis=1)
            cols = []
            for j in range(4):
                n = lists[bases[t] + 4 * i + j]
                cols.append(kvt[:, pl.ds(pl.multiple_of(n * D, D), D)])
            r = lax.dot_general(jnp.concatenate(cols, axis=1), x, NN, preferred_element_type=F32)
            out += r[D : 2 * D, 0:D]
            grad += r[0:D, D : 2 * D]
            yield
        res.append(((out * inverse).T.astype(BF16), (grad * (inverse * SCALE)).T.astype(BF16)))

    def together(*stages):
        stages = list(stages)
        while stages:
            stages = [s for s in stages if next(s, stages) is not stages]

    tops, sums, results = ([], []), ([], []), []
    together(scores(0, tops[0]))
    together(weights(0, tops[0][0], sums[0]), scores(1, tops[1]))
    together(products(0, *sums[0][0], results), weights(1, tops[1][0], sums[1]))
    together(products(1, *sums[1][0], results))
    return results


def attention_kernel(n_src, copies, lists, live, off, q_own, g_own, qg_far, *rest):
    srcs = rest[:n_src]
    o_own, o_far, d_own, d_far, kv, kvt, w_ref, s_ref, sem = rest[n_src:]
    step = pl.program_id(0)
    del off

    def copy(g, i):
        src, view, lo, size, col = copies[g][i]
        return pltpu.make_async_copy(
            view(srcs[src]), kv.at[g, lo : lo + size, :, col : col + D], sem.at[g, i]
        )

    @pl.when(step == 0)
    def _():
        for g in range(4):
            for i in range(len(copies[g])):
                copy(g, i).start()
        w_ref[...] = jnp.zeros_like(w_ref)

    for g in range(4):

        @pl.when(step == 8 * g)
        def _():
            for i in range(len(copies[g])):
                copy(g, i).wait()

    g = step // 8

    @pl.when(step % 8 == 0)
    def _():
        def turn(chip, _):
            kvt[:, pl.ds(pl.multiple_of(chip * 256, 256), 256)] = kv[g, chip].T
            return 0

        lax.fori_loop(0, 16, turn, 0)

    for quads in (1, 2, 3):

        @pl.when(live[step] == 4 * quads)
        def _():
            bases = (step * 24, step * 24 + 12)
            first, second = attend(
                quads,
                lists,
                bases,
                g,
                kv,
                kvt,
                w_ref,
                s_ref,
                (q_own[...], qg_far[0]),
                (g_own[...], qg_far[1]),
            )
            o_own[...], d_own[...] = first
            o_far[...], d_far[...] = second


def attention(lists, live, off, q_all, g_all, qg_far, srcs, copies):
    whole = pl.BlockSpec((D, D), lambda h, a, b, off: (0, off[0] + h))
    far = pl.BlockSpec((2, D, D), lambda h, a, b, off: (0, 0, h))
    res = pl.BlockSpec((D, D), lambda h, a, b, off: (0, h))
    shape = jax.ShapeDtypeStruct((D, HEADS * D), BF16)
    n_copies = max(len(c) for c in copies)
    return pl.pallas_call(
        functools.partial(attention_kernel, len(srcs), copies),
        out_shape=(shape,) * 4,
        grid_spec=pltpu.PrefetchScalarGridSpec(
            num_scalar_prefetch=3,
            grid=(HEADS,),
            in_specs=[whole, whole, far] + [pl.BlockSpec(memory_space=pl.ANY)] * len(srcs),
            out_specs=(res,) * 4,
            scratch_shapes=[
                pltpu.VMEM((4, 16, 256, 2 * D), BF16),
                pltpu.VMEM((2 * D, 4096), BF16),
                pltpu.VMEM((2, 2 * D, 2 * D), BF16),
                pltpu.VMEM((2, NBMAX * D, 2 * D), F32),
                pltpu.SemaphoreType.DMA((4, n_copies)),
            ],
        ),
        compiler_params=pltpu.CompilerParams(
            dimension_semantics=("arbitrary",), vmem_limit_bytes=40 << 20
        ),
        cost_estimate=pl.CostEstimate(
            flops=64 * 8 * 8 * D * D * D, bytes_accessed=16 << 20, transcendentals=64 * 8 * D * D
        ),
        name="attend",
    )(lists, live, off, q_all, g_all, qg_far, *srcs)


def hop(x, axis, by):
    return lax.ppermute(x, axis, [(i, (i + by) % 4) for i in range(4)])


def swap(x):
    return lax.ppermute(x, "core", [(0, 1), (1, 0)])


def ring_gather(own, first, second):
    less, more = hop(own, first, 1), hop(own, first, -1)
    k2, v2 = hop(less[0], first, 1), hop(more[1], first, -1)
    line = jnp.stack([own, less, more, jnp.stack([k2, v2])])
    less, more = hop(line, second, 1), hop(line, second, -1)
    k2, v2 = hop(less[:, 0], second, 1), hop(more[:, 1], second, -1)
    return [line, less, more, k2, v2]


def ring_copies(first_src, head):
    pick = []
    for s in range(3):
        for k in range(2):
            pick.append((first_src + s, lambda r, k=k: r.at[:, k, head], 4 * s, 4, k * D))
    for k in range(2):
        pick.append((first_src + 3 + k, lambda r: r.at[:, head], 12, 4, k * D))
    return pick


def in_order(own, others, index):
    have = [own, *others]
    out = []
    for j in range(4):
        back = (index - j) % 4
        pick = have[3]
        for d in range(3):
            pick = jnp.where(back == d, have[d], pick)
        out.append(pick)
    return out


def exchange(x, axis):
    return [hop(x, axis, d) for d in (1, 2, 3)]


def all_sum(x, axis):
    low = x.astype(BF16)
    parts = in_order(low, exchange(low, axis), lax.axis_index(axis))
    return sum(p.astype(F32) for p in parts)


def body(x, frozen, keys, values, cot, down, up, noise_down, noise_up, lists, live):
    x, frozen, keys, values, cot = x[0], frozen[0], keys[0], values[0], cot[0]
    core, y, z = lax.axis_index("core"), lax.axis_index("y"), lax.axis_index("z")
    chip = y * 4 + z
    half = HEADS * D

    kv = jnp.stack([keys, values])
    mine = lax.dynamic_slice_in_dim(kv, core * 512, 512, 2)
    far = swap(lax.dynamic_slice_in_dim(kv, (1 - core) * 512, 512, 2))
    kv = jnp.where(core == 0, jnp.concatenate([mine, far], 1), jnp.concatenate([far, mine], 1))
    kv = kv.reshape(2, 256, 4, D).transpose(0, 2, 1, 3)
    ring_a = ring_gather(kv[:, :2], "z", "y")
    ring_b = ring_gather(kv[:, 2:], "y", "z")

    x, frozen, cot, _, _ = lax.optimization_barrier((x, frozen, cot, ring_a[0], ring_b[0]))

    low = jnp.dot(x, down, preferred_element_type=F32).astype(BF16)
    query = (frozen.astype(F32) + GAIN * jnp.dot(low, up, preferred_element_type=F32)).astype(BF16)
    away = (1 - core) * half
    qg_far = swap(
        jnp.stack(
            [
                lax.dynamic_slice_in_dim(query, away, half, 1),
                lax.dynamic_slice_in_dim(cot, away, half, 1),
            ]
        )
    )
    low_far = swap(low)

    mylists = lax.dynamic_slice(lists, (core * HEADS, chip * 2, 0), (HEADS, 2, NBMAX))
    mylists = jnp.where(core == 0, mylists, mylists[:, ::-1])
    mylive = lax.dynamic_slice_in_dim(live, core * HEADS, HEADS, 0)
    place = jnp.array([0, 2, 3, 1], jnp.int32)
    at_y = place[(mylists // 8 - y) % 4]
    at_z = place[(mylists // 2 - z) % 4]
    low_bit = mylists % 2
    spot = jnp.concatenate(
        [
            (at_y * 8 + at_z * 2 + low_bit)[:16],
            (at_z * 8 + at_y * 2 + low_bit)[16:],
        ]
    )
    own_half, far_half, d_own, d_far = attention(
        spot.reshape(-1),
        mylive,
        jnp.reshape(core * HEADS, (1,)),
        query,
        cot,
        qg_far,
        ring_a + ring_b,
        [ring_copies(0, 0), ring_copies(0, 1), ring_copies(5, 0), ring_copies(5, 1)],
    )

    far_half = swap(far_half)
    attended = jnp.where(
        core == 0,
        jnp.concatenate([own_half, far_half], 1),
        jnp.concatenate([far_half, own_half], 1),
    )

    my_up = lax.dynamic_slice_in_dim(up, core * half, half, 1)
    low_grad_far = swap(lax.dot_general(d_far, my_up, NT, preferred_element_type=F32))
    low_grad = lax.dot_general(d_own, my_up, NT, preferred_element_type=F32) + low_grad_far
    low_grad = (GAIN * low_grad).astype(BF16)
    grad_up = GAIN * (
        lax.dot_general(low, d_own, TN, preferred_element_type=F32)
        + lax.dot_general(low_far, d_far, TN, preferred_element_type=F32)
    )
    grad_down = lax.dot_general(low_grad, x, TN, preferred_element_type=F32)
    down_mine = lax.dynamic_slice_in_dim(grad_down, core * half, half, 1)
    down_away = lax.dynamic_slice_in_dim(grad_down, (1 - core) * half, half, 1)
    down_mine = down_mine + swap(down_away.astype(BF16)).astype(F32)

    total = jnp.concatenate([grad_up, down_mine], axis=0)
    quarter = half // 4
    pieces = [
        lax.dynamic_slice_in_dim(total, ((z + d) % 4) * quarter, quarter, 1) for d in range(4)
    ]
    total = pieces[0] + sum(hop(pieces[d].astype(BF16), "z", d).astype(F32) for d in (1, 2, 3))
    total = all_sum(all_sum(total, "y"), "dp").astype(BF16)
    total = jnp.concatenate(in_order(total, exchange(total, "z"), z), axis=1)
    other = swap(total)
    total = jnp.where(
        core == 0, jnp.concatenate([total, other], 1), jnp.concatenate([other, total], 1)
    ).astype(F32)
    norm = (4 * 32 * x.shape[0]) ** -0.5
    step_up = total[:16] * norm + noise_up
    step_down = (total[16:] * norm).T + noise_down
    return attended[None], step_down, step_up


def solution(mesh):
    fine = Mesh(mesh.devices.reshape(4, 4, 4, 2), ("dp", "y", "z", "core"))
    rows = P("dp", ("y", "z", "core"), None)
    return jax.shard_map(
        body,
        mesh=fine,
        in_specs=(rows,) * 5 + (P(),) * 6,
        out_specs=(rows, P(), P()),
        check_vma=False,
    )
```

time: 211 us -> 181 us (0.86); the launches traced: 208 us -> 181 us
  between operations: 14.6 us -> 1.12 us
  waiting for transfers between devices: 21.4 us -> 34.2 us
  Pallas kernels: 63.9 us -> 53.6 us
  starting transfers between devices: 64 us -> 54.6 us
  local copies, waits for them, and re-layouts: 26.8 us -> 21.7 us
  matrix products: 8.15 us -> 5.47 us
    ppermute x28, waiting for transfers between devices: 20.2 us -> 32.2 us  [hop(): return lax.ppermute(x, axis, [(i, (i + by) % 4) for i in range(4)])]
    pallas_call x2 -> x1, Pallas kernels: 63.9 us -> 53.6 us  [attention(): pl.pallas_call(functools.partial(attention_kernel, len(srcs), copies), ou...]
    ppermute x8 -> x7, starting transfers between devices: 22.9 us -> 13.6 us  [swap(): return lax.ppermute(x, 'core', [(0, 1), (1, 0)])]
    unnamed x62 -> x45, local copies, waits for them, and re-layouts: 16 us -> 7.39 us
    squeeze x4, local copies, waits for them, and re-layouts: 3.05 us -> 6.73 us  [ring_gather(): k2, v2 = (hop(less[:, 0], second, 1), hop(more[:, 1], second, -1))]
  transfers between devices with their start and end apart: 37 -> 35, of which waited for: 12 -> 15; matrix products, arithmetic and copies ran while one was open for 9% -> 12% of each run, Pallas kernels for 31% -> 30%
where the time goes in v2:
time: 181 us
  starting transfers between devices  54.6 us (30%)
  Pallas kernels  53.6 us (30%)
  waiting for transfers between devices  34.2 us (19%)
  local copies, waits for them, and re-layouts  21.7 us (12%)
  other arithmetic  10 us (6%)
  matrix products  5.47 us (3%)
    pallas_call x1, Pallas kernels, attention(): pl.pallas_call(functools.partial(attention_kernel, len(srcs), copies), ou...  53.6 us
    ppermute x28, starting transfers between devices, hop(): return lax.ppermute(x, axis, [(i, (i + by) % 4) for i in range(4)])  41 us
    ppermute x28, waiting for transfers between devices, hop(): return lax.ppermute(x, axis, [(i, (i + by) % 4) for i in range(4)])  32.2 us
    ppermute x7, starting transfers between devices, swap(): return lax.ppermute(x, 'core', [(0, 1), (1, 0)])  13.6 us
    unnamed x45, local copies, waits for them, and re-layouts  7.39 us
    squeeze x4, local copies, waits for them, and re-layouts, ring_gather(): k2, v2 = (hop(less[:, 0], second, 1), hop(more[:, 1], second, -1))  6.73 us
  transfers between devices with their start and end apart: 35, of which 15 were waited for; matrix products, arithmetic and copies ran while one was open for 12% of the time, Pallas kernels for 30%

profile of v2, /device:TPU:1, one launch (start us, length us, event | category | flops | bytes accessed | tf_op | source)
XLA Modules:
  0.0 180.9 jit_solution(13283254573770081001)
XLA Ops:
  0.7 1.3 copy.36
  1.9 1.1 copy.37
  3.1 1.5 collective-permute-start
  4.7 1.0 collective-permute-done
  6.1 0.9 slice_bitcast_fusion.8
  7.0 1.4 collective-permute-start.5
  8.4 1.4 collective-permute-start.6
  9.8 1.6 collective-permute-start.1
  11.5 2.1 %collective-permute-start.2 = (bf16[2,2,256,128]{3,2,1,0:T(8,128)(2,1)S(1)}, bf16[2,2,256,128]{3,2,1,0:T(8,128)(2,1)S(1)}, u32[]{:S(2)}, u32[]{:S(2)}) collective-permute-start(bf16[2,2,256,128]{3,2,1,0:T(8,128)(2,1)S(1)} %get-tuple-element.31), channel_id=1, source_target_pairs={{0,6},{2,0},{4,2},{6,4},{1,7},{3,1},{5,3},{7,5},{8,14},{10,8},{12,... | collective-permute-start | bytes 786440 | tf_op jit(solution)/shard_map/ppermute | solution.py:182
  13.6 2.4 %collective-permute-done.5 = bf16[2,2,256,128]{3,2,1,0:T(8,128)(2,1)S(1)} collective-permute-done((bf16[2,2,256,128]{3,2,1,0:T(8,128)(2,1)S(1)}, bf16[2,2,256,128]{3,2,1,0:T(8,128)(2,1)S(1)}, u32[]{:S(2)}, u32[]{:S(2)}) %collective-permute-start.5) | collective-permute-done | bytes 262176 | tf_op jit(solution)/shard_map/ppermute | solution.py:182
  16.1 2.7 %collective-permute-start.8 = (bf16[2,256,128]{2,1,0:T(8,128)(2,1)S(1)}, bf16[2,256,128]{2,1,0:T(8,128)(2,1)S(1)}, u32[]{:S(2)}, u32[]{:S(2)}) collective-permute-start(bf16[2,256,128]{2,1,0:T(8,128)(2,1)S(1)} %slice_bitcast_fusion.4), channel_id=1, source_target_pairs={{0,24},{8,0},{16,8},{24,16},{1,25},{9,1},{17,9},{25,17},{2,26},{10... | collective-permute-start | bytes 393224 | tf_op jit(solution)/shard_map/ppermute | solution.py:182
  19.4 1.1 collective-permute-start.3
  20.5 2.2 %collective-permute-start.4 = (bf16[2,256,128]{2,1,0:T(8,128)(2,1)S(1)}, bf16[2,256,128]{2,1,0:T(8,128)(2,1)S(1)}, u32[]{:S(2)}, u32[]{:S(2)}) collective-permute-start(bf16[2,256,128]{2,1,0:T(8,128)(2,1)S(1)} %slice_bitcast_fusion.6), channel_id=1, source_target_pairs={{0,6},{2,0},{4,2},{6,4},{1,7},{3,1},{5,3},{7,5},{8,14},{10,8},{12,... | collective-permute-start | bytes 393224 | tf_op jit(solution)/shard_map/ppermute | solution.py:182
  22.8 1.2 pad_maximum_fusion.2
  23.9 2.7 %collective-permute-start.15 = (bf16[4,2,2,256,128]{4,3,2,0,1:T(8,128)(2,1)}, bf16[4,2,2,256,128]{4,3,2,0,1:T(8,128)(2,1)}, u32[]{:S(2)}, u32[]{:S(2)}) collective-permute-start(bf16[4,2,2,256,128]{4,3,2,0,1:T(8,128)(2,1)} %pad_maximum_fusion.2), channel_id=1, source_target_pairs={{0,6},{2,0},{4,2},{6,4},{1,7},{3,1},{5,3},{7,5},{8,14},{10,8},{12,... | collective-permute-start | bytes 3145736 | tf_op jit(solution)/shard_map/ppermute | solution.py:182
  27.6 1.0 copy-done.11
  29.4 0.9 copy-done.14
  30.4 1.1 copy-done.9
  31.5 1.5 pad_maximum_fusion
  33.1 2.6 %collective-permute-start.9 = (bf16[2,128,4096]{2,1,0:T(8,128)(2,1)}, bf16[2,128,4096]{2,1,0:T(8,128)(2,1)}, u32[]{:S(2)}, u32[]{:S(2)}) collective-permute-start(bf16[2,128,4096]{2,1,0:T(8,128)(2,1)} %pad_maximum_fusion), channel_id=1, source_target_pairs={{0,1},{1,0},{2,3},{3,2},{4,5},{5,4},{6,7},{7,6},{8,9},{9,8},{10,11... | collective-permute-start | bytes 6291464 | tf_op jit(solution)/shard_map/ppermute | solution.py:186
  35.7 2.5 %collective-permute-start.11 = (bf16[4,2,2,256,128]{4,3,2,1,0:T(8,128)(2,1)S(1)}, bf16[4,2,2,256,128]{4,3,2,1,0:T(8,128)(2,1)}, u32[]{:S(2)}, u32[]{:S(2)}) collective-permute-start(bf16[4,2,2,256,128]{4,3,2,1,0:T(8,128)(2,1)S(1)} %pad_maximum_fusion.1.rest_0_), channel_id=1, source_target_pairs={{0,24},{8,0},{16,8},{24,16},{1,25},{9,1},{17,9},{25,17},{2,26},{10... | collective-permute-start | bytes 3145736 | tf_op jit(solution)/shard_map/ppermute | solution.py:182
  38.1 0.9 constant_dynamic-slice_fusion
  39.0 9.2 %collective-permute-done.14 = bf16[4,2,2,256,128]{4,3,2,0,1:T(8,128)(2,1)} collective-permute-done((bf16[4,2,2,256,128]{4,3,2,0,1:T(8,128)(2,1)}, bf16[4,2,2,256,128]{4,3,2,0,1:T(8,128)(2,1)}, u32[]{:S(2)}, u32[]{:S(2)}) %collective-permute-start.14) | collective-permute-done | bytes 1048608 | tf_op jit(solution)/shard_map/ppermute | solution.py:182
  48.2 1.9 %slice_bitcast_fusion.1 = bf16[4,2,256,128]{3,2,1,0:T(8,128)(2,1)} fusion(bf16[4,2,2,256,128]{4,3,2,0,1:T(8,128)(2,1)} %collective-permute-done.14), kind=kLoop, calls=%fused_computation.34 | loop fusion | bytes 1048576 | tf_op jit(solution)/shard_map/squeeze | solution.py:194
  50.1 1.9 %slice_bitcast_fusion = bf16[4,2,256,128]{3,2,1,0:T(8,128)(2,1)} fusion(bf16[4,2,2,256,128]{4,3,2,0,1:T(8,128)(2,1)} %collective-permute-done.15), kind=kLoop, calls=%fused_computation.33 | loop fusion | bytes 1048576 | tf_op jit(solution)/shard_map/squeeze | solution.py:194
  52.0 2.7 %collective-permute-start.17 = (bf16[4,2,256,128]{3,2,1,0:T(8,128)(2,1)}, bf16[4,2,256,128]{3,2,1,0:T(8,128)(2,1)}, u32[]{:S(2)}, u32[]{:S(2)}) collective-permute-start(bf16[4,2,256,128]{3,2,1,0:T(8,128)(2,1)} %slice_bitcast_fusion), channel_id=1, source_target_pairs={{0,6},{2,0},{4,2},{6,4},{1,7},{3,1},{5,3},{7,5},{8,14},{10,8},{12,... | collective-permute-start | bytes 1572872 | tf_op jit(solution)/shard_map/ppermute | solution.py:182
  54.6 1.9 %slice_bitcast_fusion.3 = bf16[4,2,256,128]{3,2,1,0:T(8,128)(2,1)} fusion(bf16[4,2,2,256,128]{4,3,2,1,0:T(8,128)(2,1)} %collective-permute-done.10.rest_1_), kind=kLoop, calls=%fused_computation.36 | loop fusion | bytes 1048576 | tf_op jit(solution)/shard_map/squeeze | solution.py:194
  56.5 4.1 %collective-permute-done.11.rest_2_ = bf16[4,2,2,256,128]{4,3,2,1,0:T(8,128)(2,1)} collective-permute-done((bf16[4,2,2,256,128]{4,3,2,1,0:T(8,128)(2,1)S(1)}, bf16[4,2,2,256,128]{4,3,2,1,0:T(8,128)(2,1)}, u32[]{:S(2)}, u32[]{:S(2)}) %collective-permute-start.11) | collective-permute-done | bytes 1048608 | tf_op jit(solution)/shard_map/ppermute | solution.py:182
  60.6 1.1 slice_bitcast_fusion.2
  61.7 3.6 %collective-permute-start.13 = (bf16[4,2,256,128]{3,2,1,0:T(8,128)(2,1)S(1)}, bf16[4,2,256,128]{3,2,1,0:T(8,128)(2,1)S(1)}, u32[]{:S(2)}, u32[]{:S(2)}) collective-permute-start(bf16[4,2,256,128]{3,2,1,0:T(8,128)(2,1)S(1)} %slice_bitcast_fusion.2), channel_id=1, source_target_pairs={{0,24},{8,0},{16,8},{24,16},{1,25},{9,1},{17,9},{25,17},{2,26},{10... | collective-permute-start | bytes 1572872 | tf_op jit(solution)/shard_map/ppermute | solution.py:182
  65.8 1.3 copy.45.rest_5_
  67.1 1.4 copy.46.rest_6_
  68.5 1.3 copy.47.rest_7_
  69.8 1.4 collective-permute-start.19
  71.3 4.5 %collective-permute-done.13.rest_4_ = bf16[4,2,256,128]{3,2,1,0:T(8,128)(2,1)S(1)} collective-permute-done((bf16[4,2,256,128]{3,2,1,0:T(8,128)(2,1)S(1)}, bf16[4,2,256,128]{3,2,1,0:T(8,128)(2,1)S(1)}, u32[]{:S(2)}, u32[]{:S(2)}) %collective-permute-start.13) | collective-permute-done | bytes 524320 | tf_op jit(solution)/shard_map/ppermute | solution.py:182
  75.7 0.8 copy-done.7
  76.5 1.0 copy-done.8
  77.6 53.6 %attend.1 = (bf16[128,4096]{1,0:T(8,128)(2,1)S(1)}, bf16[128,4096]{1,0:T(8,128)(2,1)S(1)}, bf16[128,4096]{1,0:T(8,128)(2,1)S(1)}, bf16[128,4096]{1,0:T(8,128)(2,1)S(1)}) custom-call(s32[768]{0:T(1024)S(1)} %reshape.72.lists, s32[32]{0:T(128)S(1)} %dynamic_slice.40.live, s32[1]{0:T(128)} %bitcast.off, bf16[128,8192]{1,0:T(8,128)(2,1)} %copy-done.9, ...), custom_call_target="tpu_custom_call" | custom-call | flops 8589934592 | bytes 16777216 | tf_op jit(solution)/shard_map/attend/pallas_call | solution.py:155
  131.6 2.7 %collective-permute-start.20 = (f32[128,16]{0,1:T(8,128)S(1)}, f32[128,16]{0,1:T(8,128)S(1)}, u32[]{:S(2)}, u32[]{:S(2)}) collective-permute-start(f32[128,16]{0,1:T(8,128)S(1)} %fusion.21), channel_id=1, source_target_pairs={{0,1},{1,0},{2,3},{3,2},{4,5},{5,4},{6,7},{7,6},{8,9},{9,8},{10,11... | collective-permute-start | bytes 24584 | tf_op jit(solution)/shard_map/ppermute | solution.py:186
  134.3 1.0 fusion.39
  135.2 1.6 fusion.5
  136.8 1.0 dynamic-slice_convert_fusion
  138.1 1.2 fusion.2
  139.3 1.1 convert_add_fusion
  141.0 3.0 %collective-permute-start.23 = (bf16[32,1024]{1,0:T(8,128)(2,1)S(1)}, bf16[32,1024]{1,0:T(8,128)(2,1)}, u32[]{:S(2)}, u32[]{:S(2)}) collective-permute-start(bf16[32,1024]{1,0:T(8,128)(2,1)S(1)} %get-tuple-element.26), channel_id=1, source_target_pairs={{0,4},{2,6},{4,0},{6,2},{1,5},{3,7},{5,1},{7,3},{8,12},{10,14},{12... | collective-permute-start | bytes 196616 | tf_op jit(solution)/shard_map/ppermute | solution.py:182
  144.7 1.0 collective-permute-done.22
  145.7 1.6 collective-permute-done.23
  147.3 0.8 collective-permute-done.24
  148.1 1.0 fusion.16
  149.1 2.1 %collective-permute-start.25 = (bf16[32,1024]{1,0:T(8,128)(2,1)S(1)}, bf16[32,1024]{1,0:T(8,128)(2,1)S(1)}, u32[]{:S(2)}, u32[]{:S(2)}) collective-permute-start(bf16[32,1024]{1,0:T(8,128)(2,1)S(1)} %fusion.16), channel_id=1, source_target_pairs={{0,16},{8,24},{16,0},{24,8},{1,17},{9,25},{17,1},{25,9},{2,18},{10... | collective-permute-start | bytes 196616 | tf_op jit(solution)/shard_map/ppermute | solution.py:182
  151.2 2.1 %collective-permute-start.26 = (bf16[32,1024]{1,0:T(8,128)(2,1)S(1)}, bf16[32,1024]{1,0:T(8,128)(2,1)S(1)}, u32[]{:S(2)}, u32[]{:S(2)}) collective-permute-start(bf16[32,1024]{1,0:T(8,128)(2,1)S(1)} %fusion.16), channel_id=1, source_target_pairs={{0,8},{8,16},{16,24},{24,0},{1,9},{9,17},{17,25},{25,1},{2,10},{10... | collective-permute-start | bytes 196616 | tf_op jit(solution)/shard_map/ppermute | solution.py:182
  153.9 2.3 %collective-permute-done.26 = bf16[32,1024]{1,0:T(8,128)(2,1)S(1)} collective-permute-done((bf16[32,1024]{1,0:T(8,128)(2,1)S(1)}, bf16[32,1024]{1,0:T(8,128)(2,1)S(1)}, u32[]{:S(2)}, u32[]{:S(2)}) %collective-permute-start.26) | collective-permute-done | bytes 65568 | tf_op jit(solution)/shard_map/ppermute | solution.py:182
  156.1 1.1 collective-permute-done.27
  157.3 2.8 %collective-permute-start.28 = (bf16[32,1024]{1,0:T(8,128)(2,1)S(1)}, bf16[32,1024]{1,0:T(8,128)(2,1)S(1)}, u32[]{:S(2)}, u32[]{:S(2)}) collective-permute-start(bf16[32,1024]{1,0:T(8,128)(2,1)S(1)} %add_convert_fusion.1), channel_id=1, source_target_pairs={{0,64},{32,96},{64,0},{96,32},{1,65},{33,97},{65,1},{97,33},{2,66}... | collective-permute-start | bytes 196616 | tf_op jit(solution)/shard_map/ppermute | solution.py:182
  160.5 2.4 %collective-permute-start.30 = (bf16[32,1024]{1,0:T(8,128)(2,1)S(1)}, bf16[32,1024]{1,0:T(8,128)(2,1)S(1)}, u32[]{:S(2)}, u32[]{:S(2)}) collective-permute-start(bf16[32,1024]{1,0:T(8,128)(2,1)S(1)} %add_convert_fusion.1), channel_id=1, source_target_pairs={{0,96},{32,0},{64,32},{96,64},{1,97},{33,1},{65,33},{97,65},{2,98}... | collective-permute-start | bytes 196616 | tf_op jit(solution)/shard_map/ppermute | solution.py:182
  162.8 2.3 %collective-permute-done.29 = bf16[32,1024]{1,0:T(8,128)(2,1)S(1)} collective-permute-done((bf16[32,1024]{1,0:T(8,128)(2,1)S(1)}, bf16[32,1024]{1,0:T(8,128)(2,1)S(1)}, u32[]{:S(2)}, u32[]{:S(2)}) %collective-permute-start.29) | collective-permute-done | bytes 65568 | tf_op jit(solution)/shard_map/ppermute | solution.py:182
  165.3 1.2 collective-permute-start.32
  166.5 1.5 collective-permute-start.33
  168.1 2.0 %collective-permute-done.31 = bf16[32,1024]{1,0:T(8,128)(2,1)S(1)} collective-permute-done((bf16[32,1024]{1,0:T(8,128)(2,1)S(1)}, bf16[32,1024]{1,0:T(8,128)(2,1)S(1)}, u32[]{:S(2)}, u32[]{:S(2)}) %collective-permute-start.31) | collective-permute-done | bytes 65568 | tf_op jit(solution)/shard_map/ppermute | solution.py:182
  170.7 5.2 %collective-permute-start.34 = (bf16[32,4096]{1,0:T(8,128)(2,1)S(1)}, bf16[32,4096]{1,0:T(8,128)(2,1)S(1)}, u32[]{:S(2)}, u32[]{:S(2)}) collective-permute-start(bf16[32,4096]{1,0:T(8,128)(2,1)S(1)} %pad_maximum_fusion.3), channel_id=1, source_target_pairs={{0,1},{1,0},{2,3},{3,2},{4,5},{5,4},{6,7},{7,6},{8,9},{9,8},{10,11... | collective-permute-start | bytes 786440 | tf_op jit(solution)/shard_map/ppermute | solution.py:186
  175.9 1.1 collective-permute-done.34
  177.2 0.8 fusion.6
  178.1 0.8 fusion.8
  178.9 1.9 %maximum_select_fusion = bf16[1,128,8192]{2,1,0:T(8,128)(2,1)} fusion(bf16[1,128,4096]{2,1,0:T(8,128)(2,1)S(1)} %bitcast.71, bf16[1,128,4096]{2,1,0:T(8,128)(2,1)S(1)} %bitcast.69, pred[]{:T(512)S(6)} %eq.135), kind=kLoop, calls=%fused_computation.6 | loop fusion | flops 9437184 | bytes 4194305 | tf_op jit(solution)/shard_map/jit(_where)/select_n | solution.py:284
  (103 shorter events, 7.6 us)
Async XLA Ops:
  0.6 26.3 %copy-start = (bf16[1,128,8192]{2,1,0:T(8,128)(2,1)S(1)}, bf16[1,128,8192]{2,1,0:T(8,128)(2,1)}, u32[]{:S(2)}) copy-start(bf16[1,128,8192]{2,1,0:T(8,128)(2,1)} %param.12) | copy-start | bytes 6291460
  3.1 2.6 %collective-permute-start = (bf16[2,128,512]{1,2,0:T(8,128)(2,1)S(1)}, bf16[2,128,512]{1,2,0:T(8,128)(2,1)S(1)}, u32[]{:S(2)}, u32[]{:S(2)}) collective-permute-start(bf16[2,128,512]{1,2,0:T(8,128)(2,1)S(1)} %get-tuple-element.33), channel_id=1, source_target_pairs={{0,1},{1,0},{2,3},{3,2},{4,5},{5,4},{6,7},{7,6},{8,9},{9,8},{10,11... | collective-permute-start | bytes 786440 | tf_op jit(solution)/shard_map/ppermute | solution.py:186
  7.0 9.0 %collective-permute-start.5 = (bf16[2,2,256,128]{3,2,1,0:T(8,128)(2,1)S(1)}, bf16[2,2,256,128]{3,2,1,0:T(8,128)(2,1)S(1)}, u32[]{:S(2)}, u32[]{:S(2)}) collective-permute-start(bf16[2,2,256,128]{3,2,1,0:T(8,128)(2,1)S(1)} %get-tuple-element.30), channel_id=1, source_target_pairs={{0,8},{8,16},{16,24},{24,0},{1,9},{9,17},{17,25},{25,1},{2,10},{10... | collective-permute-start | bytes 786440 | tf_op jit(solution)/shard_map/ppermute | solution.py:182
  8.4 7.7 %collective-permute-start.6 = (bf16[2,2,256,128]{3,2,1,0:T(8,128)(2,1)S(1)}, bf16[2,2,256,128]{3,2,1,0:T(8,128)(2,1)S(1)}, u32[]{:S(2)}, u32[]{:S(2)}) collective-permute-start(bf16[2,2,256,128]{3,2,1,0:T(8,128)(2,1)S(1)} %get-tuple-element.30), channel_id=1, source_target_pairs={{0,24},{8,0},{16,8},{24,16},{1,25},{9,1},{17,9},{25,17},{2,26},{10... | collective-permute-start | bytes 786440 | tf_op jit(solution)/shard_map/ppermute | solution.py:182
  9.8 16.8 %copy-start.13 = (bf16[1,2,2,256,128]{4,3,2,1,0:T(8,128)(2,1)S(1)}, bf16[1,2,2,256,128]{4,3,2,1,0:T(8,128)(2,1)}, u32[]{:S(2)}) copy-start(bf16[1,2,2,256,128]{4,3,2,1,0:T(8,128)(2,1)} %get-tuple-element.29) | copy-start | bytes 786436
  9.8 9.6 %collective-permute-start.1 = (bf16[2,2,256,128]{3,2,1,0:T(8,128)(2,1)S(1)}, bf16[2,2,256,128]{3,2,1,0:T(8,128)(2,1)S(1)}, u32[]{:S(2)}, u32[]{:S(2)}) collective-permute-start(bf16[2,2,256,128]{3,2,1,0:T(8,128)(2,1)S(1)} %get-tuple-element.31), channel_id=1, source_target_pairs={{0,2},{2,4},{4,6},{6,0},{1,3},{3,5},{5,7},{7,1},{8,10},{10,12},{12... | collective-permute-start | bytes 786440 | tf_op jit(solution)/shard_map/ppermute | solution.py:182
  11.5 9.0 %collective-permute-start.2 = (bf16[2,2,256,128]{3,2,1,0:T(8,128)(2,1)S(1)}, bf16[2,2,256,128]{3,2,1,0:T(8,128)(2,1)S(1)}, u32[]{:S(2)}, u32[]{:S(2)}) collective-permute-start(bf16[2,2,256,128]{3,2,1,0:T(8,128)(2,1)S(1)} %get-tuple-element.31), channel_id=1, source_target_pairs={{0,6},{2,0},{4,2},{6,4},{1,7},{3,1},{5,3},{7,5},{8,14},{10,8},{12,... | collective-permute-start | bytes 786440 | tf_op jit(solution)/shard_map/ppermute | solution.py:182
  16.0 6.7 %collective-permute-start.7 = (bf16[2,256,128]{2,1,0:T(8,128)(2,1)S(1)}, bf16[2,256,128]{2,1,0:T(8,128)(2,1)S(1)}, u32[]{:S(2)}, u32[]{:S(2)}) collective-permute-start(bf16[2,256,128]{2,1,0:T(8,128)(2,1)S(1)} %slice_bitcast_fusion.5), channel_id=1, source_target_pairs={{0,8},{8,16},{16,24},{24,0},{1,9},{9,17},{17,25},{25,1},{2,10},{10... | collective-permute-start | bytes 393224 | tf_op jit(solution)/shard_map/ppermute | solution.py:182
  16.1 6.6 %collective-permute-start.8 = (bf16[2,256,128]{2,1,0:T(8,128)(2,1)S(1)}, bf16[2,256,128]{2,1,0:T(8,128)(2,1)S(1)}, u32[]{:S(2)}, u32[]{:S(2)}) collective-permute-start(bf16[2,256,128]{2,1,0:T(8,128)(2,1)S(1)} %slice_bitcast_fusion.4), channel_id=1, source_target_pairs={{0,24},{8,0},{16,8},{24,16},{1,25},{9,1},{17,9},{25,17},{2,26},{10... | collective-permute-start | bytes 393224 | tf_op jit(solution)/shard_map/ppermute | solution.py:182
  19.4 7.2 %collective-permute-start.3 = (bf16[2,256,128]{2,1,0:T(8,128)(2,1)S(1)}, bf16[2,256,128]{2,1,0:T(8,128)(2,1)S(1)}, u32[]{:S(2)}, u32[]{:S(2)}) collective-permute-start(bf16[2,256,128]{2,1,0:T(8,128)(2,1)S(1)} %slice_bitcast_fusion.7), channel_id=1, source_target_pairs={{0,2},{2,4},{4,6},{6,0},{1,3},{3,5},{5,7},{7,1},{8,10},{10,12},{12... | collective-permute-start | bytes 393224 | tf_op jit(solution)/shard_map/ppermute | solution.py:182
  20.5 6.1 %collective-permute-start.4 = (bf16[2,256,128]{2,1,0:T(8,128)(2,1)S(1)}, bf16[2,256,128]{2,1,0:T(8,128)(2,1)S(1)}, u32[]{:S(2)}, u32[]{:S(2)}) collective-permute-start(bf16[2,256,128]{2,1,0:T(8,128)(2,1)S(1)} %slice_bitcast_fusion.6), channel_id=1, source_target_pairs={{0,6},{2,0},{4,2},{6,4},{1,7},{3,1},{5,3},{7,5},{8,14},{10,8},{12,... | collective-permute-start | bytes 393224 | tf_op jit(solution)/shard_map/ppermute | solution.py:182
  22.7 4.2 %copy-start.17 = (bf16[8192,16]{0,1:T(8,128)(2,1)S(1)}, bf16[8192,16]{0,1:T(8,128)(2,1)}, u32[]{:S(2)}) copy-start(bf16[8192,16]{0,1:T(8,128)(2,1)} %param.17) | copy-start | bytes 786436
  23.9 24.2 %collective-permute-start.14 = (bf16[4,2,2,256,128]{4,3,2,0,1:T(8,128)(2,1)}, bf16[4,2,2,256,128]{4,3,2,0,1:T(8,128)(2,1)}, u32[]{:S(2)}, u32[]{:S(2)}) collective-permute-start(bf16[4,2,2,256,128]{4,3,2,0,1:T(8,128)(2,1)} %pad_maximum_fusion.2), channel_id=1, source_target_pairs={{0,2},{2,4},{4,6},{6,0},{1,3},{3,5},{5,7},{7,1},{8,10},{10,12},{12... | collective-permute-start | bytes 3145736 | tf_op jit(solution)/shard_map/ppermute | solution.py:182
  23.9 26.1 %collective-permute-start.15 = (bf16[4,2,2,256,128]{4,3,2,0,1:T(8,128)(2,1)}, bf16[4,2,2,256,128]{4,3,2,0,1:T(8,128)(2,1)}, u32[]{:S(2)}, u32[]{:S(2)}) collective-permute-start(bf16[4,2,2,256,128]{4,3,2,0,1:T(8,128)(2,1)} %pad_maximum_fusion.2), channel_id=1, source_target_pairs={{0,6},{2,0},{4,2},{6,4},{1,7},{3,1},{5,3},{7,5},{8,14},{10,8},{12,... | collective-permute-start | bytes 3145736 | tf_op jit(solution)/shard_map/ppermute | solution.py:182
  26.7 2.0 %copy-start.11 = (bf16[1,128,8192]{2,1,0:T(8,128)(2,1)S(1)}, bf16[1,128,8192]{2,1,0:T(8,128)(2,1)}, u32[]{:S(2)}) copy-start(bf16[1,128,8192]{2,1,0:T(8,128)(2,1)} %param.13) | copy-start | bytes 6291460
  26.7 2.0 %copy-start.12 = (bf16[16,8192]{1,0:T(8,128)(2,1)S(1)}, bf16[16,8192]{1,0:T(8,128)(2,1)}, u32[]{:S(2)}) copy-start(bf16[16,8192]{1,0:T(8,128)(2,1)} %param.18) | copy-start | bytes 786436
  26.8 8.8 %copy-start.3 = (bf16[4,2,2,256,128]{4,3,2,1,0:T(8,128)(2,1)}, bf16[4,2,2,256,128]{4,3,2,1,0:T(8,128)(2,1)S(1)}, u32[]{:S(2)}) copy-start(bf16[4,2,2,256,128]{4,3,2,1,0:T(8,128)(2,1)S(1)} %pad_maximum_fusion.1.rest_0_) | copy-start | bytes 3145732
  26.8 27.8 %collective-permute-start.10 = (bf16[4,2,2,256,128]{4,3,2,1,0:T(8,128)(2,1)S(1)}, bf16[4,2,2,256,128]{4,3,2,1,0:T(8,128)(2,1)}, u32[]{:S(2)}, u32[]{:S(2)}) collective-permute-start(bf16[4,2,2,256,128]{4,3,2,1,0:T(8,128)(2,1)S(1)} %pad_maximum_fusion.1.rest_0_), channel_id=1, source_target_pairs={{0,8},{8,16},{16,24},{24,0},{1,9},{9,17},{17,25},{25,1},{2,10},{10... | collective-permute-start | bytes 3145736 | tf_op jit(solution)/shard_map/ppermute | solution.py:182
  28.6 1.6 copy-start.14
  30.2 1.3 copy-start.9
  33.1 43.4 %collective-permute-start.9 = (bf16[2,128,4096]{2,1,0:T(8,128)(2,1)}, bf16[2,128,4096]{2,1,0:T(8,128)(2,1)}, u32[]{:S(2)}, u32[]{:S(2)}) collective-permute-start(bf16[2,128,4096]{2,1,0:T(8,128)(2,1)} %pad_maximum_fusion), channel_id=1, source_target_pairs={{0,1},{1,0},{2,3},{3,2},{4,5},{5,4},{6,7},{7,6},{8,9},{9,8},{10,11... | collective-permute-start | bytes 6291464 | tf_op jit(solution)/shard_map/ppermute | solution.py:186
  35.7 25.0 %collective-permute-start.11 = (bf16[4,2,2,256,128]{4,3,2,1,0:T(8,128)(2,1)S(1)}, bf16[4,2,2,256,128]{4,3,2,1,0:T(8,128)(2,1)}, u32[]{:S(2)}, u32[]{:S(2)}) collective-permute-start(bf16[4,2,2,256,128]{4,3,2,1,0:T(8,128)(2,1)S(1)} %pad_maximum_fusion.1.rest_0_), channel_id=1, source_target_pairs={{0,24},{8,0},{16,8},{24,16},{1,25},{9,1},{17,9},{25,17},{2,26},{10... | collective-permute-start | bytes 3145736 | tf_op jit(solution)/shard_map/ppermute | solution.py:182
  39.0 26.7 %copy-start.18 = (s32[64]{0:T(128)S(1)}, s32[64]{0:T(128)}, u32[]{:S(2)}) copy-start(s32[64]{0:T(128)} %param.22) | copy-start | bytes 772
  50.0 19.8 %collective-permute-start.16 = (bf16[4,2,256,128]{3,2,1,0:T(8,128)(2,1)}, bf16[4,2,256,128]{3,2,1,0:T(8,128)(2,1)}, u32[]{:S(2)}, u32[]{:S(2)}) collective-permute-start(bf16[4,2,256,128]{3,2,1,0:T(8,128)(2,1)} %slice_bitcast_fusion.1), channel_id=1, source_target_pairs={{0,2},{2,4},{4,6},{6,0},{1,3},{3,5},{5,7},{7,1},{8,10},{10,12},{12... | collective-permute-start | bytes 1572872 | tf_op jit(solution)/shard_map/ppermute | solution.py:182
  52.0 19.3 %collective-permute-start.17 = (bf16[4,2,256,128]{3,2,1,0:T(8,128)(2,1)}, bf16[4,2,256,128]{3,2,1,0:T(8,128)(2,1)}, u32[]{:S(2)}, u32[]{:S(2)}) collective-permute-start(bf16[4,2,256,128]{3,2,1,0:T(8,128)(2,1)} %slice_bitcast_fusion), channel_id=1, source_target_pairs={{0,6},{2,0},{4,2},{6,4},{1,7},{3,1},{5,3},{7,5},{8,14},{10,8},{12,... | collective-permute-start | bytes 1572872 | tf_op jit(solution)/shard_map/ppermute | solution.py:182
  56.5 14.7 %collective-permute-start.12 = (bf16[4,2,256,128]{3,2,1,0:T(8,128)(2,1)}, bf16[4,2,256,128]{3,2,1,0:T(8,128)(2,1)}, u32[]{:S(2)}, u32[]{:S(2)}) collective-permute-start(bf16[4,2,256,128]{3,2,1,0:T(8,128)(2,1)} %slice_bitcast_fusion.3), channel_id=1, source_target_pairs={{0,8},{8,16},{16,24},{24,0},{1,9},{9,17},{17,25},{25,1},{2,10},{10... | collective-permute-start | bytes 1572872 | tf_op jit(solution)/shard_map/ppermute | solution.py:182
  61.7 14.0 %collective-permute-start.13 = (bf16[4,2,256,128]{3,2,1,0:T(8,128)(2,1)S(1)}, bf16[4,2,256,128]{3,2,1,0:T(8,128)(2,1)S(1)}, u32[]{:S(2)}, u32[]{:S(2)}) collective-permute-start(bf16[4,2,256,128]{3,2,1,0:T(8,128)(2,1)S(1)} %slice_bitcast_fusion.2), channel_id=1, source_target_pairs={{0,24},{8,0},{16,8},{24,16},{1,25},{9,1},{17,9},{25,17},{2,26},{10... | collective-permute-start | bytes 1572872 | tf_op jit(solution)/shard_map/ppermute | solution.py:182
  67.1 9.4 %copy-start.4 = (bf16[4,2,2,256,128]{4,3,2,1,0:T(8,128)(2,1)S(1)}, bf16[4,2,2,256,128]{4,3,2,1,0:T(8,128)(2,1)}, u32[]{:S(2)}) copy-start(bf16[4,2,2,256,128]{4,3,2,1,0:T(8,128)(2,1)} %copy-done.3) | copy-start | bytes 3145732
  69.8 64.4 %collective-permute-start.19 = (bf16[128,16]{0,1:T(8,128)(2,1)S(1)}, bf16[128,16]{0,1:T(8,128)(2,1)S(1)}, u32[]{:S(2)}, u32[]{:S(2)}) collective-permute-start(bf16[128,16]{0,1:T(8,128)(2,1)S(1)} %convolution_convert_fusion), channel_id=1, source_target_pairs={{0,1},{1,0},{2,3},{3,2},{4,5},{5,4},{6,7},{7,6},{8,9},{9,8},{10,11... | collective-permute-start | bytes 12296 | tf_op jit(solution)/shard_map/ppermute | solution.py:186
  75.7 0.8 copy-start.7
  76.5 1.0 copy-start.8
  131.2 4.0 %copy-start.1 = (bf16[128,4096]{1,0:T(8,128)(2,1)}, bf16[128,4096]{1,0:T(8,128)(2,1)S(1)}, u32[]{:S(2)}) copy-start(bf16[128,4096]{1,0:T(8,128)(2,1)S(1)} %get-tuple-element.13) | copy-start | bytes 3145732
  131.2 4.0 %copy-start.5 = (bf16[128,4096]{1,0:T(8,128)(2,1)}, bf16[128,4096]{1,0:T(8,128)(2,1)S(1)}, u32[]{:S(2)}) copy-start(bf16[128,4096]{1,0:T(8,128)(2,1)S(1)} %get-tuple-element.14) | copy-start | bytes 3145732
  131.6 3.6 %collective-permute-start.20 = (f32[128,16]{0,1:T(8,128)S(1)}, f32[128,16]{0,1:T(8,128)S(1)}, u32[]{:S(2)}, u32[]{:S(2)}) collective-permute-start(f32[128,16]{0,1:T(8,128)S(1)} %fusion.21), channel_id=1, source_target_pairs={{0,1},{1,0},{2,3},{3,2},{4,5},{5,4},{6,7},{7,6},{8,9},{9,8},{10,11... | collective-permute-start | bytes 24584 | tf_op jit(solution)/shard_map/ppermute | solution.py:186
  137.8 1.5 collective-permute-start.21
  139.3 1.1 copy-start.10
  141.0 34.8 %copy-start.6 = (bf16[128,4096]{1,0:T(8,128)(2,1)S(1)}, bf16[128,4096]{1,0:T(8,128)(2,1)}, u32[]{:S(2)}) copy-start(bf16[128,4096]{1,0:T(8,128)(2,1)} %copy-done.5) | copy-start | bytes 3145732
  141.0 4.6 %collective-permute-start.22 = (bf16[32,1024]{1,0:T(8,128)(2,1)}, bf16[32,1024]{1,0:T(8,128)(2,1)}, u32[]{:S(2)}, u32[]{:S(2)}) collective-permute-start(bf16[32,1024]{1,0:T(8,128)(2,1)} %get-tuple-element.25), channel_id=1, source_target_pairs={{0,2},{2,4},{4,6},{6,0},{1,3},{3,5},{5,7},{7,1},{8,10},{10,12},{12... | collective-permute-start | bytes 196616 | tf_op jit(solution)/shard_map/ppermute | solution.py:182
  141.0 6.3 %collective-permute-start.23 = (bf16[32,1024]{1,0:T(8,128)(2,1)S(1)}, bf16[32,1024]{1,0:T(8,128)(2,1)}, u32[]{:S(2)}, u32[]{:S(2)}) collective-permute-start(bf16[32,1024]{1,0:T(8,128)(2,1)S(1)} %get-tuple-element.26), channel_id=1, source_target_pairs={{0,4},{2,6},{4,0},{6,2},{1,5},{3,7},{5,1},{7,3},{8,12},{10,14},{12... | collective-permute-start | bytes 196616 | tf_op jit(solution)/shard_map/ppermute | solution.py:182
  144.0 4.1 %collective-permute-start.24 = (bf16[32,1024]{1,0:T(8,128)(2,1)S(1)}, bf16[32,1024]{1,0:T(8,128)(2,1)}, u32[]{:S(2)}, u32[]{:S(2)}) collective-permute-start(bf16[32,1024]{1,0:T(8,128)(2,1)S(1)} %get-tuple-element.27), channel_id=1, source_target_pairs={{0,6},{2,0},{4,2},{6,4},{1,7},{3,1},{5,3},{7,5},{8,14},{10,8},{12,... | collective-permute-start | bytes 196616 | tf_op jit(solution)/shard_map/ppermute | solution.py:182
  149.1 4.8 %collective-permute-start.25 = (bf16[32,1024]{1,0:T(8,128)(2,1)S(1)}, bf16[32,1024]{1,0:T(8,128)(2,1)S(1)}, u32[]{:S(2)}, u32[]{:S(2)}) collective-permute-start(bf16[32,1024]{1,0:T(8,128)(2,1)S(1)} %fusion.16), channel_id=1, source_target_pairs={{0,16},{8,24},{16,0},{24,8},{1,17},{9,25},{17,1},{25,9},{2,18},{10... | collective-permute-start | bytes 196616 | tf_op jit(solution)/shard_map/ppermute | solution.py:182
  151.2 4.9 %collective-permute-start.26 = (bf16[32,1024]{1,0:T(8,128)(2,1)S(1)}, bf16[32,1024]{1,0:T(8,128)(2,1)S(1)}, u32[]{:S(2)}, u32[]{:S(2)}) collective-permute-start(bf16[32,1024]{1,0:T(8,128)(2,1)S(1)} %fusion.16), channel_id=1, source_target_pairs={{0,8},{8,16},{16,24},{24,0},{1,9},{9,17},{17,25},{25,1},{2,10},{10... | collective-permute-start | bytes 196616 | tf_op jit(solution)/shard_map/ppermute | solution.py:182
  153.3 3.9 %collective-permute-start.27 = (bf16[32,1024]{1,0:T(8,128)(2,1)S(1)}, bf16[32,1024]{1,0:T(8,128)(2,1)S(1)}, u32[]{:S(2)}, u32[]{:S(2)}) collective-permute-start(bf16[32,1024]{1,0:T(8,128)(2,1)S(1)} %fusion.16), channel_id=1, source_target_pairs={{0,24},{8,0},{16,8},{24,16},{1,25},{9,1},{17,9},{25,17},{2,26},{10... | collective-permute-start | bytes 196616 | tf_op jit(solution)/shard_map/ppermute | solution.py:182
  157.3 5.5 %collective-permute-start.28 = (bf16[32,1024]{1,0:T(8,128)(2,1)S(1)}, bf16[32,1024]{1,0:T(8,128)(2,1)S(1)}, u32[]{:S(2)}, u32[]{:S(2)}) collective-permute-start(bf16[32,1024]{1,0:T(8,128)(2,1)S(1)} %add_convert_fusion.1), channel_id=1, source_target_pairs={{0,64},{32,96},{64,0},{96,32},{1,65},{33,97},{65,1},{97,33},{2,66}... | collective-permute-start | bytes 196616 | tf_op jit(solution)/shard_map/ppermute | solution.py:182
  160.1 5.0 %collective-permute-start.29 = (bf16[32,1024]{1,0:T(8,128)(2,1)S(1)}, bf16[32,1024]{1,0:T(8,128)(2,1)S(1)}, u32[]{:S(2)}, u32[]{:S(2)}) collective-permute-start(bf16[32,1024]{1,0:T(8,128)(2,1)S(1)} %add_convert_fusion.1), channel_id=1, source_target_pairs={{0,32},{32,64},{64,96},{96,0},{1,33},{33,65},{65,97},{97,1},{2,34}... | collective-permute-start | bytes 196616 | tf_op jit(solution)/shard_map/ppermute | solution.py:182
  160.5 4.7 %collective-permute-start.30 = (bf16[32,1024]{1,0:T(8,128)(2,1)S(1)}, bf16[32,1024]{1,0:T(8,128)(2,1)S(1)}, u32[]{:S(2)}, u32[]{:S(2)}) collective-permute-start(bf16[32,1024]{1,0:T(8,128)(2,1)S(1)} %add_convert_fusion.1), channel_id=1, source_target_pairs={{0,96},{32,0},{64,32},{96,64},{1,97},{33,1},{65,33},{97,65},{2,98}... | collective-permute-start | bytes 196616 | tf_op jit(solution)/shard_map/ppermute | solution.py:182
  165.2 4.8 %collective-permute-start.31 = (bf16[32,1024]{1,0:T(8,128)(2,1)S(1)}, bf16[32,1024]{1,0:T(8,128)(2,1)S(1)}, u32[]{:S(2)}, u32[]{:S(2)}) collective-permute-start(bf16[32,1024]{1,0:T(8,128)(2,1)S(1)} %add_convert_fusion), channel_id=1, source_target_pairs={{0,4},{2,6},{4,0},{6,2},{1,5},{3,7},{5,1},{7,3},{8,12},{10,14},{12... | collective-permute-start | bytes 196616 | tf_op jit(solution)/shard_map/ppermute | solution.py:182
  165.3 5.1 %collective-permute-start.32 = (bf16[32,1024]{1,0:T(8,128)(2,1)S(1)}, bf16[32,1024]{1,0:T(8,128)(2,1)S(1)}, u32[]{:S(2)}, u32[]{:S(2)}) collective-permute-start(bf16[32,1024]{1,0:T(8,128)(2,1)S(1)} %add_convert_fusion), channel_id=1, source_target_pairs={{0,2},{2,4},{4,6},{6,0},{1,3},{3,5},{5,7},{7,1},{8,10},{10,12},{12... | collective-permute-start | bytes 196616 | tf_op jit(solution)/shard_map/ppermute | solution.py:182
  166.5 3.9 %collective-permute-start.33 = (bf16[32,1024]{1,0:T(8,128)(2,1)S(1)}, bf16[32,1024]{1,0:T(8,128)(2,1)S(1)}, u32[]{:S(2)}, u32[]{:S(2)}) collective-permute-start(bf16[32,1024]{1,0:T(8,128)(2,1)S(1)} %add_convert_fusion), channel_id=1, source_target_pairs={{0,6},{2,0},{4,2},{6,4},{1,7},{3,1},{5,3},{7,5},{8,14},{10,8},{12,... | collective-permute-start | bytes 196616 | tf_op jit(solution)/shard_map/ppermute | solution.py:182
  170.6 6.6 %copy-start.15 = (f32[16,8192]{1,0:T(8,128)S(1)}, f32[16,8192]{1,0:T(8,128)}, u32[]{:S(2)}) copy-start(f32[16,8192]{1,0:T(8,128)} %param.20) | copy-start | bytes 1572868
  170.7 6.3 %collective-permute-start.34 = (bf16[32,4096]{1,0:T(8,128)(2,1)S(1)}, bf16[32,4096]{1,0:T(8,128)(2,1)S(1)}, u32[]{:S(2)}, u32[]{:S(2)}) collective-permute-start(bf16[32,4096]{1,0:T(8,128)(2,1)S(1)} %pad_maximum_fusion.3), channel_id=1, source_target_pairs={{0,1},{1,0},{2,3},{3,2},{4,5},{5,4},{6,7},{7,6},{8,9},{9,8},{10,11... | collective-permute-start | bytes 786440 | tf_op jit(solution)/shard_map/ppermute | solution.py:186
  175.8 3.1 %collective-permute-start.18 = (bf16[128,4096]{1,0:T(8,128)(2,1)S(1)}, bf16[128,4096]{1,0:T(8,128)(2,1)S(1)}, u32[]{:S(2)}, u32[]{:S(2)}) collective-permute-start(bf16[128,4096]{1,0:T(8,128)(2,1)S(1)} %copy-done.6), channel_id=1, source_target_pairs={{0,1},{1,0},{2,3},{3,2},{4,5},{5,4},{6,7},{7,6},{8,9},{9,8},{10,11... | collective-permute-start | bytes 3145736 | tf_op jit(solution)/shard_map/ppermute | solution.py:186
  177.0 1.0 copy-start.16
  177.2 1.7 copy-start.2

commit v3 on v2

--- a/solution.py
+++ b/solution.py
@@ -5,6 +5,7 @@
 import jax.numpy as jnp
 from jax import lax
 from jax.experimental import pallas as pl
+from jax.experimental.layout import Layout, with_layout_constraint
 from jax.experimental.pallas import tpu as pltpu
 from jax.sharding import Mesh, PartitionSpec as P
 
@@ -20,7 +21,7 @@
 TN = (((0,), (0,)), ((), ()))
 
 
-def attend(quads, lists, bases, g, kv, kvt, w_ref, s_ref, queries, cots):
+def attend(quads, zero, lists, bases, g, kv, kvt, w_ref, s_ref, queries, cots):
     def rows(i, part=0, parts=1):
         return pl.ds((512 * i) + part * (512 // parts), 512 // parts)
 
@@ -28,9 +29,9 @@
         return op(x.reshape(x.shape[0] // 8, 8, D), axis=0)
 
     def scores(t, out):
-        w_ref[t, 0:D, 0:D] = queries[t]
-        w_ref[t, D : 2 * D, D : 2 * D] = cots[t]
-        w = w_ref[t]
+        w_ref[t][0:D, 0:D] = queries[t]
+        w_ref[t][D : 2 * D, D : 2 * D] = cots[t]
+        w = w_ref[t][...]
         top = jnp.full((8, D), -jnp.inf, F32)
         for i in range(quads):
             tiles = []
@@ -40,21 +41,25 @@
             both = lax.dot_general(
                 jnp.concatenate(tiles, axis=0), w, NT, preferred_element_type=F32
             )
-            s_ref[t, rows(i), :] = both
+            s_ref[t][rows(i), :] = both
             top = jnp.maximum(top, fold(both[:, :D], jnp.max))
             yield
         out.append(jnp.max(top, axis=0, keepdims=True))
+
+    def later(i, part=0, parts=1):
+        start = 512 * i + part * (512 // parts)
+        return pl.ds(pl.multiple_of(zero + start, 8), 512 // parts)
 
     def weights(t, largest, out):
         total = jnp.zeros((8, D), F32)
         inner = jnp.zeros((8, D), F32)
         for i in range(quads):
             for part in range(4):
-                r = rows(i, part, 4)
-                e = jnp.exp2((s_ref[t, r, 0:D] - largest) * EXP2_SCALE)
-                s_ref[t, r, 0:D] = e
+                r = later(i, part, 4)
+                e = jnp.exp2((s_ref[t][r, 0:D] - largest) * EXP2_SCALE)
+                s_ref[t][r, 0:D] = e
                 total += fold(e, jnp.sum)
-                inner += fold(e * s_ref[t, r, D : 2 * D], jnp.sum)
+                inner += fold(e * s_ref[t][r, D : 2 * D], jnp.sum)
             yield
         inverse = 1.0 / jnp.sum(total, axis=0, keepdims=True)
         out.append((inverse, jnp.sum(inner, axis=0, keepdims=True) * inverse))
@@ -63,8 +68,8 @@
         out = jnp.zeros((D, D), F32)
         grad = jnp.zeros((D, D), F32)
         for i in range(quads):
-            e = s_ref[t, rows(i), 0:D]
-            ds = e * (s_ref[t, rows(i), D : 2 * D] - inner)
+            e = s_ref[t][later(i), 0:D]
+            ds = e * (s_ref[t][later(i), D : 2 * D] - inner)
             x = jnp.concatenate([e.astype(BF16), ds.astype(BF16)], axis=1)
             cols = []
             for j in range(4):
@@ -91,9 +96,9 @@
 
 def attention_kernel(n_src, copies, lists, live, off, q_own, g_own, qg_far, *rest):
     srcs = rest[:n_src]
-    o_own, o_far, d_own, d_far, kv, kvt, w_ref, s_ref, sem = rest[n_src:]
+    o_own, o_far, d_own, d_far, kv, kvt, w0, w1, sc0, sc1, sem = rest[n_src:]
+    w_ref, s_ref = (w0, w1), (sc0, sc1)
     step = pl.program_id(0)
-    del off
 
     def copy(g, i):
         src, view, lo, size, col = copies[g][i]
@@ -106,7 +111,8 @@
         for g in range(4):
             for i in range(len(copies[g])):
                 copy(g, i).start()
-        w_ref[...] = jnp.zeros_like(w_ref)
+        for w in w_ref:
+            w[...] = jnp.zeros_like(w)
 
     for g in range(4):
 
@@ -132,6 +138,7 @@
             bases = (step * 24, step * 24 + 12)
             first, second = attend(
                 quads,
+                off[1],
                 lists,
                 bases,
                 g,
@@ -163,8 +170,10 @@
             scratch_shapes=[
                 pltpu.VMEM((4, 16, 256, 2 * D), BF16),
                 pltpu.VMEM((2 * D, 4096), BF16),
-                pltpu.VMEM((2, 2 * D, 2 * D), BF16),
-                pltpu.VMEM((2, NBMAX * D, 2 * D), F32),
+                pltpu.VMEM((2 * D, 2 * D), BF16),
+                pltpu.VMEM((2 * D, 2 * D), BF16),
+                pltpu.VMEM((NBMAX * D, 2 * D), F32),
+                pltpu.VMEM((NBMAX * D, 2 * D), F32),
                 pltpu.SemaphoreType.DMA((4, n_copies)),
             ],
         ),
@@ -186,23 +195,28 @@
     return lax.ppermute(x, "core", [(0, 1), (1, 0)])
 
 
+def row_major(x):
+    return with_layout_constraint(x, Layout(major_to_minor=tuple(range(x.ndim))))
+
+
 def ring_gather(own, first, second):
     less, more = hop(own, first, 1), hop(own, first, -1)
-    k2, v2 = hop(less[0], first, 1), hop(more[1], first, -1)
-    line = jnp.stack([own, less, more, jnp.stack([k2, v2])])
-    less, more = hop(line, second, 1), hop(line, second, -1)
-    k2, v2 = hop(less[:, 0], second, 1), hop(more[:, 1], second, -1)
-    return [line, less, more, k2, v2]
+    keys2, values2 = hop(less[0], first, 1), hop(more[1], first, -1)
+    keys = row_major(jnp.stack([own[0], less[0], more[0], keys2]))
+    values = row_major(jnp.stack([own[1], less[1], more[1], values2]))
+    keys_less = hop(keys, second, 1)
+    values_more = hop(values, second, -1)
+    keys_more, values_less = hop(keys, second, -1), hop(values, second, 1)
+    keys2, values2 = hop(keys_less, second, 1), hop(values_more, second, -1)
+    return [keys, keys_less, keys_more, keys2, values, values_less, values_more, values2]
 
 
 def ring_copies(first_src, head):
-    pick = []
-    for s in range(3):
-        for k in range(2):
-            pick.append((first_src + s, lambda r, k=k: r.at[:, k, head], 4 * s, 4, k * D))
-    for k in range(2):
-        pick.append((first_src + 3 + k, lambda r: r.at[:, head], 12, 4, k * D))
-    return pick
+    return [
+        (first_src + 4 * k + s, lambda r: r.at[:, head], 4 * s, 4, k * D)
+        for k in range(2)
+        for s in range(4)
+    ]
 
 
 def in_order(own, others, index):
@@ -218,7 +232,7 @@
 
 
 def exchange(x, axis):
-    return [hop(x, axis, d) for d in (1, 2, 3)]
+    return [hop(x, axis, 1), hop(x, axis, 2), hop(x, axis, 3)]
 
 
 def all_sum(x, axis):
@@ -227,7 +241,7 @@
     return sum(p.astype(F32) for p in parts)
 
 
-def body(x, frozen, keys, values, cot, down, up, noise_down, noise_up, lists, live):
+def device(x, frozen, keys, values, cot, down, up, noise_down, noise_up, lists, live):
     x, frozen, keys, values, cot = x[0], frozen[0], keys[0], values[0], cot[0]
     core, y, z = lax.axis_index("core"), lax.axis_index("y"), lax.axis_index("z")
     chip = y * 4 + z
@@ -237,11 +251,13 @@
     mine = lax.dynamic_slice_in_dim(kv, core * 512, 512, 2)
     far = swap(lax.dynamic_slice_in_dim(kv, (1 - core) * 512, 512, 2))
     kv = jnp.where(core == 0, jnp.concatenate([mine, far], 1), jnp.concatenate([far, mine], 1))
-    kv = kv.reshape(2, 256, 4, D).transpose(0, 2, 1, 3)
-    ring_a = ring_gather(kv[:, :2], "z", "y")
-    ring_b = ring_gather(kv[:, 2:], "y", "z")
-
-    x, frozen, cot, _, _ = lax.optimization_barrier((x, frozen, cot, ring_a[0], ring_b[0]))
+    heads = [jnp.stack([kv[:, :, i * D : (i + 1) * D] for i in (j, j + 1)], axis=1) for j in (0, 2)]
+    ring_a = ring_gather(heads[0], "z", "y")
+    ring_b = ring_gather(heads[1], "y", "z")
+
+    x, frozen, cot, *_ = lax.optimization_barrier(
+        (x, frozen, cot, ring_a[0], ring_a[4], ring_b[0], ring_b[4])
+    )
 
     low = jnp.dot(x, down, preferred_element_type=F32).astype(BF16)
     query = (frozen.astype(F32) + GAIN * jnp.dot(low, up, preferred_element_type=F32)).astype(BF16)
@@ -272,12 +288,12 @@
     own_half, far_half, d_own, d_far = attention(
         spot.reshape(-1),
         mylive,
-        jnp.reshape(core * HEADS, (1,)),
+        jnp.stack([core * HEADS, 0 * core]),
         query,
         cot,
         qg_far,
         ring_a + ring_b,
-        [ring_copies(0, 0), ring_copies(0, 1), ring_copies(5, 0), ring_copies(5, 1)],
+        [ring_copies(0, 0), ring_copies(0, 1), ring_copies(8, 0), ring_copies(8, 1)],
     )
 
     far_half = swap(far_half)
@@ -322,7 +338,7 @@
     fine = Mesh(mesh.devices.reshape(4, 4, 4, 2), ("dp", "y", "z", "core"))
     rows = P("dp", ("y", "z", "core"), None)
     return jax.shard_map(
-        body,
+        device,
         mesh=fine,
         in_specs=(rows,) * 5 + (P(),) * 6,
         out_specs=(rows, P(), P()),

time: 181 us -> 207 us (1.14)
  waiting for transfers between devices: 34.2 us -> 58.1 us
  starting transfers between devices: 54.6 us -> 62.2 us
  Pallas kernels: 53.6 us -> 50.7 us
  local copies, waits for them, and re-layouts: 21.7 us -> 19.5 us
    ppermute x28 -> x32, waiting for transfers between devices: 32.2 us -> 55.9 us  [hop(): return lax.ppermute(x, axis, [(i, (i + by) % 4) for i in range(4)])]
    unnamed x45 -> x70, local copies, waits for them, and re-layouts: 7.39 us -> 15.8 us
    ppermute x7, starting transfers between devices: 13.6 us -> 20.5 us  [swap(): return lax.ppermute(x, 'core', [(0, 1), (1, 0)])]
    squeeze x8 -> x0, local copies, waits for them, and re-layouts: 6.77 us -> none  [the longest x4 6.73 us: ring_gather(): k2, v2 = (hop(less[:, 0], second, 1), hop(more[:, 1], second, -1))]
    pallas_call x1, Pallas kernels: 53.6 us -> 50.7 us  [attention(): pl.pallas_call(functools.partial(attention_kernel, len(srcs), copies), ou...]
    ppermute x2 -> x0, local copies, waits for them, and re-layouts: 2.68 us -> none  [hop(): return lax.ppermute(x, axis, [(i, (i + by) % 4) for i in range(4)])]
    ppermute x28 -> x32, starting transfers between devices: 41 us -> 41.6 us  [hop(): return lax.ppermute(x, axis, [(i, (i + by) % 4) for i in range(4)])]
  transfers between devices with their start and end apart: 35 -> 39, of which waited for: 15 -> 18; matrix products, arithmetic and copies ran while one was open for 12% -> 3% of each run, Pallas kernels for 30% -> 25%
where the time goes in v3:
time: 207 us; the launch traced here: 206 us
  starting transfers between devices  62.2 us (30%)
  waiting for transfers between devices  58.1 us (28%)
  Pallas kernels  50.7 us (24%)
  local copies, waits for them, and re-layouts  19.5 us (9%)
  other arithmetic  9.15 us (4%)
  matrix products  5.48 us (3%)
    ppermute x32, waiting for transfers between devices, hop(): return lax.ppermute(x, axis, [(i, (i + by) % 4) for i in range(4)])  55.9 us
    pallas_call x1, Pallas kernels, attention(): pl.pallas_call(functools.partial(attention_kernel, len(srcs), copies), ou...  50.7 us
    ppermute x32, starting transfers between devices, hop(): return lax.ppermute(x, axis, [(i, (i + by) % 4) for i in range(4)])  41.6 us
    ppermute x7, starting transfers between devices, swap(): return lax.ppermute(x, 'core', [(0, 1), (1, 0)])  20.5 us
    unnamed x70, local copies, waits for them, and re-layouts  15.8 us
  transfers between devices with their start and end apart: 39, of which 18 were waited for; matrix products, arithmetic and copies ran while one was open for 3% of the time, Pallas kernels for 25%

profile of v3, /device:TPU:1, one launch (start us, length us, event | category | flops | bytes accessed | tf_op | source)
XLA Modules:
  0.0 206.3 jit_solution(17722015675979856918)
XLA Ops:
  0.7 1.1 constant_dynamic-update-slice_fusion.1
  1.8 1.0 constant_dynamic-update-slice_fusion
  2.8 1.5 collective-permute-start
  4.3 1.2 collective-permute-done
  5.8 2.9 %collective-permute-start.6 = (bf16[2,2,256,128]{3,2,1,0:T(8,128)(2,1)S(1)}, bf16[2,2,256,128]{3,2,1,0:T(8,128)(2,1)S(1)}, u32[]{:S(2)}, u32[]{:S(2)}) collective-permute-start(bf16[2,2,256,128]{3,2,1,0:T(8,128)(2,1)S(1)} %pad_maximum_fusion.5), channel_id=1, source_target_pairs={{0,24},{8,0},{16,8},{24,16},{1,25},{9,1},{17,9},{25,17},{2,26},{10... | collective-permute-start | bytes 786440 | tf_op jit(solution)/shard_map/ppermute | solution.py:191
  8.7 3.8 %collective-permute-start.2 = (bf16[2,2,256,128]{3,2,1,0:T(8,128)(2,1)S(1)}, bf16[2,2,256,128]{3,2,1,0:T(8,128)(2,1)S(1)}, u32[]{:S(2)}, u32[]{:S(2)}) collective-permute-start(bf16[2,2,256,128]{3,2,1,0:T(8,128)(2,1)S(1)} %copy.32), channel_id=1, source_target_pairs={{0,6},{2,0},{4,2},{6,4},{1,7},{3,1},{5,3},{7,5},{8,14},{10,8},{12,... | collective-permute-start | bytes 786440 | tf_op jit(solution)/shard_map/ppermute | solution.py:191
  12.6 1.3 collective-permute-done.6
  14.0 3.5 %collective-permute-start.8 = (bf16[2,256,128]{2,1,0:T(8,128)(2,1)S(1)}, bf16[2,256,128]{2,1,0:T(8,128)(2,1)S(1)}, u32[]{:S(2)}, u32[]{:S(2)}) collective-permute-start(bf16[2,256,128]{2,1,0:T(8,128)(2,1)S(1)} %get-tuple-element.42), channel_id=1, source_target_pairs={{0,24},{8,0},{16,8},{24,16},{1,25},{9,1},{17,9},{25,17},{2,26},{10... | collective-permute-start | bytes 393224 | tf_op jit(solution)/shard_map/ppermute | solution.py:191
  17.7 3.8 %collective-permute-start.4 = (bf16[2,256,128]{2,1,0:T(8,128)(2,1)S(1)}, bf16[2,256,128]{2,1,0:T(8,128)(2,1)S(1)}, u32[]{:S(2)}, u32[]{:S(2)}) collective-permute-start(bf16[2,256,128]{2,1,0:T(8,128)(2,1)S(1)} %get-tuple-element.48), channel_id=1, source_target_pairs={{0,6},{2,0},{4,2},{6,4},{1,7},{3,1},{5,3},{7,5},{8,14},{10,8},{12,... | collective-permute-start | bytes 393224 | tf_op jit(solution)/shard_map/ppermute | solution.py:191
  21.8 1.7 collective-permute-done.4
  23.7 3.0 %collective-permute-done.3 = bf16[2,256,128]{2,1,0:T(8,128)(2,1)S(1)} collective-permute-done((bf16[2,256,128]{2,1,0:T(8,128)(2,1)S(1)}, bf16[2,256,128]{2,1,0:T(8,128)(2,1)S(1)}, u32[]{:S(2)}, u32[]{:S(2)}) %collective-permute-start.3) | collective-permute-done | bytes 131104 | tf_op jit(solution)/shard_map/ppermute | solution.py:191
  28.2 0.8 copy-done.27
  29.3 1.1 copy-done.23
  30.4 1.5 pad_maximum_fusion
  31.9 2.9 %collective-permute-start.9 = (bf16[2,128,4096]{2,1,0:T(8,128)(2,1)}, bf16[2,128,4096]{2,1,0:T(8,128)(2,1)}, u32[]{:S(2)}, u32[]{:S(2)}) collective-permute-start(bf16[2,128,4096]{2,1,0:T(8,128)(2,1)} %pad_maximum_fusion), channel_id=1, source_target_pairs={{0,1},{1,0},{2,3},{3,2},{4,5},{5,4},{6,7},{7,6},{8,9},{9,8},{10,11... | collective-permute-start | bytes 6291464 | tf_op jit(solution)/shard_map/ppermute | solution.py:195
  34.8 1.1 collective-permute-start.20
  36.3 2.7 %collective-permute-start.17 = (bf16[4,2,256,128]{3,2,1,0:T(8,128)(2,1)S(1)}, bf16[4,2,256,128]{3,2,1,0:T(8,128)(2,1)S(1)}, u32[]{:S(2)}, u32[]{:S(2)}) collective-permute-start(bf16[4,2,256,128]{3,2,1,0:T(8,128)(2,1)S(1)} %pad_maximum_fusion.3.rest_8_), channel_id=1, source_target_pairs={{0,6},{2,0},{4,2},{6,4},{1,7},{3,1},{5,3},{7,5},{8,14},{10,8},{12,... | collective-permute-start | bytes 1572872 | tf_op jit(solution)/shard_map/ppermute | solution.py:191
  39.0 9.3 %collective-permute-done.20.rest_14_ = bf16[4,2,256,128]{3,2,1,0:T(8,128)(2,1)S(1)} collective-permute-done((bf16[4,2,256,128]{3,2,1,0:T(8,128)(2,1)S(1)}, bf16[4,2,256,128]{3,2,1,0:T(8,128)(2,1)S(1)}, u32[]{:S(2)}, u32[]{:S(2)}) %collective-permute-start.20) | collective-permute-done | bytes 524320 | tf_op jit(solution)/shard_map/ppermute | solution.py:191
  48.3 2.9 %collective-permute-start.14 = (bf16[4,2,256,128]{3,2,1,0:T(8,128)(2,1)S(1)}, bf16[4,2,256,128]{3,2,1,0:T(8,128)(2,1)}, u32[]{:S(2)}, u32[]{:S(2)}) collective-permute-start(bf16[4,2,256,128]{3,2,1,0:T(8,128)(2,1)S(1)} %copy.37.rest_4_), channel_id=1, source_target_pairs={{0,24},{8,0},{16,8},{24,16},{1,25},{9,1},{17,9},{25,17},{2,26},{10... | collective-permute-start | bytes 1572872 | tf_op jit(solution)/shard_map/ppermute | solution.py:191
  51.3 0.8 copy-done.15
  52.1 9.7 %collective-permute-done.16.rest_9_ = bf16[4,2,256,128]{3,2,1,0:T(8,128)(2,1)S(1)} collective-permute-done((bf16[4,2,256,128]{3,2,1,0:T(8,128)(2,1)S(1)}, bf16[4,2,256,128]{3,2,1,0:T(8,128)(2,1)S(1)}, u32[]{:S(2)}, u32[]{:S(2)}) %collective-permute-start.16) | collective-permute-done | bytes 524320 | tf_op jit(solution)/shard_map/ppermute | solution.py:191
  62.5 0.8 copy-done.19
  63.3 2.9 %collective-permute-start.11 = (bf16[4,2,256,128]{3,2,1,0:T(8,128)(2,1)S(1)}, bf16[4,2,256,128]{3,2,1,0:T(8,128)(2,1)}, u32[]{:S(2)}, u32[]{:S(2)}) collective-permute-start(bf16[4,2,256,128]{3,2,1,0:T(8,128)(2,1)S(1)} %pad_maximum_fusion.1.rest_0_), channel_id=1, source_target_pairs={{0,24},{8,0},{16,8},{24,16},{1,25},{9,1},{17,9},{25,17},{2,26},{10... | collective-permute-start | bytes 1572872 | tf_op jit(solution)/shard_map/ppermute | solution.py:191
  66.3 0.9 constant_dynamic-slice_fusion.2
  67.2 1.4 collective-permute-start.18
  68.7 8.6 %collective-permute-done.10.rest_1_ = bf16[4,2,256,128]{3,2,1,0:T(8,128)(2,1)} collective-permute-done((bf16[4,2,256,128]{3,2,1,0:T(8,128)(2,1)S(1)}, bf16[4,2,256,128]{3,2,1,0:T(8,128)(2,1)}, u32[]{:S(2)}, u32[]{:S(2)}) %collective-permute-start.10) | collective-permute-done | bytes 524320 | tf_op jit(solution)/shard_map/ppermute | solution.py:191
  77.3 1.4 collective-permute-start.15
  79.7 2.2 %collective-permute-start.23 = (bf16[128,16]{0,1:T(8,128)(2,1)S(1)}, bf16[128,16]{0,1:T(8,128)(2,1)S(1)}, u32[]{:S(2)}, u32[]{:S(2)}) collective-permute-start(bf16[128,16]{0,1:T(8,128)(2,1)S(1)} %convolution_convert_fusion), channel_id=1, source_target_pairs={{0,1},{1,0},{2,3},{3,2},{4,5},{5,4},{6,7},{7,6},{8,9},{9,8},{10,11... | collective-permute-start | bytes 12296 | tf_op jit(solution)/shard_map/ppermute | solution.py:195
  81.9 7.5 %collective-permute-done.15.rest_7_ = bf16[4,2,256,128]{3,2,1,0:T(8,128)(2,1)} collective-permute-done((bf16[4,2,256,128]{3,2,1,0:T(8,128)(2,1)}, bf16[4,2,256,128]{3,2,1,0:T(8,128)(2,1)}, u32[]{:S(2)}, u32[]{:S(2)}) %collective-permute-start.15) | collective-permute-done | bytes 524320 | tf_op jit(solution)/shard_map/ppermute | solution.py:191
  89.4 2.7 %collective-permute-done.12.rest_3_ = bf16[4,2,256,128]{3,2,1,0:T(8,128)(2,1)S(1)} collective-permute-done((bf16[4,2,256,128]{3,2,1,0:T(8,128)(2,1)}, bf16[4,2,256,128]{3,2,1,0:T(8,128)(2,1)S(1)}, u32[]{:S(2)}, u32[]{:S(2)}) %collective-permute-start.12) | collective-permute-done | bytes 524320 | tf_op jit(solution)/shard_map/ppermute | solution.py:191
  92.8 1.0 copy-done.4
  93.9 1.0 copy-done.6
  94.9 1.0 copy-done.8
  96.0 1.0 copy-done.10
  97.0 1.0 copy-done.14
  98.0 1.0 copy-done.16
  99.1 1.0 copy-done.18
  100.1 1.0 copy-done.20
  101.2 1.0 copy-done.22
  102.2 50.7 %attend.1 = (bf16[128,4096]{1,0:T(8,128)(2,1)S(1)}, bf16[128,4096]{1,0:T(8,128)(2,1)S(1)}, bf16[128,4096]{1,0:T(8,128)(2,1)S(1)}, bf16[128,4096]{1,0:T(8,128)(2,1)S(1)}) custom-call(s32[768]{0:T(1024)S(1)} %reshape.64.lists, s32[32]{0:T(128)S(1)} %dynamic_slice.40.live, s32[2]{0:T(128)S(1)} %pad_add_fusion.1.off, bf16[128,8192]{1,0:T(8,128)(2,1)} %copy-done.23, ...), custom_call_target="tpu_custom_call" | custom-call | flops 8589934592 | bytes 16777216 | tf_op jit(solution)/shard_map/attend/pallas_call | solution.py:162
  153.3 9.3 %collective-permute-start.24 = (f32[128,16]{0,1:T(8,128)S(1)}, f32[128,16]{0,1:T(8,128)S(1)}, u32[]{:S(2)}, u32[]{:S(2)}) collective-permute-start(f32[128,16]{0,1:T(8,128)S(1)} %fusion.21), channel_id=1, source_target_pairs={{0,1},{1,0},{2,3},{3,2},{4,5},{5,4},{6,7},{7,6},{8,9},{9,8},{10,11... | collective-permute-start | bytes 24584 | tf_op jit(solution)/shard_map/ppermute | solution.py:195
  162.6 1.0 fusion.41
  163.6 1.6 fusion.5
  165.2 1.0 dynamic-slice_convert_fusion
  166.4 1.2 fusion.2
  167.6 1.1 convert_add_fusion
  169.4 1.4 collective-permute-start.27
  170.8 1.2 collective-permute-start.28
  172.1 4.0 %collective-permute-done.26 = bf16[32,1024]{1,0:T(8,128)(2,1)} collective-permute-done((bf16[32,1024]{1,0:T(8,128)(2,1)}, bf16[32,1024]{1,0:T(8,128)(2,1)}, u32[]{:S(2)}, u32[]{:S(2)}) %collective-permute-start.26) | collective-permute-done | bytes 65568 | tf_op jit(solution)/shard_map/ppermute | solution.py:191
  176.1 1.0 fusion.16
  177.2 0.9 collective-permute-start.30
  178.1 1.8 collective-permute-start.31
  179.9 2.0 collective-permute-done.29
  182.3 2.8 %collective-permute-start.32 = (bf16[32,1024]{1,0:T(8,128)(2,1)S(1)}, bf16[32,1024]{1,0:T(8,128)(2,1)S(1)}, u32[]{:S(2)}, u32[]{:S(2)}) collective-permute-start(bf16[32,1024]{1,0:T(8,128)(2,1)S(1)} %add_convert_fusion.1), channel_id=1, source_target_pairs={{0,64},{32,96},{64,0},{96,32},{1,65},{33,97},{65,1},{97,33},{2,66}... | collective-permute-start | bytes 196616 | tf_op jit(solution)/shard_map/ppermute | solution.py:191
  185.5 2.4 %collective-permute-start.34 = (bf16[32,1024]{1,0:T(8,128)(2,1)S(1)}, bf16[32,1024]{1,0:T(8,128)(2,1)S(1)}, u32[]{:S(2)}, u32[]{:S(2)}) collective-permute-start(bf16[32,1024]{1,0:T(8,128)(2,1)S(1)} %add_convert_fusion.1), channel_id=1, source_target_pairs={{0,96},{32,0},{64,32},{96,64},{1,97},{33,1},{65,33},{97,65},{2,98}... | collective-permute-start | bytes 196616 | tf_op jit(solution)/shard_map/ppermute | solution.py:191
  187.8 2.3 %collective-permute-done.33 = bf16[32,1024]{1,0:T(8,128)(2,1)S(1)} collective-permute-done((bf16[32,1024]{1,0:T(8,128)(2,1)S(1)}, bf16[32,1024]{1,0:T(8,128)(2,1)S(1)}, u32[]{:S(2)}, u32[]{:S(2)}) %collective-permute-start.33) | collective-permute-done | bytes 65568 | tf_op jit(solution)/shard_map/ppermute | solution.py:191
  191.0 2.6 %collective-permute-start.36 = (bf16[32,1024]{1,0:T(8,128)(2,1)S(1)}, bf16[32,1024]{1,0:T(8,128)(2,1)S(1)}, u32[]{:S(2)}, u32[]{:S(2)}) collective-permute-start(bf16[32,1024]{1,0:T(8,128)(2,1)S(1)} %add_convert_fusion), channel_id=1, source_target_pairs={{0,2},{2,4},{4,6},{6,0},{1,3},{3,5},{5,7},{7,1},{8,10},{10,12},{12... | collective-permute-start | bytes 196616 | tf_op jit(solution)/shard_map/ppermute | solution.py:191
  193.7 1.3 collective-permute-done.35
  195.7 1.1 collective-permute-done.37
  197.0 4.3 %collective-permute-start.38 = (bf16[32,4096]{1,0:T(8,128)(2,1)S(1)}, bf16[32,4096]{1,0:T(8,128)(2,1)S(1)}, u32[]{:S(2)}, u32[]{:S(2)}) collective-permute-start(bf16[32,4096]{1,0:T(8,128)(2,1)S(1)} %pad_maximum_fusion.7), channel_id=1, source_target_pairs={{0,1},{1,0},{2,3},{3,2},{4,5},{5,4},{6,7},{7,6},{8,9},{9,8},{10,11... | collective-permute-start | bytes 786440 | tf_op jit(solution)/shard_map/ppermute | solution.py:195
  201.4 1.1 collective-permute-done.38
  202.6 0.8 fusion.6
  203.5 0.8 fusion.8
  204.4 1.9 maximum_select_fusion
  (136 shorter events, 10.0 us)
Async XLA Ops:
  0.6 26.1 %copy-start = (bf16[1,128,8192]{2,1,0:T(8,128)(2,1)S(1)}, bf16[1,128,8192]{2,1,0:T(8,128)(2,1)}, u32[]{:S(2)}) copy-start(bf16[1,128,8192]{2,1,0:T(8,128)(2,1)} %param.12) | copy-start | bytes 6291460
  2.8 2.6 %collective-permute-start = (bf16[2,128,512]{2,1,0:T(8,128)(2,1)S(1)}, bf16[2,128,512]{2,1,0:T(8,128)(2,1)S(1)}, u32[]{:S(2)}, u32[]{:S(2)}) collective-permute-start(bf16[2,128,512]{2,1,0:T(8,128)(2,1)S(1)} %get-tuple-element.33), channel_id=1, source_target_pairs={{0,1},{1,0},{2,3},{3,2},{4,5},{5,4},{6,7},{7,6},{8,9},{9,8},{10,11... | collective-permute-start | bytes 786440 | tf_op jit(solution)/shard_map/ppermute | solution.py:195
  5.8 8.2 %collective-permute-start.6 = (bf16[2,2,256,128]{3,2,1,0:T(8,128)(2,1)S(1)}, bf16[2,2,256,128]{3,2,1,0:T(8,128)(2,1)S(1)}, u32[]{:S(2)}, u32[]{:S(2)}) collective-permute-start(bf16[2,2,256,128]{3,2,1,0:T(8,128)(2,1)S(1)} %pad_maximum_fusion.5), channel_id=1, source_target_pairs={{0,24},{8,0},{16,8},{24,16},{1,25},{9,1},{17,9},{25,17},{2,26},{10... | collective-permute-start | bytes 786440 | tf_op jit(solution)/shard_map/ppermute | solution.py:191
  8.7 8.8 %collective-permute-start.5 = (bf16[2,2,256,128]{3,2,1,0:T(8,128)(2,1)S(1)}, bf16[2,2,256,128]{3,2,1,0:T(8,128)(2,1)S(1)}, u32[]{:S(2)}, u32[]{:S(2)}) collective-permute-start(bf16[2,2,256,128]{3,2,1,0:T(8,128)(2,1)S(1)} %pad_maximum_fusion.5), channel_id=1, source_target_pairs={{0,8},{8,16},{16,24},{24,0},{1,9},{9,17},{17,25},{25,1},{2,10},{10... | collective-permute-start | bytes 786440 | tf_op jit(solution)/shard_map/ppermute | solution.py:191
  8.7 8.9 %collective-permute-start.2 = (bf16[2,2,256,128]{3,2,1,0:T(8,128)(2,1)S(1)}, bf16[2,2,256,128]{3,2,1,0:T(8,128)(2,1)S(1)}, u32[]{:S(2)}, u32[]{:S(2)}) collective-permute-start(bf16[2,2,256,128]{3,2,1,0:T(8,128)(2,1)S(1)} %copy.32), channel_id=1, source_target_pairs={{0,6},{2,0},{4,2},{6,4},{1,7},{3,1},{5,3},{7,5},{8,14},{10,8},{12,... | collective-permute-start | bytes 786440 | tf_op jit(solution)/shard_map/ppermute | solution.py:191
  12.6 9.0 %collective-permute-start.1 = (bf16[2,2,256,128]{3,2,1,0:T(8,128)(2,1)S(1)}, bf16[2,2,256,128]{3,2,1,0:T(8,128)(2,1)S(1)}, u32[]{:S(2)}, u32[]{:S(2)}) collective-permute-start(bf16[2,2,256,128]{3,2,1,0:T(8,128)(2,1)S(1)} %copy.32), channel_id=1, source_target_pairs={{0,2},{2,4},{4,6},{6,0},{1,3},{3,5},{5,7},{7,1},{8,10},{10,12},{12... | collective-permute-start | bytes 786440 | tf_op jit(solution)/shard_map/ppermute | solution.py:191
  14.0 7.6 %collective-permute-start.8 = (bf16[2,256,128]{2,1,0:T(8,128)(2,1)S(1)}, bf16[2,256,128]{2,1,0:T(8,128)(2,1)S(1)}, u32[]{:S(2)}, u32[]{:S(2)}) collective-permute-start(bf16[2,256,128]{2,1,0:T(8,128)(2,1)S(1)} %get-tuple-element.42), channel_id=1, source_target_pairs={{0,24},{8,0},{16,8},{24,16},{1,25},{9,1},{17,9},{25,17},{2,26},{10... | collective-permute-start | bytes 393224 | tf_op jit(solution)/shard_map/ppermute | solution.py:191
  17.6 6.0 %collective-permute-start.7 = (bf16[2,256,128]{2,1,0:T(8,128)(2,1)S(1)}, bf16[2,256,128]{2,1,0:T(8,128)(2,1)S(1)}, u32[]{:S(2)}, u32[]{:S(2)}) collective-permute-start(bf16[2,256,128]{2,1,0:T(8,128)(2,1)S(1)} %get-tuple-element.39), channel_id=1, source_target_pairs={{0,8},{8,16},{16,24},{24,0},{1,9},{9,17},{17,25},{25,1},{2,10},{10... | collective-permute-start | bytes 393224 | tf_op jit(solution)/shard_map/ppermute | solution.py:191
  17.7 5.8 %collective-permute-start.4 = (bf16[2,256,128]{2,1,0:T(8,128)(2,1)S(1)}, bf16[2,256,128]{2,1,0:T(8,128)(2,1)S(1)}, u32[]{:S(2)}, u32[]{:S(2)}) collective-permute-start(bf16[2,256,128]{2,1,0:T(8,128)(2,1)S(1)} %get-tuple-element.48), channel_id=1, source_target_pairs={{0,6},{2,0},{4,2},{6,4},{1,7},{3,1},{5,3},{7,5},{8,14},{10,8},{12,... | collective-permute-start | bytes 393224 | tf_op jit(solution)/shard_map/ppermute | solution.py:191
  21.6 5.1 %collective-permute-start.3 = (bf16[2,256,128]{2,1,0:T(8,128)(2,1)S(1)}, bf16[2,256,128]{2,1,0:T(8,128)(2,1)S(1)}, u32[]{:S(2)}, u32[]{:S(2)}) collective-permute-start(bf16[2,256,128]{2,1,0:T(8,128)(2,1)S(1)} %get-tuple-element.45), channel_id=1, source_target_pairs={{0,2},{2,4},{4,6},{6,0},{1,3},{3,5},{5,7},{7,1},{8,10},{10,12},{12... | collective-permute-start | bytes 393224 | tf_op jit(solution)/shard_map/ppermute | solution.py:191
  21.7 14.2 %copy-start.3 = (bf16[4,2,256,128]{3,2,1,0:T(8,128)(2,1)}, bf16[4,2,256,128]{3,2,1,0:T(8,128)(2,1)S(1)}, u32[]{:S(2)}) copy-start(bf16[4,2,256,128]{3,2,1,0:T(8,128)(2,1)S(1)} %pad_maximum_fusion.4.rest_12_) | copy-start | bytes 1572868
  23.5 3.3 %copy-start.30 = (bf16[8192,16]{0,1:T(8,128)(2,1)S(1)}, bf16[8192,16]{0,1:T(8,128)(2,1)}, u32[]{:S(2)}) copy-start(bf16[8192,16]{0,1:T(8,128)(2,1)} %param.17) | copy-start | bytes 786436
  23.6 27.7 %copy-start.5 = (bf16[4,2,256,128]{3,2,1,0:T(8,128)(2,1)}, bf16[4,2,256,128]{3,2,1,0:T(8,128)(2,1)S(1)}, u32[]{:S(2)}) copy-start(bf16[4,2,256,128]{3,2,1,0:T(8,128)(2,1)S(1)} %copy.37.rest_4_) | copy-start | bytes 1572868
  23.6 3.8 %copy-start.25 = (bf16[1,128,8192]{2,1,0:T(8,128)(2,1)S(1)}, bf16[1,128,8192]{2,1,0:T(8,128)(2,1)}, u32[]{:S(2)}) copy-start(bf16[1,128,8192]{2,1,0:T(8,128)(2,1)} %param.13) | copy-start | bytes 6291460
  23.6 3.8 %copy-start.26 = (bf16[16,8192]{1,0:T(8,128)(2,1)S(1)}, bf16[16,8192]{1,0:T(8,128)(2,1)}, u32[]{:S(2)}) copy-start(bf16[16,8192]{1,0:T(8,128)(2,1)} %param.18) | copy-start | bytes 786436
  23.7 12.6 %copy-start.7 = (bf16[4,2,256,128]{3,2,1,0:T(8,128)(2,1)}, bf16[4,2,256,128]{3,2,1,0:T(8,128)(2,1)S(1)}, u32[]{:S(2)}) copy-start(bf16[4,2,256,128]{3,2,1,0:T(8,128)(2,1)S(1)} %pad_maximum_fusion.3.rest_8_) | copy-start | bytes 1572868
  26.8 35.0 %copy-start.9 = (bf16[4,2,256,128]{3,2,1,0:T(8,128)(2,1)}, bf16[4,2,256,128]{3,2,1,0:T(8,128)(2,1)S(1)}, u32[]{:S(2)}) copy-start(bf16[4,2,256,128]{3,2,1,0:T(8,128)(2,1)S(1)} %pad_maximum_fusion.1.rest_0_) | copy-start | bytes 1572868
  27.4 1.6 copy-start.27
  29.0 1.3 copy-start.23
  30.4 48.9 %copy-start.31 = (s32[64]{0:T(128)S(1)}, s32[64]{0:T(128)}, u32[]{:S(2)}) copy-start(s32[64]{0:T(128)} %param.22) | copy-start | bytes 772
  31.9 60.9 %collective-permute-start.9 = (bf16[2,128,4096]{2,1,0:T(8,128)(2,1)}, bf16[2,128,4096]{2,1,0:T(8,128)(2,1)}, u32[]{:S(2)}, u32[]{:S(2)}) collective-permute-start(bf16[2,128,4096]{2,1,0:T(8,128)(2,1)} %pad_maximum_fusion), channel_id=1, source_target_pairs={{0,1},{1,0},{2,3},{3,2},{4,5},{5,4},{6,7},{7,6},{8,9},{9,8},{10,11... | collective-permute-start | bytes 6291464 | tf_op jit(solution)/shard_map/ppermute | solution.py:195
  34.8 13.5 %collective-permute-start.20 = (bf16[4,2,256,128]{3,2,1,0:T(8,128)(2,1)S(1)}, bf16[4,2,256,128]{3,2,1,0:T(8,128)(2,1)S(1)}, u32[]{:S(2)}, u32[]{:S(2)}) collective-permute-start(bf16[4,2,256,128]{3,2,1,0:T(8,128)(2,1)S(1)} %pad_maximum_fusion.4.rest_12_), channel_id=1, source_target_pairs={{0,6},{2,0},{4,2},{6,4},{1,7},{3,1},{5,3},{7,5},{8,14},{10,8},{12,... | collective-permute-start | bytes 1572872 | tf_op jit(solution)/shard_map/ppermute | solution.py:191
  36.0 15.3 %collective-permute-start.19 = (bf16[4,2,256,128]{3,2,1,0:T(8,128)(2,1)S(1)}, bf16[4,2,256,128]{3,2,1,0:T(8,128)(2,1)S(1)}, u32[]{:S(2)}, u32[]{:S(2)}) collective-permute-start(bf16[4,2,256,128]{3,2,1,0:T(8,128)(2,1)S(1)} %pad_maximum_fusion.4.rest_12_), channel_id=1, source_target_pairs={{0,2},{2,4},{4,6},{6,0},{1,3},{3,5},{5,7},{7,1},{8,10},{10,12},{12... | collective-permute-start | bytes 1572872 | tf_op jit(solution)/shard_map/ppermute | solution.py:191
  36.3 25.4 %collective-permute-start.16 = (bf16[4,2,256,128]{3,2,1,0:T(8,128)(2,1)S(1)}, bf16[4,2,256,128]{3,2,1,0:T(8,128)(2,1)S(1)}, u32[]{:S(2)}, u32[]{:S(2)}) collective-permute-start(bf16[4,2,256,128]{3,2,1,0:T(8,128)(2,1)S(1)} %pad_maximum_fusion.3.rest_8_), channel_id=1, source_target_pairs={{0,2},{2,4},{4,6},{6,0},{1,3},{3,5},{5,7},{7,1},{8,10},{10,12},{12... | collective-permute-start | bytes 1572872 | tf_op jit(solution)/shard_map/ppermute | solution.py:191
  36.3 25.4 %collective-permute-start.17 = (bf16[4,2,256,128]{3,2,1,0:T(8,128)(2,1)S(1)}, bf16[4,2,256,128]{3,2,1,0:T(8,128)(2,1)S(1)}, u32[]{:S(2)}, u32[]{:S(2)}) collective-permute-start(bf16[4,2,256,128]{3,2,1,0:T(8,128)(2,1)S(1)} %pad_maximum_fusion.3.rest_8_), channel_id=1, source_target_pairs={{0,6},{2,0},{4,2},{6,4},{1,7},{3,1},{5,3},{7,5},{8,14},{10,8},{12,... | collective-permute-start | bytes 1572872 | tf_op jit(solution)/shard_map/ppermute | solution.py:191
  48.3 13.4 %copy-start.13 = (bf16[4,2,256,128]{3,2,1,0:T(8,128)(2,1)}, bf16[4,2,256,128]{3,2,1,0:T(8,128)(2,1)S(1)}, u32[]{:S(2)}) copy-start(bf16[4,2,256,128]{3,2,1,0:T(8,128)(2,1)S(1)} %collective-permute-done.20.rest_14_) | copy-start | bytes 1572868
  48.3 18.8 %collective-permute-start.14 = (bf16[4,2,256,128]{3,2,1,0:T(8,128)(2,1)S(1)}, bf16[4,2,256,128]{3,2,1,0:T(8,128)(2,1)}, u32[]{:S(2)}, u32[]{:S(2)}) collective-permute-start(bf16[4,2,256,128]{3,2,1,0:T(8,128)(2,1)S(1)} %copy.37.rest_4_), channel_id=1, source_target_pairs={{0,24},{8,0},{16,8},{24,16},{1,25},{9,1},{17,9},{25,17},{2,26},{10... | collective-permute-start | bytes 1572872 | tf_op jit(solution)/shard_map/ppermute | solution.py:191
  52.1 15.2 %collective-permute-start.13 = (bf16[4,2,256,128]{3,2,1,0:T(8,128)(2,1)S(1)}, bf16[4,2,256,128]{3,2,1,0:T(8,128)(2,1)}, u32[]{:S(2)}, u32[]{:S(2)}) collective-permute-start(bf16[4,2,256,128]{3,2,1,0:T(8,128)(2,1)S(1)} %copy.37.rest_4_), channel_id=1, source_target_pairs={{0,8},{8,16},{16,24},{24,0},{1,9},{9,17},{17,25},{25,1},{2,10},{10... | collective-permute-start | bytes 1572872 | tf_op jit(solution)/shard_map/ppermute | solution.py:191
  61.7 15.5 %collective-permute-start.10 = (bf16[4,2,256,128]{3,2,1,0:T(8,128)(2,1)S(1)}, bf16[4,2,256,128]{3,2,1,0:T(8,128)(2,1)}, u32[]{:S(2)}, u32[]{:S(2)}) collective-permute-start(bf16[4,2,256,128]{3,2,1,0:T(8,128)(2,1)S(1)} %pad_maximum_fusion.1.rest_0_), channel_id=1, source_target_pairs={{0,8},{8,16},{16,24},{24,0},{1,9},{9,17},{17,25},{25,1},{2,10},{10... | collective-permute-start | bytes 1572872 | tf_op jit(solution)/shard_map/ppermute | solution.py:191
  63.3 15.3 %collective-permute-start.11 = (bf16[4,2,256,128]{3,2,1,0:T(8,128)(2,1)S(1)}, bf16[4,2,256,128]{3,2,1,0:T(8,128)(2,1)}, u32[]{:S(2)}, u32[]{:S(2)}) collective-permute-start(bf16[4,2,256,128]{3,2,1,0:T(8,128)(2,1)S(1)} %pad_maximum_fusion.1.rest_0_), channel_id=1, source_target_pairs={{0,24},{8,0},{16,8},{24,16},{1,25},{9,1},{17,9},{25,17},{2,26},{10... | collective-permute-start | bytes 1572872 | tf_op jit(solution)/shard_map/ppermute | solution.py:191
  67.2 12.6 %collective-permute-start.21 = (bf16[4,2,256,128]{3,2,1,0:T(8,128)(2,1)}, bf16[4,2,256,128]{3,2,1,0:T(8,128)(2,1)}, u32[]{:S(2)}, u32[]{:S(2)}) collective-permute-start(bf16[4,2,256,128]{3,2,1,0:T(8,128)(2,1)} %copy-done.13), channel_id=1, source_target_pairs={{0,6},{2,0},{4,2},{6,4},{1,7},{3,1},{5,3},{7,5},{8,14},{10,8},{12,... | collective-permute-start | bytes 1572872 | tf_op jit(solution)/shard_map/ppermute | solution.py:191
  67.2 14.6 %collective-permute-start.18 = (bf16[4,2,256,128]{3,2,1,0:T(8,128)(2,1)}, bf16[4,2,256,128]{3,2,1,0:T(8,128)(2,1)}, u32[]{:S(2)}, u32[]{:S(2)}) collective-permute-start(bf16[4,2,256,128]{3,2,1,0:T(8,128)(2,1)} %copy-done.17), channel_id=1, source_target_pairs={{0,2},{2,4},{4,6},{6,0},{1,3},{3,5},{5,7},{7,1},{8,10},{10,12},{12... | collective-permute-start | bytes 1572872 | tf_op jit(solution)/shard_map/ppermute | solution.py:191
  77.3 12.1 %collective-permute-start.15 = (bf16[4,2,256,128]{3,2,1,0:T(8,128)(2,1)}, bf16[4,2,256,128]{3,2,1,0:T(8,128)(2,1)}, u32[]{:S(2)}, u32[]{:S(2)}) collective-permute-start(bf16[4,2,256,128]{3,2,1,0:T(8,128)(2,1)} %collective-permute-done.14.rest_6_), channel_id=1, source_target_pairs={{0,24},{8,0},{16,8},{24,16},{1,25},{9,1},{17,9},{25,17},{2,26},{10... | collective-permute-start | bytes 1572872 | tf_op jit(solution)/shard_map/ppermute | solution.py:191
  78.6 13.4 %collective-permute-start.12 = (bf16[4,2,256,128]{3,2,1,0:T(8,128)(2,1)}, bf16[4,2,256,128]{3,2,1,0:T(8,128)(2,1)S(1)}, u32[]{:S(2)}, u32[]{:S(2)}) collective-permute-start(bf16[4,2,256,128]{3,2,1,0:T(8,128)(2,1)} %collective-permute-done.10.rest_1_), channel_id=1, source_target_pairs={{0,8},{8,16},{16,24},{24,0},{1,9},{9,17},{17,25},{25,1},{2,10},{10... | collective-permute-start | bytes 1572872 | tf_op jit(solution)/shard_map/ppermute | solution.py:191
  79.7 82.9 %collective-permute-start.23 = (bf16[128,16]{0,1:T(8,128)(2,1)S(1)}, bf16[128,16]{0,1:T(8,128)(2,1)S(1)}, u32[]{:S(2)}, u32[]{:S(2)}) collective-permute-start(bf16[128,16]{0,1:T(8,128)(2,1)S(1)} %convolution_convert_fusion), channel_id=1, source_target_pairs={{0,1},{1,0},{2,3},{3,2},{4,5},{5,4},{6,7},{7,6},{8,9},{9,8},{10,11... | collective-permute-start | bytes 12296 | tf_op jit(solution)/shard_map/ppermute | solution.py:195
  92.8 1.0 copy-start.4
  93.9 1.0 copy-start.6
  94.9 1.0 copy-start.8
  96.0 1.0 copy-start.10
  97.0 1.0 copy-start.14
  98.0 1.0 copy-start.16
  152.9 10.7 %copy-start.1 = (bf16[128,4096]{1,0:T(8,128)(2,1)}, bf16[128,4096]{1,0:T(8,128)(2,1)S(1)}, u32[]{:S(2)}) copy-start(bf16[128,4096]{1,0:T(8,128)(2,1)S(1)} %get-tuple-element.13) | copy-start | bytes 3145732
  152.9 10.7 %copy-start.11 = (bf16[128,4096]{1,0:T(8,128)(2,1)}, bf16[128,4096]{1,0:T(8,128)(2,1)S(1)}, u32[]{:S(2)}) copy-start(bf16[128,4096]{1,0:T(8,128)(2,1)S(1)} %get-tuple-element.14) | copy-start | bytes 3145732
  153.3 10.3 %collective-permute-start.24 = (f32[128,16]{0,1:T(8,128)S(1)}, f32[128,16]{0,1:T(8,128)S(1)}, u32[]{:S(2)}, u32[]{:S(2)}) collective-permute-start(f32[128,16]{0,1:T(8,128)S(1)} %fusion.21), channel_id=1, source_target_pairs={{0,1},{1,0},{2,3},{3,2},{4,5},{5,4},{6,7},{7,6},{8,9},{9,8},{10,11... | collective-permute-start | bytes 24584 | tf_op jit(solution)/shard_map/ppermute | solution.py:195
  166.1 1.5 collective-permute-start.25
  167.6 1.1 copy-start.24
  169.4 31.9 %copy-start.12 = (bf16[128,4096]{1,0:T(8,128)(2,1)S(1)}, bf16[128,4096]{1,0:T(8,128)(2,1)}, u32[]{:S(2)}) copy-start(bf16[128,4096]{1,0:T(8,128)(2,1)} %copy-done.11) | copy-start | bytes 3145732
  169.4 6.7 %collective-permute-start.26 = (bf16[32,1024]{1,0:T(8,128)(2,1)}, bf16[32,1024]{1,0:T(8,128)(2,1)}, u32[]{:S(2)}, u32[]{:S(2)}) collective-permute-start(bf16[32,1024]{1,0:T(8,128)(2,1)} %get-tuple-element.25), channel_id=1, source_target_pairs={{0,2},{2,4},{4,6},{6,0},{1,3},{3,5},{5,7},{7,1},{8,10},{10,12},{12... | collective-permute-start | bytes 196616 | tf_op jit(solution)/shard_map/ppermute | solution.py:191
  169.4 6.7 %collective-permute-start.27 = (bf16[32,1024]{1,0:T(8,128)(2,1)S(1)}, bf16[32,1024]{1,0:T(8,128)(2,1)}, u32[]{:S(2)}, u32[]{:S(2)}) collective-permute-start(bf16[32,1024]{1,0:T(8,128)(2,1)S(1)} %get-tuple-element.26), channel_id=1, source_target_pairs={{0,4},{2,6},{4,0},{6,2},{1,5},{3,7},{5,1},{7,3},{8,12},{10,14},{12... | collective-permute-start | bytes 196616 | tf_op jit(solution)/shard_map/ppermute | solution.py:191
  170.8 5.3 %collective-permute-start.28 = (bf16[32,1024]{1,0:T(8,128)(2,1)S(1)}, bf16[32,1024]{1,0:T(8,128)(2,1)}, u32[]{:S(2)}, u32[]{:S(2)}) collective-permute-start(bf16[32,1024]{1,0:T(8,128)(2,1)S(1)} %get-tuple-element.27), channel_id=1, source_target_pairs={{0,6},{2,0},{4,2},{6,4},{1,7},{3,1},{5,3},{7,5},{8,14},{10,8},{12,... | collective-permute-start | bytes 196616 | tf_op jit(solution)/shard_map/ppermute | solution.py:191
  177.1 4.8 %collective-permute-start.29 = (bf16[32,1024]{1,0:T(8,128)(2,1)S(1)}, bf16[32,1024]{1,0:T(8,128)(2,1)S(1)}, u32[]{:S(2)}, u32[]{:S(2)}) collective-permute-start(bf16[32,1024]{1,0:T(8,128)(2,1)S(1)} %fusion.16), channel_id=1, source_target_pairs={{0,16},{8,24},{16,0},{24,8},{1,17},{9,25},{17,1},{25,9},{2,18},{10... | collective-permute-start | bytes 196616 | tf_op jit(solution)/shard_map/ppermute | solution.py:191
  177.2 5.1 %collective-permute-start.30 = (bf16[32,1024]{1,0:T(8,128)(2,1)S(1)}, bf16[32,1024]{1,0:T(8,128)(2,1)S(1)}, u32[]{:S(2)}, u32[]{:S(2)}) collective-permute-start(bf16[32,1024]{1,0:T(8,128)(2,1)S(1)} %fusion.16), channel_id=1, source_target_pairs={{0,8},{8,16},{16,24},{24,0},{1,9},{9,17},{17,25},{25,1},{2,10},{10... | collective-permute-start | bytes 196616 | tf_op jit(solution)/shard_map/ppermute | solution.py:191
  178.1 4.2 %collective-permute-start.31 = (bf16[32,1024]{1,0:T(8,128)(2,1)S(1)}, bf16[32,1024]{1,0:T(8,128)(2,1)S(1)}, u32[]{:S(2)}, u32[]{:S(2)}) collective-permute-start(bf16[32,1024]{1,0:T(8,128)(2,1)S(1)} %fusion.16), channel_id=1, source_target_pairs={{0,24},{8,0},{16,8},{24,16},{1,25},{9,1},{17,9},{25,17},{2,26},{10... | collective-permute-start | bytes 196616 | tf_op jit(solution)/shard_map/ppermute | solution.py:191
  182.3 5.5 %collective-permute-start.32 = (bf16[32,1024]{1,0:T(8,128)(2,1)S(1)}, bf16[32,1024]{1,0:T(8,128)(2,1)S(1)}, u32[]{:S(2)}, u32[]{:S(2)}) collective-permute-start(bf16[32,1024]{1,0:T(8,128)(2,1)S(1)} %add_convert_fusion.1), channel_id=1, source_target_pairs={{0,64},{32,96},{64,0},{96,32},{1,65},{33,97},{65,1},{97,33},{2,66}... | collective-permute-start | bytes 196616 | tf_op jit(solution)/shard_map/ppermute | solution.py:191
  185.2 5.0 %collective-permute-start.33 = (bf16[32,1024]{1,0:T(8,128)(2,1)S(1)}, bf16[32,1024]{1,0:T(8,128)(2,1)S(1)}, u32[]{:S(2)}, u32[]{:S(2)}) collective-permute-start(bf16[32,1024]{1,0:T(8,128)(2,1)S(1)} %add_convert_fusion.1), channel_id=1, source_target_pairs={{0,32},{32,64},{64,96},{96,0},{1,33},{33,65},{65,97},{97,1},{2,34}... | collective-permute-start | bytes 196616 | tf_op jit(solution)/shard_map/ppermute | solution.py:191
  185.5 4.7 %collective-permute-start.34 = (bf16[32,1024]{1,0:T(8,128)(2,1)S(1)}, bf16[32,1024]{1,0:T(8,128)(2,1)S(1)}, u32[]{:S(2)}, u32[]{:S(2)}) collective-permute-start(bf16[32,1024]{1,0:T(8,128)(2,1)S(1)} %add_convert_fusion.1), channel_id=1, source_target_pairs={{0,96},{32,0},{64,32},{96,64},{1,97},{33,1},{65,33},{97,65},{2,98}... | collective-permute-start | bytes 196616 | tf_op jit(solution)/shard_map/ppermute | solution.py:191
  190.3 4.7 %collective-permute-start.35 = (bf16[32,1024]{1,0:T(8,128)(2,1)S(1)}, bf16[32,1024]{1,0:T(8,128)(2,1)S(1)}, u32[]{:S(2)}, u32[]{:S(2)}) collective-permute-start(bf16[32,1024]{1,0:T(8,128)(2,1)S(1)} %add_convert_fusion), channel_id=1, source_target_pairs={{0,4},{2,6},{4,0},{6,2},{1,5},{3,7},{5,1},{7,3},{8,12},{10,14},{12... | collective-permute-start | bytes 196616 | tf_op jit(solution)/shard_map/ppermute | solution.py:191
  191.0 4.7 %collective-permute-start.36 = (bf16[32,1024]{1,0:T(8,128)(2,1)S(1)}, bf16[32,1024]{1,0:T(8,128)(2,1)S(1)}, u32[]{:S(2)}, u32[]{:S(2)}) collective-permute-start(bf16[32,1024]{1,0:T(8,128)(2,1)S(1)} %add_convert_fusion), channel_id=1, source_target_pairs={{0,2},{2,4},{4,6},{6,0},{1,3},{3,5},{5,7},{7,1},{8,10},{10,12},{12... | collective-permute-start | bytes 196616 | tf_op jit(solution)/shard_map/ppermute | solution.py:191
  193.7 3.1 %collective-permute-start.37 = (bf16[32,1024]{1,0:T(8,128)(2,1)S(1)}, bf16[32,1024]{1,0:T(8,128)(2,1)S(1)}, u32[]{:S(2)}, u32[]{:S(2)}) collective-permute-start(bf16[32,1024]{1,0:T(8,128)(2,1)S(1)} %add_convert_fusion), channel_id=1, source_target_pairs={{0,6},{2,0},{4,2},{6,4},{1,7},{3,1},{5,3},{7,5},{8,14},{10,8},{12,... | collective-permute-start | bytes 196616 | tf_op jit(solution)/shard_map/ppermute | solution.py:191
  196.9 5.7 %copy-start.28 = (f32[16,8192]{1,0:T(8,128)S(1)}, f32[16,8192]{1,0:T(8,128)}, u32[]{:S(2)}) copy-start(f32[16,8192]{1,0:T(8,128)} %param.20) | copy-start | bytes 1572868
  197.0 5.4 %collective-permute-start.38 = (bf16[32,4096]{1,0:T(8,128)(2,1)S(1)}, bf16[32,4096]{1,0:T(8,128)(2,1)S(1)}, u32[]{:S(2)}, u32[]{:S(2)}) collective-permute-start(bf16[32,4096]{1,0:T(8,128)(2,1)S(1)} %pad_maximum_fusion.7), channel_id=1, source_target_pairs={{0,1},{1,0},{2,3},{3,2},{4,5},{5,4},{6,7},{7,6},{8,9},{9,8},{10,11... | collective-permute-start | bytes 786440 | tf_op jit(solution)/shard_map/ppermute | solution.py:195
  201.3 3.1 %collective-permute-start.22 = (bf16[128,4096]{1,0:T(8,128)(2,1)S(1)}, bf16[128,4096]{1,0:T(8,128)(2,1)S(1)}, u32[]{:S(2)}, u32[]{:S(2)}) collective-permute-start(bf16[128,4096]{1,0:T(8,128)(2,1)S(1)} %copy-done.12), channel_id=1, source_target_pairs={{0,1},{1,0},{2,3},{3,2},{4,5},{5,4},{6,7},{7,6},{8,9},{9,8},{10,11... | collective-permute-start | bytes 3145736 | tf_op jit(solution)/shard_map/ppermute | solution.py:195
  202.5 1.0 copy-start.29
  202.6 1.7 copy-start.2
  (7 other events, 6.3 us)

commit v4 on v3

--- a/solution.py
+++ b/solution.py
@@ -158,15 +158,16 @@
     far = pl.BlockSpec((2, D, D), lambda h, a, b, off: (0, 0, h))
     res = pl.BlockSpec((D, D), lambda h, a, b, off: (0, h))
     shape = jax.ShapeDtypeStruct((D, HEADS * D), BF16)
+    both = jax.ShapeDtypeStruct((D, 2 * HEADS * D), BF16)
     n_copies = max(len(c) for c in copies)
     return pl.pallas_call(
         functools.partial(attention_kernel, len(srcs), copies),
-        out_shape=(shape,) * 4,
+        out_shape=(both, shape, shape, shape),
         grid_spec=pltpu.PrefetchScalarGridSpec(
             num_scalar_prefetch=3,
             grid=(HEADS,),
             in_specs=[whole, whole, far] + [pl.BlockSpec(memory_space=pl.ANY)] * len(srcs),
-            out_specs=(res,) * 4,
+            out_specs=(whole, res, res, res),
             scratch_shapes=[
                 pltpu.VMEM((4, 16, 256, 2 * D), BF16),
                 pltpu.VMEM((2 * D, 4096), BF16),
@@ -204,8 +205,7 @@
     keys2, values2 = hop(less[0], first, 1), hop(more[1], first, -1)
     keys = row_major(jnp.stack([own[0], less[0], more[0], keys2]))
     values = row_major(jnp.stack([own[1], less[1], more[1], values2]))
-    keys_less = hop(keys, second, 1)
-    values_more = hop(values, second, -1)
+    keys_less, values_more = hop(keys, second, 1), hop(values, second, -1)
     keys_more, values_less = hop(keys, second, -1), hop(values, second, 1)
     keys2, values2 = hop(keys_less, second, 1), hop(values_more, second, -1)
     return [keys, keys_less, keys_more, keys2, values, values_less, values_more, values2]
@@ -297,11 +297,7 @@
     )
 
     far_half = swap(far_half)
-    attended = jnp.where(
-        core == 0,
-        jnp.concatenate([own_half, far_half], 1),
-        jnp.concatenate([far_half, own_half], 1),
-    )
+    attended = lax.dynamic_update_slice(own_half, far_half, (0, away))
 
     my_up = lax.dynamic_slice_in_dim(up, core * half, half, 1)
     low_grad_far = swap(lax.dot_general(d_far, my_up, NT, preferred_element_type=F32))

time: 207 us -> 210 us (1.014)
  local copies, waits for them, and re-layouts: 19.5 us -> 22.5 us
    unnamed x70 -> x72, local copies, waits for them, and re-layouts: 15.8 us -> 18.8 us
where the time goes in v4:
time: 210 us; the launch traced here: 209 us
  starting transfers between devices  62.2 us (30%)
  waiting for transfers between devices  58.1 us (28%)
  Pallas kernels  52.2 us (25%)
  local copies, waits for them, and re-layouts  22.5 us (11%)
  other arithmetic  7.24 us (3%)
  matrix products  5.48 us (3%)
    ppermute x32, waiting for transfers between devices, hop(): return lax.ppermute(x, axis, [(i, (i + by) % 4) for i in range(4)])  55.9 us
    pallas_call x1, Pallas kernels, attention(): pl.pallas_call(functools.partial(attention_kernel, len(srcs), copies), ou...  52.2 us
    ppermute x32, starting transfers between devices, hop(): return lax.ppermute(x, axis, [(i, (i + by) % 4) for i in range(4)])  41.7 us
    ppermute x7, starting transfers between devices, swap(): return lax.ppermute(x, 'core', [(0, 1), (1, 0)])  20.5 us
    unnamed x72, local copies, waits for them, and re-layouts  18.8 us
  transfers between devices with their start and end apart: 39, of which 18 were waited for; matrix products, arithmetic and copies ran while one was open for 3% of the time, Pallas kernels for 25%

profile of v4, /device:TPU:1, one launch (start us, length us, event | category | flops | bytes accessed | tf_op | source)
XLA Modules:
  0.0 208.9 jit_solution(7022273374943771797)
XLA Ops:
  0.7 1.1 constant_dynamic-update-slice_fusion.1
  1.8 1.0 constant_dynamic-update-slice_fusion
  2.8 1.5 collective-permute-start
  4.3 1.2 collective-permute-done
  5.8 2.9 %collective-permute-start.6 = (bf16[2,2,256,128]{3,2,1,0:T(8,128)(2,1)S(1)}, bf16[2,2,256,128]{3,2,1,0:T(8,128)(2,1)S(1)}, u32[]{:S(2)}, u32[]{:S(2)}) collective-permute-start(bf16[2,2,256,128]{3,2,1,0:T(8,128)(2,1)S(1)} %pad_maximum_fusion.5), channel_id=1, source_target_pairs={{0,24},{8,0},{16,8},{24,16},{1,25},{9,1},{17,9},{25,17},{2,26},{10... | collective-permute-start | bytes 786440 | tf_op jit(solution)/shard_map/ppermute | solution.py:192
  8.7 3.8 %collective-permute-start.2 = (bf16[2,2,256,128]{3,2,1,0:T(8,128)(2,1)S(1)}, bf16[2,2,256,128]{3,2,1,0:T(8,128)(2,1)S(1)}, u32[]{:S(2)}, u32[]{:S(2)}) collective-permute-start(bf16[2,2,256,128]{3,2,1,0:T(8,128)(2,1)S(1)} %copy.32), channel_id=1, source_target_pairs={{0,6},{2,0},{4,2},{6,4},{1,7},{3,1},{5,3},{7,5},{8,14},{10,8},{12,... | collective-permute-start | bytes 786440 | tf_op jit(solution)/shard_map/ppermute | solution.py:192
  12.6 1.3 collective-permute-done.6
  14.0 3.5 %collective-permute-start.8 = (bf16[2,256,128]{2,1,0:T(8,128)(2,1)S(1)}, bf16[2,256,128]{2,1,0:T(8,128)(2,1)S(1)}, u32[]{:S(2)}, u32[]{:S(2)}) collective-permute-start(bf16[2,256,128]{2,1,0:T(8,128)(2,1)S(1)} %get-tuple-element.42), channel_id=1, source_target_pairs={{0,24},{8,0},{16,8},{24,16},{1,25},{9,1},{17,9},{25,17},{2,26},{10... | collective-permute-start | bytes 393224 | tf_op jit(solution)/shard_map/ppermute | solution.py:192
  17.7 3.8 %collective-permute-start.4 = (bf16[2,256,128]{2,1,0:T(8,128)(2,1)S(1)}, bf16[2,256,128]{2,1,0:T(8,128)(2,1)S(1)}, u32[]{:S(2)}, u32[]{:S(2)}) collective-permute-start(bf16[2,256,128]{2,1,0:T(8,128)(2,1)S(1)} %get-tuple-element.48), channel_id=1, source_target_pairs={{0,6},{2,0},{4,2},{6,4},{1,7},{3,1},{5,3},{7,5},{8,14},{10,8},{12,... | collective-permute-start | bytes 393224 | tf_op jit(solution)/shard_map/ppermute | solution.py:192
  21.8 1.7 collective-permute-done.4
  23.7 3.0 %collective-permute-done.3 = bf16[2,256,128]{2,1,0:T(8,128)(2,1)S(1)} collective-permute-done((bf16[2,256,128]{2,1,0:T(8,128)(2,1)S(1)}, bf16[2,256,128]{2,1,0:T(8,128)(2,1)S(1)}, u32[]{:S(2)}, u32[]{:S(2)}) %collective-permute-start.3) | collective-permute-done | bytes 131104 | tf_op jit(solution)/shard_map/ppermute | solution.py:192
  28.2 0.8 copy-done.26
  29.3 1.1 copy-done.1
  30.4 1.6 pad_maximum_fusion
  31.9 2.9 %collective-permute-start.9 = (bf16[2,128,4096]{2,1,0:T(8,128)(2,1)}, bf16[2,128,4096]{2,1,0:T(8,128)(2,1)}, u32[]{:S(2)}, u32[]{:S(2)}) collective-permute-start(bf16[2,128,4096]{2,1,0:T(8,128)(2,1)} %pad_maximum_fusion), channel_id=1, source_target_pairs={{0,1},{1,0},{2,3},{3,2},{4,5},{5,4},{6,7},{7,6},{8,9},{9,8},{10,11... | collective-permute-start | bytes 6291464 | tf_op jit(solution)/shard_map/ppermute | solution.py:196
  34.9 1.1 collective-permute-start.20
  36.4 2.7 %collective-permute-start.17 = (bf16[4,2,256,128]{3,2,1,0:T(8,128)(2,1)S(1)}, bf16[4,2,256,128]{3,2,1,0:T(8,128)(2,1)S(1)}, u32[]{:S(2)}, u32[]{:S(2)}) collective-permute-start(bf16[4,2,256,128]{3,2,1,0:T(8,128)(2,1)S(1)} %pad_maximum_fusion.3.rest_8_), channel_id=1, source_target_pairs={{0,6},{2,0},{4,2},{6,4},{1,7},{3,1},{5,3},{7,5},{8,14},{10,8},{12,... | collective-permute-start | bytes 1572872 | tf_op jit(solution)/shard_map/ppermute | solution.py:192
  39.0 9.3 %collective-permute-done.20.rest_14_ = bf16[4,2,256,128]{3,2,1,0:T(8,128)(2,1)S(1)} collective-permute-done((bf16[4,2,256,128]{3,2,1,0:T(8,128)(2,1)S(1)}, bf16[4,2,256,128]{3,2,1,0:T(8,128)(2,1)S(1)}, u32[]{:S(2)}, u32[]{:S(2)}) %collective-permute-start.20) | collective-permute-done | bytes 524320 | tf_op jit(solution)/shard_map/ppermute | solution.py:192
  48.4 2.9 %collective-permute-start.14 = (bf16[4,2,256,128]{3,2,1,0:T(8,128)(2,1)S(1)}, bf16[4,2,256,128]{3,2,1,0:T(8,128)(2,1)}, u32[]{:S(2)}, u32[]{:S(2)}) collective-permute-start(bf16[4,2,256,128]{3,2,1,0:T(8,128)(2,1)S(1)} %copy.37.rest_4_), channel_id=1, source_target_pairs={{0,24},{8,0},{16,8},{24,16},{1,25},{9,1},{17,9},{25,17},{2,26},{10... | collective-permute-start | bytes 1572872 | tf_op jit(solution)/shard_map/ppermute | solution.py:192
  52.1 9.7 %collective-permute-done.16.rest_9_ = bf16[4,2,256,128]{3,2,1,0:T(8,128)(2,1)S(1)} collective-permute-done((bf16[4,2,256,128]{3,2,1,0:T(8,128)(2,1)S(1)}, bf16[4,2,256,128]{3,2,1,0:T(8,128)(2,1)S(1)}, u32[]{:S(2)}, u32[]{:S(2)}) %collective-permute-start.16) | collective-permute-done | bytes 524320 | tf_op jit(solution)/shard_map/ppermute | solution.py:192
  62.6 0.8 copy-done.19
  63.4 2.9 %collective-permute-start.11 = (bf16[4,2,256,128]{3,2,1,0:T(8,128)(2,1)S(1)}, bf16[4,2,256,128]{3,2,1,0:T(8,128)(2,1)}, u32[]{:S(2)}, u32[]{:S(2)}) collective-permute-start(bf16[4,2,256,128]{3,2,1,0:T(8,128)(2,1)S(1)} %pad_maximum_fusion.1.rest_0_), channel_id=1, source_target_pairs={{0,24},{8,0},{16,8},{24,16},{1,25},{9,1},{17,9},{25,17},{2,26},{10... | collective-permute-start | bytes 1572872 | tf_op jit(solution)/shard_map/ppermute | solution.py:192
  66.3 0.9 constant_dynamic-slice_fusion.2
  67.3 1.4 collective-permute-start.18
  68.7 8.6 %collective-permute-done.10.rest_1_ = bf16[4,2,256,128]{3,2,1,0:T(8,128)(2,1)} collective-permute-done((bf16[4,2,256,128]{3,2,1,0:T(8,128)(2,1)S(1)}, bf16[4,2,256,128]{3,2,1,0:T(8,128)(2,1)}, u32[]{:S(2)}, u32[]{:S(2)}) %collective-permute-start.10) | collective-permute-done | bytes 524320 | tf_op jit(solution)/shard_map/ppermute | solution.py:192
  77.3 1.3 collective-permute-start.15
  79.8 2.2 %collective-permute-start.23 = (bf16[128,16]{0,1:T(8,128)(2,1)S(1)}, bf16[128,16]{0,1:T(8,128)(2,1)S(1)}, u32[]{:S(2)}, u32[]{:S(2)}) collective-permute-start(bf16[128,16]{0,1:T(8,128)(2,1)S(1)} %convolution_convert_fusion), channel_id=1, source_target_pairs={{0,1},{1,0},{2,3},{3,2},{4,5},{5,4},{6,7},{7,6},{8,9},{9,8},{10,11... | collective-permute-start | bytes 12296 | tf_op jit(solution)/shard_map/ppermute | solution.py:196
  81.9 7.5 %collective-permute-done.15.rest_7_ = bf16[4,2,256,128]{3,2,1,0:T(8,128)(2,1)} collective-permute-done((bf16[4,2,256,128]{3,2,1,0:T(8,128)(2,1)}, bf16[4,2,256,128]{3,2,1,0:T(8,128)(2,1)}, u32[]{:S(2)}, u32[]{:S(2)}) %collective-permute-start.15) | collective-permute-done | bytes 524320 | tf_op jit(solution)/shard_map/ppermute | solution.py:192
  89.4 2.6 %collective-permute-done.12.rest_3_ = bf16[4,2,256,128]{3,2,1,0:T(8,128)(2,1)S(1)} collective-permute-done((bf16[4,2,256,128]{3,2,1,0:T(8,128)(2,1)}, bf16[4,2,256,128]{3,2,1,0:T(8,128)(2,1)S(1)}, u32[]{:S(2)}, u32[]{:S(2)}) %collective-permute-start.12) | collective-permute-done | bytes 524320 | tf_op jit(solution)/shard_map/ppermute | solution.py:192
  92.9 1.6 copy-done.2
  94.4 1.0 copy-done.4
  95.5 1.0 copy-done.6
  96.5 1.0 copy-done.8
  97.6 1.0 copy-done.10
  98.6 1.0 copy-done.14
  99.7 1.0 copy-done.16
  100.7 1.0 copy-done.18
  101.7 1.0 copy-done.20
  102.8 1.0 copy-done.22
  103.8 52.2 %attend.1 = (bf16[128,8192]{1,0:T(8,128)(2,1)}, bf16[128,4096]{1,0:T(8,128)(2,1)S(1)}, bf16[128,4096]{1,0:T(8,128)(2,1)S(1)}, bf16[128,4096]{1,0:T(8,128)(2,1)S(1)}) custom-call(s32[768]{0:T(1024)S(1)} %reshape.11.lists, s32[32]{0:T(128)S(1)} %dynamic_slice.40.live, s32[2]{0:T(128)S(1)} %pad_add_fusion.1.off, bf16[128,8192]{1,0:T(8,128)(2,1)S(1)} %copy-done.2, ...), custom_call_target="tpu_custom_call" | custom-call | flops 8589934592 | bytes 16777216 | tf_op jit(solution)/shard_map/attend/pallas_call | solution.py:163
  156.4 9.3 %collective-permute-start.24 = (f32[128,16]{0,1:T(8,128)S(1)}, f32[128,16]{0,1:T(8,128)S(1)}, u32[]{:S(2)}, u32[]{:S(2)}) collective-permute-start(f32[128,16]{0,1:T(8,128)S(1)} %fusion.21), channel_id=1, source_target_pairs={{0,1},{1,0},{2,3},{3,2},{4,5},{5,4},{6,7},{7,6},{8,9},{9,8},{10,11... | collective-permute-start | bytes 24584 | tf_op jit(solution)/shard_map/ppermute | solution.py:196
  165.7 1.0 fusion.41
  166.6 1.6 fusion.5
  168.2 1.0 dynamic-slice_convert_fusion
  169.4 1.2 fusion.2
  170.7 1.1 convert_add_fusion
  172.4 1.5 collective-permute-start.27
  173.9 1.2 collective-permute-start.28
  175.1 4.0 %collective-permute-done.26 = bf16[32,1024]{1,0:T(8,128)(2,1)} collective-permute-done((bf16[32,1024]{1,0:T(8,128)(2,1)}, bf16[32,1024]{1,0:T(8,128)(2,1)}, u32[]{:S(2)}, u32[]{:S(2)}) %collective-permute-start.26) | collective-permute-done | bytes 65568 | tf_op jit(solution)/shard_map/ppermute | solution.py:192
  179.1 1.0 fusion.16
  180.2 1.0 collective-permute-start.30
  181.2 1.7 collective-permute-start.31
  182.9 2.0 collective-permute-done.29
  185.3 2.8 %collective-permute-start.32 = (bf16[32,1024]{1,0:T(8,128)(2,1)S(1)}, bf16[32,1024]{1,0:T(8,128)(2,1)S(1)}, u32[]{:S(2)}, u32[]{:S(2)}) collective-permute-start(bf16[32,1024]{1,0:T(8,128)(2,1)S(1)} %add_convert_fusion.1), channel_id=1, source_target_pairs={{0,64},{32,96},{64,0},{96,32},{1,65},{33,97},{65,1},{97,33},{2,66}... | collective-permute-start | bytes 196616 | tf_op jit(solution)/shard_map/ppermute | solution.py:192
  188.5 2.4 %collective-permute-start.34 = (bf16[32,1024]{1,0:T(8,128)(2,1)S(1)}, bf16[32,1024]{1,0:T(8,128)(2,1)S(1)}, u32[]{:S(2)}, u32[]{:S(2)}) collective-permute-start(bf16[32,1024]{1,0:T(8,128)(2,1)S(1)} %add_convert_fusion.1), channel_id=1, source_target_pairs={{0,96},{32,0},{64,32},{96,64},{1,97},{33,1},{65,33},{97,65},{2,98}... | collective-permute-start | bytes 196616 | tf_op jit(solution)/shard_map/ppermute | solution.py:192
  190.9 2.3 %collective-permute-done.33 = bf16[32,1024]{1,0:T(8,128)(2,1)S(1)} collective-permute-done((bf16[32,1024]{1,0:T(8,128)(2,1)S(1)}, bf16[32,1024]{1,0:T(8,128)(2,1)S(1)}, u32[]{:S(2)}, u32[]{:S(2)}) %collective-permute-start.33) | collective-permute-done | bytes 65568 | tf_op jit(solution)/shard_map/ppermute | solution.py:192
  194.0 2.7 %collective-permute-start.36 = (bf16[32,1024]{1,0:T(8,128)(2,1)S(1)}, bf16[32,1024]{1,0:T(8,128)(2,1)S(1)}, u32[]{:S(2)}, u32[]{:S(2)}) collective-permute-start(bf16[32,1024]{1,0:T(8,128)(2,1)S(1)} %add_convert_fusion), channel_id=1, source_target_pairs={{0,2},{2,4},{4,6},{6,0},{1,3},{3,5},{5,7},{7,1},{8,10},{10,12},{12... | collective-permute-start | bytes 196616 | tf_op jit(solution)/shard_map/ppermute | solution.py:192
  196.7 1.3 collective-permute-done.35
  198.7 1.1 collective-permute-done.37
  200.0 4.3 %collective-permute-start.38 = (bf16[32,4096]{1,0:T(8,128)(2,1)S(1)}, bf16[32,4096]{1,0:T(8,128)(2,1)S(1)}, u32[]{:S(2)}, u32[]{:S(2)}) collective-permute-start(bf16[32,4096]{1,0:T(8,128)(2,1)S(1)} %pad_maximum_fusion.7), channel_id=1, source_target_pairs={{0,1},{1,0},{2,3},{3,2},{4,5},{5,4},{6,7},{7,6},{8,9},{9,8},{10,11... | collective-permute-start | bytes 786440 | tf_op jit(solution)/shard_map/ppermute | solution.py:196
  204.4 1.1 collective-permute-done.38
  205.7 0.8 fusion.6
  206.6 0.8 fusion.8
  207.6 1.3 copy-done.31
  (138 shorter events, 11.0 us)
Async XLA Ops:
  0.6 26.1 %copy-start = (bf16[1,128,8192]{2,1,0:T(8,128)(2,1)S(1)}, bf16[1,128,8192]{2,1,0:T(8,128)(2,1)}, u32[]{:S(2)}) copy-start(bf16[1,128,8192]{2,1,0:T(8,128)(2,1)} %param.12) | copy-start | bytes 6291460
  2.8 2.6 %collective-permute-start = (bf16[2,128,512]{2,1,0:T(8,128)(2,1)S(1)}, bf16[2,128,512]{2,1,0:T(8,128)(2,1)S(1)}, u32[]{:S(2)}, u32[]{:S(2)}) collective-permute-start(bf16[2,128,512]{2,1,0:T(8,128)(2,1)S(1)} %get-tuple-element.33), channel_id=1, source_target_pairs={{0,1},{1,0},{2,3},{3,2},{4,5},{5,4},{6,7},{7,6},{8,9},{9,8},{10,11... | collective-permute-start | bytes 786440 | tf_op jit(solution)/shard_map/ppermute | solution.py:196
  5.8 8.2 %collective-permute-start.6 = (bf16[2,2,256,128]{3,2,1,0:T(8,128)(2,1)S(1)}, bf16[2,2,256,128]{3,2,1,0:T(8,128)(2,1)S(1)}, u32[]{:S(2)}, u32[]{:S(2)}) collective-permute-start(bf16[2,2,256,128]{3,2,1,0:T(8,128)(2,1)S(1)} %pad_maximum_fusion.5), channel_id=1, source_target_pairs={{0,24},{8,0},{16,8},{24,16},{1,25},{9,1},{17,9},{25,17},{2,26},{10... | collective-permute-start | bytes 786440 | tf_op jit(solution)/shard_map/ppermute | solution.py:192
  8.7 8.8 %collective-permute-start.5 = (bf16[2,2,256,128]{3,2,1,0:T(8,128)(2,1)S(1)}, bf16[2,2,256,128]{3,2,1,0:T(8,128)(2,1)S(1)}, u32[]{:S(2)}, u32[]{:S(2)}) collective-permute-start(bf16[2,2,256,128]{3,2,1,0:T(8,128)(2,1)S(1)} %pad_maximum_fusion.5), channel_id=1, source_target_pairs={{0,8},{8,16},{16,24},{24,0},{1,9},{9,17},{17,25},{25,1},{2,10},{10... | collective-permute-start | bytes 786440 | tf_op jit(solution)/shard_map/ppermute | solution.py:192
  8.7 8.9 %collective-permute-start.2 = (bf16[2,2,256,128]{3,2,1,0:T(8,128)(2,1)S(1)}, bf16[2,2,256,128]{3,2,1,0:T(8,128)(2,1)S(1)}, u32[]{:S(2)}, u32[]{:S(2)}) collective-permute-start(bf16[2,2,256,128]{3,2,1,0:T(8,128)(2,1)S(1)} %copy.32), channel_id=1, source_target_pairs={{0,6},{2,0},{4,2},{6,4},{1,7},{3,1},{5,3},{7,5},{8,14},{10,8},{12,... | collective-permute-start | bytes 786440 | tf_op jit(solution)/shard_map/ppermute | solution.py:192
  12.6 9.0 %collective-permute-start.1 = (bf16[2,2,256,128]{3,2,1,0:T(8,128)(2,1)S(1)}, bf16[2,2,256,128]{3,2,1,0:T(8,128)(2,1)S(1)}, u32[]{:S(2)}, u32[]{:S(2)}) collective-permute-start(bf16[2,2,256,128]{3,2,1,0:T(8,128)(2,1)S(1)} %copy.32), channel_id=1, source_target_pairs={{0,2},{2,4},{4,6},{6,0},{1,3},{3,5},{5,7},{7,1},{8,10},{10,12},{12... | collective-permute-start | bytes 786440 | tf_op jit(solution)/shard_map/ppermute | solution.py:192
  14.0 7.6 %collective-permute-start.8 = (bf16[2,256,128]{2,1,0:T(8,128)(2,1)S(1)}, bf16[2,256,128]{2,1,0:T(8,128)(2,1)S(1)}, u32[]{:S(2)}, u32[]{:S(2)}) collective-permute-start(bf16[2,256,128]{2,1,0:T(8,128)(2,1)S(1)} %get-tuple-element.42), channel_id=1, source_target_pairs={{0,24},{8,0},{16,8},{24,16},{1,25},{9,1},{17,9},{25,17},{2,26},{10... | collective-permute-start | bytes 393224 | tf_op jit(solution)/shard_map/ppermute | solution.py:192
  17.6 6.0 %collective-permute-start.7 = (bf16[2,256,128]{2,1,0:T(8,128)(2,1)S(1)}, bf16[2,256,128]{2,1,0:T(8,128)(2,1)S(1)}, u32[]{:S(2)}, u32[]{:S(2)}) collective-permute-start(bf16[2,256,128]{2,1,0:T(8,128)(2,1)S(1)} %get-tuple-element.39), channel_id=1, source_target_pairs={{0,8},{8,16},{16,24},{24,0},{1,9},{9,17},{17,25},{25,1},{2,10},{10... | collective-permute-start | bytes 393224 | tf_op jit(solution)/shard_map/ppermute | solution.py:192
  17.7 5.8 %collective-permute-start.4 = (bf16[2,256,128]{2,1,0:T(8,128)(2,1)S(1)}, bf16[2,256,128]{2,1,0:T(8,128)(2,1)S(1)}, u32[]{:S(2)}, u32[]{:S(2)}) collective-permute-start(bf16[2,256,128]{2,1,0:T(8,128)(2,1)S(1)} %get-tuple-element.48), channel_id=1, source_target_pairs={{0,6},{2,0},{4,2},{6,4},{1,7},{3,1},{5,3},{7,5},{8,14},{10,8},{12,... | collective-permute-start | bytes 393224 | tf_op jit(solution)/shard_map/ppermute | solution.py:192
  21.6 5.1 %collective-permute-start.3 = (bf16[2,256,128]{2,1,0:T(8,128)(2,1)S(1)}, bf16[2,256,128]{2,1,0:T(8,128)(2,1)S(1)}, u32[]{:S(2)}, u32[]{:S(2)}) collective-permute-start(bf16[2,256,128]{2,1,0:T(8,128)(2,1)S(1)} %get-tuple-element.45), channel_id=1, source_target_pairs={{0,2},{2,4},{4,6},{6,0},{1,3},{3,5},{5,7},{7,1},{8,10},{10,12},{12... | collective-permute-start | bytes 393224 | tf_op jit(solution)/shard_map/ppermute | solution.py:192
  21.7 14.3 %copy-start.3 = (bf16[4,2,256,128]{3,2,1,0:T(8,128)(2,1)}, bf16[4,2,256,128]{3,2,1,0:T(8,128)(2,1)S(1)}, u32[]{:S(2)}) copy-start(bf16[4,2,256,128]{3,2,1,0:T(8,128)(2,1)S(1)} %pad_maximum_fusion.4.rest_12_) | copy-start | bytes 1572868
  23.5 3.3 %copy-start.29 = (bf16[8192,16]{0,1:T(8,128)(2,1)S(1)}, bf16[8192,16]{0,1:T(8,128)(2,1)}, u32[]{:S(2)}) copy-start(bf16[8192,16]{0,1:T(8,128)(2,1)} %param.17) | copy-start | bytes 786436
  23.6 27.7 %copy-start.5 = (bf16[4,2,256,128]{3,2,1,0:T(8,128)(2,1)}, bf16[4,2,256,128]{3,2,1,0:T(8,128)(2,1)S(1)}, u32[]{:S(2)}) copy-start(bf16[4,2,256,128]{3,2,1,0:T(8,128)(2,1)S(1)} %copy.37.rest_4_) | copy-start | bytes 1572868
  23.6 3.8 %copy-start.24 = (bf16[1,128,8192]{2,1,0:T(8,128)(2,1)S(1)}, bf16[1,128,8192]{2,1,0:T(8,128)(2,1)}, u32[]{:S(2)}) copy-start(bf16[1,128,8192]{2,1,0:T(8,128)(2,1)} %param.13) | copy-start | bytes 6291460
  23.6 3.8 %copy-start.25 = (bf16[16,8192]{1,0:T(8,128)(2,1)S(1)}, bf16[16,8192]{1,0:T(8,128)(2,1)}, u32[]{:S(2)}) copy-start(bf16[16,8192]{1,0:T(8,128)(2,1)} %param.18) | copy-start | bytes 786436
  23.7 12.7 %copy-start.7 = (bf16[4,2,256,128]{3,2,1,0:T(8,128)(2,1)}, bf16[4,2,256,128]{3,2,1,0:T(8,128)(2,1)S(1)}, u32[]{:S(2)}) copy-start(bf16[4,2,256,128]{3,2,1,0:T(8,128)(2,1)S(1)} %pad_maximum_fusion.3.rest_8_) | copy-start | bytes 1572868
  26.8 35.0 %copy-start.9 = (bf16[4,2,256,128]{3,2,1,0:T(8,128)(2,1)}, bf16[4,2,256,128]{3,2,1,0:T(8,128)(2,1)S(1)}, u32[]{:S(2)}) copy-start(bf16[4,2,256,128]{3,2,1,0:T(8,128)(2,1)S(1)} %pad_maximum_fusion.1.rest_0_) | copy-start | bytes 1572868
  27.4 1.6 copy-start.26
  29.0 1.3 copy-start.1
  30.4 48.9 %copy-start.32 = (s32[64]{0:T(128)S(1)}, s32[64]{0:T(128)}, u32[]{:S(2)}) copy-start(s32[64]{0:T(128)} %param.22) | copy-start | bytes 772
  31.9 60.9 %collective-permute-start.9 = (bf16[2,128,4096]{2,1,0:T(8,128)(2,1)}, bf16[2,128,4096]{2,1,0:T(8,128)(2,1)}, u32[]{:S(2)}, u32[]{:S(2)}) collective-permute-start(bf16[2,128,4096]{2,1,0:T(8,128)(2,1)} %pad_maximum_fusion), channel_id=1, source_target_pairs={{0,1},{1,0},{2,3},{3,2},{4,5},{5,4},{6,7},{7,6},{8,9},{9,8},{10,11... | collective-permute-start | bytes 6291464 | tf_op jit(solution)/shard_map/ppermute | solution.py:196
  34.9 13.5 %collective-permute-start.20 = (bf16[4,2,256,128]{3,2,1,0:T(8,128)(2,1)S(1)}, bf16[4,2,256,128]{3,2,1,0:T(8,128)(2,1)S(1)}, u32[]{:S(2)}, u32[]{:S(2)}) collective-permute-start(bf16[4,2,256,128]{3,2,1,0:T(8,128)(2,1)S(1)} %pad_maximum_fusion.4.rest_12_), channel_id=1, source_target_pairs={{0,6},{2,0},{4,2},{6,4},{1,7},{3,1},{5,3},{7,5},{8,14},{10,8},{12,... | collective-permute-start | bytes 1572872 | tf_op jit(solution)/shard_map/ppermute | solution.py:192
  36.0 15.3 %collective-permute-start.19 = (bf16[4,2,256,128]{3,2,1,0:T(8,128)(2,1)S(1)}, bf16[4,2,256,128]{3,2,1,0:T(8,128)(2,1)S(1)}, u32[]{:S(2)}, u32[]{:S(2)}) collective-permute-start(bf16[4,2,256,128]{3,2,1,0:T(8,128)(2,1)S(1)} %pad_maximum_fusion.4.rest_12_), channel_id=1, source_target_pairs={{0,2},{2,4},{4,6},{6,0},{1,3},{3,5},{5,7},{7,1},{8,10},{10,12},{12... | collective-permute-start | bytes 1572872 | tf_op jit(solution)/shard_map/ppermute | solution.py:192
  36.3 25.4 %collective-permute-start.16 = (bf16[4,2,256,128]{3,2,1,0:T(8,128)(2,1)S(1)}, bf16[4,2,256,128]{3,2,1,0:T(8,128)(2,1)S(1)}, u32[]{:S(2)}, u32[]{:S(2)}) collective-permute-start(bf16[4,2,256,128]{3,2,1,0:T(8,128)(2,1)S(1)} %pad_maximum_fusion.3.rest_8_), channel_id=1, source_target_pairs={{0,2},{2,4},{4,6},{6,0},{1,3},{3,5},{5,7},{7,1},{8,10},{10,12},{12... | collective-permute-start | bytes 1572872 | tf_op jit(solution)/shard_map/ppermute | solution.py:192
  36.4 25.4 %collective-permute-start.17 = (bf16[4,2,256,128]{3,2,1,0:T(8,128)(2,1)S(1)}, bf16[4,2,256,128]{3,2,1,0:T(8,128)(2,1)S(1)}, u32[]{:S(2)}, u32[]{:S(2)}) collective-permute-start(bf16[4,2,256,128]{3,2,1,0:T(8,128)(2,1)S(1)} %pad_maximum_fusion.3.rest_8_), channel_id=1, source_target_pairs={{0,6},{2,0},{4,2},{6,4},{1,7},{3,1},{5,3},{7,5},{8,14},{10,8},{12,... | collective-permute-start | bytes 1572872 | tf_op jit(solution)/shard_map/ppermute | solution.py:192
  48.4 13.4 %copy-start.13 = (bf16[4,2,256,128]{3,2,1,0:T(8,128)(2,1)}, bf16[4,2,256,128]{3,2,1,0:T(8,128)(2,1)S(1)}, u32[]{:S(2)}) copy-start(bf16[4,2,256,128]{3,2,1,0:T(8,128)(2,1)S(1)} %collective-permute-done.20.rest_14_) | copy-start | bytes 1572868
  48.4 18.8 %collective-permute-start.14 = (bf16[4,2,256,128]{3,2,1,0:T(8,128)(2,1)S(1)}, bf16[4,2,256,128]{3,2,1,0:T(8,128)(2,1)}, u32[]{:S(2)}, u32[]{:S(2)}) collective-permute-start(bf16[4,2,256,128]{3,2,1,0:T(8,128)(2,1)S(1)} %copy.37.rest_4_), channel_id=1, source_target_pairs={{0,24},{8,0},{16,8},{24,16},{1,25},{9,1},{17,9},{25,17},{2,26},{10... | collective-permute-start | bytes 1572872 | tf_op jit(solution)/shard_map/ppermute | solution.py:192
  52.1 15.2 %collective-permute-start.13 = (bf16[4,2,256,128]{3,2,1,0:T(8,128)(2,1)S(1)}, bf16[4,2,256,128]{3,2,1,0:T(8,128)(2,1)}, u32[]{:S(2)}, u32[]{:S(2)}) collective-permute-start(bf16[4,2,256,128]{3,2,1,0:T(8,128)(2,1)S(1)} %copy.37.rest_4_), channel_id=1, source_target_pairs={{0,8},{8,16},{16,24},{24,0},{1,9},{9,17},{17,25},{25,1},{2,10},{10... | collective-permute-start | bytes 1572872 | tf_op jit(solution)/shard_map/ppermute | solution.py:192
  61.8 15.5 %collective-permute-start.10 = (bf16[4,2,256,128]{3,2,1,0:T(8,128)(2,1)S(1)}, bf16[4,2,256,128]{3,2,1,0:T(8,128)(2,1)}, u32[]{:S(2)}, u32[]{:S(2)}) collective-permute-start(bf16[4,2,256,128]{3,2,1,0:T(8,128)(2,1)S(1)} %pad_maximum_fusion.1.rest_0_), channel_id=1, source_target_pairs={{0,8},{8,16},{16,24},{24,0},{1,9},{9,17},{17,25},{25,1},{2,10},{10... | collective-permute-start | bytes 1572872 | tf_op jit(solution)/shard_map/ppermute | solution.py:192
  63.4 15.3 %collective-permute-start.11 = (bf16[4,2,256,128]{3,2,1,0:T(8,128)(2,1)S(1)}, bf16[4,2,256,128]{3,2,1,0:T(8,128)(2,1)}, u32[]{:S(2)}, u32[]{:S(2)}) collective-permute-start(bf16[4,2,256,128]{3,2,1,0:T(8,128)(2,1)S(1)} %pad_maximum_fusion.1.rest_0_), channel_id=1, source_target_pairs={{0,24},{8,0},{16,8},{24,16},{1,25},{9,1},{17,9},{25,17},{2,26},{10... | collective-permute-start | bytes 1572872 | tf_op jit(solution)/shard_map/ppermute | solution.py:192
  67.2 12.6 %collective-permute-start.21 = (bf16[4,2,256,128]{3,2,1,0:T(8,128)(2,1)}, bf16[4,2,256,128]{3,2,1,0:T(8,128)(2,1)}, u32[]{:S(2)}, u32[]{:S(2)}) collective-permute-start(bf16[4,2,256,128]{3,2,1,0:T(8,128)(2,1)} %copy-done.13), channel_id=1, source_target_pairs={{0,6},{2,0},{4,2},{6,4},{1,7},{3,1},{5,3},{7,5},{8,14},{10,8},{12,... | collective-permute-start | bytes 1572872 | tf_op jit(solution)/shard_map/ppermute | solution.py:192
  67.3 14.6 %collective-permute-start.18 = (bf16[4,2,256,128]{3,2,1,0:T(8,128)(2,1)}, bf16[4,2,256,128]{3,2,1,0:T(8,128)(2,1)}, u32[]{:S(2)}, u32[]{:S(2)}) collective-permute-start(bf16[4,2,256,128]{3,2,1,0:T(8,128)(2,1)} %copy-done.17), channel_id=1, source_target_pairs={{0,2},{2,4},{4,6},{6,0},{1,3},{3,5},{5,7},{7,1},{8,10},{10,12},{12... | collective-permute-start | bytes 1572872 | tf_op jit(solution)/shard_map/ppermute | solution.py:192
  77.3 12.1 %collective-permute-start.15 = (bf16[4,2,256,128]{3,2,1,0:T(8,128)(2,1)}, bf16[4,2,256,128]{3,2,1,0:T(8,128)(2,1)}, u32[]{:S(2)}, u32[]{:S(2)}) collective-permute-start(bf16[4,2,256,128]{3,2,1,0:T(8,128)(2,1)} %collective-permute-done.14.rest_6_), channel_id=1, source_target_pairs={{0,24},{8,0},{16,8},{24,16},{1,25},{9,1},{17,9},{25,17},{2,26},{10... | collective-permute-start | bytes 1572872 | tf_op jit(solution)/shard_map/ppermute | solution.py:192
  78.6 13.4 %collective-permute-start.12 = (bf16[4,2,256,128]{3,2,1,0:T(8,128)(2,1)}, bf16[4,2,256,128]{3,2,1,0:T(8,128)(2,1)S(1)}, u32[]{:S(2)}, u32[]{:S(2)}) collective-permute-start(bf16[4,2,256,128]{3,2,1,0:T(8,128)(2,1)} %collective-permute-done.10.rest_1_), channel_id=1, source_target_pairs={{0,8},{8,16},{16,24},{24,0},{1,9},{9,17},{17,25},{25,1},{2,10},{10... | collective-permute-start | bytes 1572872 | tf_op jit(solution)/shard_map/ppermute | solution.py:192
  79.8 85.9 %collective-permute-start.23 = (bf16[128,16]{0,1:T(8,128)(2,1)S(1)}, bf16[128,16]{0,1:T(8,128)(2,1)S(1)}, u32[]{:S(2)}, u32[]{:S(2)}) collective-permute-start(bf16[128,16]{0,1:T(8,128)(2,1)S(1)} %convolution_convert_fusion), channel_id=1, source_target_pairs={{0,1},{1,0},{2,3},{3,2},{4,5},{5,4},{6,7},{7,6},{8,9},{9,8},{10,11... | collective-permute-start | bytes 12296 | tf_op jit(solution)/shard_map/ppermute | solution.py:196
  92.8 1.6 copy-start.2
  94.4 1.0 copy-start.4
  95.5 1.0 copy-start.6
  96.5 1.0 copy-start.8
  97.6 1.0 copy-start.10
  98.6 1.0 copy-start.14
  156.0 10.6 %copy-start.11 = (bf16[128,4096]{1,0:T(8,128)(2,1)}, bf16[128,4096]{1,0:T(8,128)(2,1)S(1)}, u32[]{:S(2)}) copy-start(bf16[128,4096]{1,0:T(8,128)(2,1)S(1)} %get-tuple-element.14) | copy-start | bytes 3145732
  156.4 10.2 %collective-permute-start.24 = (f32[128,16]{0,1:T(8,128)S(1)}, f32[128,16]{0,1:T(8,128)S(1)}, u32[]{:S(2)}, u32[]{:S(2)}) collective-permute-start(f32[128,16]{0,1:T(8,128)S(1)} %fusion.21), channel_id=1, source_target_pairs={{0,1},{1,0},{2,3},{3,2},{4,5},{5,4},{6,7},{7,6},{8,9},{9,8},{10,11... | collective-permute-start | bytes 24584 | tf_op jit(solution)/shard_map/ppermute | solution.py:196
  169.2 1.5 collective-permute-start.25
  170.6 1.1 copy-start.23
  172.4 31.9 %copy-start.12 = (bf16[128,4096]{1,0:T(8,128)(2,1)S(1)}, bf16[128,4096]{1,0:T(8,128)(2,1)}, u32[]{:S(2)}) copy-start(bf16[128,4096]{1,0:T(8,128)(2,1)} %copy-done.11) | copy-start | bytes 3145732
  172.4 6.7 %collective-permute-start.26 = (bf16[32,1024]{1,0:T(8,128)(2,1)}, bf16[32,1024]{1,0:T(8,128)(2,1)}, u32[]{:S(2)}, u32[]{:S(2)}) collective-permute-start(bf16[32,1024]{1,0:T(8,128)(2,1)} %get-tuple-element.25), channel_id=1, source_target_pairs={{0,2},{2,4},{4,6},{6,0},{1,3},{3,5},{5,7},{7,1},{8,10},{10,12},{12... | collective-permute-start | bytes 196616 | tf_op jit(solution)/shard_map/ppermute | solution.py:192
  172.4 6.7 %collective-permute-start.27 = (bf16[32,1024]{1,0:T(8,128)(2,1)S(1)}, bf16[32,1024]{1,0:T(8,128)(2,1)}, u32[]{:S(2)}, u32[]{:S(2)}) collective-permute-start(bf16[32,1024]{1,0:T(8,128)(2,1)S(1)} %get-tuple-element.26), channel_id=1, source_target_pairs={{0,4},{2,6},{4,0},{6,2},{1,5},{3,7},{5,1},{7,3},{8,12},{10,14},{12... | collective-permute-start | bytes 196616 | tf_op jit(solution)/shard_map/ppermute | solution.py:192
  173.9 5.2 %collective-permute-start.28 = (bf16[32,1024]{1,0:T(8,128)(2,1)S(1)}, bf16[32,1024]{1,0:T(8,128)(2,1)}, u32[]{:S(2)}, u32[]{:S(2)}) collective-permute-start(bf16[32,1024]{1,0:T(8,128)(2,1)S(1)} %get-tuple-element.27), channel_id=1, source_target_pairs={{0,6},{2,0},{4,2},{6,4},{1,7},{3,1},{5,3},{7,5},{8,14},{10,8},{12,... | collective-permute-start | bytes 196616 | tf_op jit(solution)/shard_map/ppermute | solution.py:192
  180.1 4.8 %collective-permute-start.29 = (bf16[32,1024]{1,0:T(8,128)(2,1)S(1)}, bf16[32,1024]{1,0:T(8,128)(2,1)S(1)}, u32[]{:S(2)}, u32[]{:S(2)}) collective-permute-start(bf16[32,1024]{1,0:T(8,128)(2,1)S(1)} %fusion.16), channel_id=1, source_target_pairs={{0,16},{8,24},{16,0},{24,8},{1,17},{9,25},{17,1},{25,9},{2,18},{10... | collective-permute-start | bytes 196616 | tf_op jit(solution)/shard_map/ppermute | solution.py:192
  180.2 5.1 %collective-permute-start.30 = (bf16[32,1024]{1,0:T(8,128)(2,1)S(1)}, bf16[32,1024]{1,0:T(8,128)(2,1)S(1)}, u32[]{:S(2)}, u32[]{:S(2)}) collective-permute-start(bf16[32,1024]{1,0:T(8,128)(2,1)S(1)} %fusion.16), channel_id=1, source_target_pairs={{0,8},{8,16},{16,24},{24,0},{1,9},{9,17},{17,25},{25,1},{2,10},{10... | collective-permute-start | bytes 196616 | tf_op jit(solution)/shard_map/ppermute | solution.py:192
  181.2 4.1 %collective-permute-start.31 = (bf16[32,1024]{1,0:T(8,128)(2,1)S(1)}, bf16[32,1024]{1,0:T(8,128)(2,1)S(1)}, u32[]{:S(2)}, u32[]{:S(2)}) collective-permute-start(bf16[32,1024]{1,0:T(8,128)(2,1)S(1)} %fusion.16), channel_id=1, source_target_pairs={{0,24},{8,0},{16,8},{24,16},{1,25},{9,1},{17,9},{25,17},{2,26},{10... | collective-permute-start | bytes 196616 | tf_op jit(solution)/shard_map/ppermute | solution.py:192
  185.3 5.5 %collective-permute-start.32 = (bf16[32,1024]{1,0:T(8,128)(2,1)S(1)}, bf16[32,1024]{1,0:T(8,128)(2,1)S(1)}, u32[]{:S(2)}, u32[]{:S(2)}) collective-permute-start(bf16[32,1024]{1,0:T(8,128)(2,1)S(1)} %add_convert_fusion.1), channel_id=1, source_target_pairs={{0,64},{32,96},{64,0},{96,32},{1,65},{33,97},{65,1},{97,33},{2,66}... | collective-permute-start | bytes 196616 | tf_op jit(solution)/shard_map/ppermute | solution.py:192
  188.2 5.0 %collective-permute-start.33 = (bf16[32,1024]{1,0:T(8,128)(2,1)S(1)}, bf16[32,1024]{1,0:T(8,128)(2,1)S(1)}, u32[]{:S(2)}, u32[]{:S(2)}) collective-permute-start(bf16[32,1024]{1,0:T(8,128)(2,1)S(1)} %add_convert_fusion.1), channel_id=1, source_target_pairs={{0,32},{32,64},{64,96},{96,0},{1,33},{33,65},{65,97},{97,1},{2,34}... | collective-permute-start | bytes 196616 | tf_op jit(solution)/shard_map/ppermute | solution.py:192
  188.5 4.7 %collective-permute-start.34 = (bf16[32,1024]{1,0:T(8,128)(2,1)S(1)}, bf16[32,1024]{1,0:T(8,128)(2,1)S(1)}, u32[]{:S(2)}, u32[]{:S(2)}) collective-permute-start(bf16[32,1024]{1,0:T(8,128)(2,1)S(1)} %add_convert_fusion.1), channel_id=1, source_target_pairs={{0,96},{32,0},{64,32},{96,64},{1,97},{33,1},{65,33},{97,65},{2,98}... | collective-permute-start | bytes 196616 | tf_op jit(solution)/shard_map/ppermute | solution.py:192
  193.3 4.7 %collective-permute-start.35 = (bf16[32,1024]{1,0:T(8,128)(2,1)S(1)}, bf16[32,1024]{1,0:T(8,128)(2,1)S(1)}, u32[]{:S(2)}, u32[]{:S(2)}) collective-permute-start(bf16[32,1024]{1,0:T(8,128)(2,1)S(1)} %add_convert_fusion), channel_id=1, source_target_pairs={{0,4},{2,6},{4,0},{6,2},{1,5},{3,7},{5,1},{7,3},{8,12},{10,14},{12... | collective-permute-start | bytes 196616 | tf_op jit(solution)/shard_map/ppermute | solution.py:192
  194.0 4.6 %collective-permute-start.36 = (bf16[32,1024]{1,0:T(8,128)(2,1)S(1)}, bf16[32,1024]{1,0:T(8,128)(2,1)S(1)}, u32[]{:S(2)}, u32[]{:S(2)}) collective-permute-start(bf16[32,1024]{1,0:T(8,128)(2,1)S(1)} %add_convert_fusion), channel_id=1, source_target_pairs={{0,2},{2,4},{4,6},{6,0},{1,3},{3,5},{5,7},{7,1},{8,10},{10,12},{12... | collective-permute-start | bytes 196616 | tf_op jit(solution)/shard_map/ppermute | solution.py:192
  196.7 3.1 %collective-permute-start.37 = (bf16[32,1024]{1,0:T(8,128)(2,1)S(1)}, bf16[32,1024]{1,0:T(8,128)(2,1)S(1)}, u32[]{:S(2)}, u32[]{:S(2)}) collective-permute-start(bf16[32,1024]{1,0:T(8,128)(2,1)S(1)} %add_convert_fusion), channel_id=1, source_target_pairs={{0,6},{2,0},{4,2},{6,4},{1,7},{3,1},{5,3},{7,5},{8,14},{10,8},{12,... | collective-permute-start | bytes 196616 | tf_op jit(solution)/shard_map/ppermute | solution.py:192
  199.9 5.7 %copy-start.27 = (f32[16,8192]{1,0:T(8,128)S(1)}, f32[16,8192]{1,0:T(8,128)}, u32[]{:S(2)}) copy-start(f32[16,8192]{1,0:T(8,128)} %param.20) | copy-start | bytes 1572868
  200.0 5.4 %collective-permute-start.38 = (bf16[32,4096]{1,0:T(8,128)(2,1)S(1)}, bf16[32,4096]{1,0:T(8,128)(2,1)S(1)}, u32[]{:S(2)}, u32[]{:S(2)}) collective-permute-start(bf16[32,4096]{1,0:T(8,128)(2,1)S(1)} %pad_maximum_fusion.7), channel_id=1, source_target_pairs={{0,1},{1,0},{2,3},{3,2},{4,5},{5,4},{6,7},{7,6},{8,9},{9,8},{10,11... | collective-permute-start | bytes 786440 | tf_op jit(solution)/shard_map/ppermute | solution.py:196
  204.3 3.1 %collective-permute-start.22 = (bf16[128,4096]{1,0:T(8,128)(2,1)S(1)}, bf16[128,4096]{1,0:T(8,128)(2,1)S(1)}, u32[]{:S(2)}, u32[]{:S(2)}) collective-permute-start(bf16[128,4096]{1,0:T(8,128)(2,1)S(1)} %copy-done.12), channel_id=1, source_target_pairs={{0,1},{1,0},{2,3},{3,2},{4,5},{5,4},{6,7},{7,6},{8,9},{9,8},{10,11... | collective-permute-start | bytes 3145736 | tf_op jit(solution)/shard_map/ppermute | solution.py:196
  205.5 1.0 copy-start.28
  205.7 1.8 copy-start.30
  207.6 1.3 copy-start.31
  (8 other events, 7.4 us)

commit v5 on v4

--- a/solution.py
+++ b/solution.py
@@ -179,7 +179,7 @@
             ],
         ),
         compiler_params=pltpu.CompilerParams(
-            dimension_semantics=("arbitrary",), vmem_limit_bytes=40 << 20
+            dimension_semantics=("arbitrary",), vmem_limit_bytes=42 << 20
         ),
         cost_estimate=pl.CostEstimate(
             flops=64 * 8 * 8 * D * D * D, bytes_accessed=16 << 20, transcendentals=64 * 8 * D * D
@@ -247,9 +247,12 @@
     chip = y * 4 + z
     half = HEADS * D
 
-    kv = jnp.stack([keys, values])
-    mine = lax.dynamic_slice_in_dim(kv, core * 512, 512, 2)
-    far = swap(lax.dynamic_slice_in_dim(kv, (1 - core) * 512, 512, 2))
+    def half_of(which):
+        return jnp.stack(
+            [lax.dynamic_slice_in_dim(t, which * 512, 512, 1) for t in (keys, values)]
+        )
+
+    mine, far = half_of(core), swap(half_of(1 - core))
     kv = jnp.where(core == 0, jnp.concatenate([mine, far], 1), jnp.concatenate([far, mine], 1))
     heads = [jnp.stack([kv[:, :, i * D : (i + 1) * D] for i in (j, j + 1)], axis=1) for j in (0, 2)]
     ring_a = ring_gather(heads[0], "z", "y")

time: 210 us -> 207 us (0.986)
    unnamed x72 -> x69, local copies, waits for them, and re-layouts: 18.8 us -> 17 us
where the time goes in v5:
time: 207 us
  starting transfers between devices  62.1 us (30%)
  waiting for transfers between devices  58.1 us (28%)
  Pallas kernels  51.3 us (25%)
  local copies, waits for them, and re-layouts  20.9 us (10%)
  other arithmetic  7.23 us (3%)
  matrix products  5.47 us (3%)
    ppermute x32, waiting for transfers between devices, hop(): return lax.ppermute(x, axis, [(i, (i + by) % 4) for i in range(4)])  55.9 us
    pallas_call x1, Pallas kernels, attention(): pl.pallas_call(functools.partial(attention_kernel, len(srcs), copies), ou...  51.3 us
    ppermute x32, starting transfers between devices, hop(): return lax.ppermute(x, axis, [(i, (i + by) % 4) for i in range(4)])  41.6 us
    ppermute x7, starting transfers between devices, swap(): return lax.ppermute(x, 'core', [(0, 1), (1, 0)])  20.5 us
    unnamed x69, local copies, waits for them, and re-layouts  17 us
  transfers between devices with their start and end apart: 39, of which 18 were waited for; matrix products, arithmetic and copies ran while one was open for 3% of the time, Pallas kernels for 25%

profile of v5, /device:TPU:1, one launch (start us, length us, event | category | flops | bytes accessed | tf_op | source)
XLA Modules:
  0.0 206.5 jit_solution(9170909484634396181)
XLA Ops:
  0.7 1.3 constant_dynamic-slice_fusion.2
  2.0 1.5 collective-permute-start
  3.4 1.2 collective-permute-done
  4.9 2.9 %collective-permute-start.6 = (bf16[2,2,256,128]{3,2,1,0:T(8,128)(2,1)S(1)}, bf16[2,2,256,128]{3,2,1,0:T(8,128)(2,1)S(1)}, u32[]{:S(2)}, u32[]{:S(2)}) collective-permute-start(bf16[2,2,256,128]{3,2,1,0:T(8,128)(2,1)S(1)} %pad_maximum_fusion.5), channel_id=1, source_target_pairs={{0,24},{8,0},{16,8},{24,16},{1,25},{9,1},{17,9},{25,17},{2,26},{10... | collective-permute-start | bytes 786440 | tf_op jit(solution)/shard_map/ppermute | solution.py:192
  8.0 3.8 %collective-permute-start.2 = (bf16[2,2,256,128]{3,2,1,0:T(8,128)(2,1)S(1)}, bf16[2,2,256,128]{3,2,1,0:T(8,128)(2,1)S(1)}, u32[]{:S(2)}, u32[]{:S(2)}) collective-permute-start(bf16[2,2,256,128]{3,2,1,0:T(8,128)(2,1)S(1)} %copy.32), channel_id=1, source_target_pairs={{0,6},{2,0},{4,2},{6,4},{1,7},{3,1},{5,3},{7,5},{8,14},{10,8},{12,... | collective-permute-start | bytes 786440 | tf_op jit(solution)/shard_map/ppermute | solution.py:192
  11.8 1.3 collective-permute-done.6
  13.2 3.5 %collective-permute-start.8 = (bf16[2,256,128]{2,1,0:T(8,128)(2,1)S(1)}, bf16[2,256,128]{2,1,0:T(8,128)(2,1)S(1)}, u32[]{:S(2)}, u32[]{:S(2)}) collective-permute-start(bf16[2,256,128]{2,1,0:T(8,128)(2,1)S(1)} %get-tuple-element.40), channel_id=1, source_target_pairs={{0,24},{8,0},{16,8},{24,16},{1,25},{9,1},{17,9},{25,17},{2,26},{10... | collective-permute-start | bytes 393224 | tf_op jit(solution)/shard_map/ppermute | solution.py:192
  16.9 3.8 %collective-permute-start.4 = (bf16[2,256,128]{2,1,0:T(8,128)(2,1)S(1)}, bf16[2,256,128]{2,1,0:T(8,128)(2,1)S(1)}, u32[]{:S(2)}, u32[]{:S(2)}) collective-permute-start(bf16[2,256,128]{2,1,0:T(8,128)(2,1)S(1)} %get-tuple-element.46), channel_id=1, source_target_pairs={{0,6},{2,0},{4,2},{6,4},{1,7},{3,1},{5,3},{7,5},{8,14},{10,8},{12,... | collective-permute-start | bytes 393224 | tf_op jit(solution)/shard_map/ppermute | solution.py:192
  20.9 1.7 collective-permute-done.4
  22.9 3.0 %collective-permute-done.3 = bf16[2,256,128]{2,1,0:T(8,128)(2,1)S(1)} collective-permute-done((bf16[2,256,128]{2,1,0:T(8,128)(2,1)S(1)}, bf16[2,256,128]{2,1,0:T(8,128)(2,1)S(1)}, u32[]{:S(2)}, u32[]{:S(2)}) %collective-permute-start.3) | collective-permute-done | bytes 131104 | tf_op jit(solution)/shard_map/ppermute | solution.py:192
  27.4 1.3 copy-done.21
  28.8 1.5 copy-done.27
  30.4 1.5 pad_maximum_fusion
  31.9 2.9 %collective-permute-start.9 = (bf16[2,128,4096]{2,1,0:T(8,128)(2,1)}, bf16[2,128,4096]{2,1,0:T(8,128)(2,1)}, u32[]{:S(2)}, u32[]{:S(2)}) collective-permute-start(bf16[2,128,4096]{2,1,0:T(8,128)(2,1)} %pad_maximum_fusion), channel_id=1, source_target_pairs={{0,1},{1,0},{2,3},{3,2},{4,5},{5,4},{6,7},{7,6},{8,9},{9,8},{10,11... | collective-permute-start | bytes 6291464 | tf_op jit(solution)/shard_map/ppermute | solution.py:196
  34.8 1.1 collective-permute-start.20
  36.3 2.7 %collective-permute-start.17 = (bf16[4,2,256,128]{3,2,1,0:T(8,128)(2,1)S(1)}, bf16[4,2,256,128]{3,2,1,0:T(8,128)(2,1)S(1)}, u32[]{:S(2)}, u32[]{:S(2)}) collective-permute-start(bf16[4,2,256,128]{3,2,1,0:T(8,128)(2,1)S(1)} %pad_maximum_fusion.3.rest_8_), channel_id=1, source_target_pairs={{0,6},{2,0},{4,2},{6,4},{1,7},{3,1},{5,3},{7,5},{8,14},{10,8},{12,... | collective-permute-start | bytes 1572872 | tf_op jit(solution)/shard_map/ppermute | solution.py:192
  39.0 9.3 %collective-permute-done.20.rest_14_ = bf16[4,2,256,128]{3,2,1,0:T(8,128)(2,1)S(1)} collective-permute-done((bf16[4,2,256,128]{3,2,1,0:T(8,128)(2,1)S(1)}, bf16[4,2,256,128]{3,2,1,0:T(8,128)(2,1)S(1)}, u32[]{:S(2)}, u32[]{:S(2)}) %collective-permute-start.20) | collective-permute-done | bytes 524320 | tf_op jit(solution)/shard_map/ppermute | solution.py:192
  48.3 2.9 %collective-permute-start.14 = (bf16[4,2,256,128]{3,2,1,0:T(8,128)(2,1)S(1)}, bf16[4,2,256,128]{3,2,1,0:T(8,128)(2,1)}, u32[]{:S(2)}, u32[]{:S(2)}) collective-permute-start(bf16[4,2,256,128]{3,2,1,0:T(8,128)(2,1)S(1)} %copy.37.rest_4_), channel_id=1, source_target_pairs={{0,24},{8,0},{16,8},{24,16},{1,25},{9,1},{17,9},{25,17},{2,26},{10... | collective-permute-start | bytes 1572872 | tf_op jit(solution)/shard_map/ppermute | solution.py:192
  51.3 0.8 copy-done.13
  52.1 9.7 %collective-permute-done.16.rest_9_ = bf16[4,2,256,128]{3,2,1,0:T(8,128)(2,1)S(1)} collective-permute-done((bf16[4,2,256,128]{3,2,1,0:T(8,128)(2,1)S(1)}, bf16[4,2,256,128]{3,2,1,0:T(8,128)(2,1)S(1)}, u32[]{:S(2)}, u32[]{:S(2)}) %collective-permute-start.16) | collective-permute-done | bytes 524320 | tf_op jit(solution)/shard_map/ppermute | solution.py:192
  62.5 0.8 copy-done.17
  63.4 2.9 %collective-permute-start.11 = (bf16[4,2,256,128]{3,2,1,0:T(8,128)(2,1)S(1)}, bf16[4,2,256,128]{3,2,1,0:T(8,128)(2,1)}, u32[]{:S(2)}, u32[]{:S(2)}) collective-permute-start(bf16[4,2,256,128]{3,2,1,0:T(8,128)(2,1)S(1)} %pad_maximum_fusion.1.rest_0_), channel_id=1, source_target_pairs={{0,24},{8,0},{16,8},{24,16},{1,25},{9,1},{17,9},{25,17},{2,26},{10... | collective-permute-start | bytes 1572872 | tf_op jit(solution)/shard_map/ppermute | solution.py:192
  66.3 0.9 constant_dynamic-slice_fusion.4
  67.3 1.4 collective-permute-start.18
  68.7 8.5 %collective-permute-done.10.rest_1_ = bf16[4,2,256,128]{3,2,1,0:T(8,128)(2,1)} collective-permute-done((bf16[4,2,256,128]{3,2,1,0:T(8,128)(2,1)S(1)}, bf16[4,2,256,128]{3,2,1,0:T(8,128)(2,1)}, u32[]{:S(2)}, u32[]{:S(2)}) %collective-permute-start.10) | collective-permute-done | bytes 524320 | tf_op jit(solution)/shard_map/ppermute | solution.py:192
  77.2 1.4 collective-permute-start.15
  79.7 2.2 %collective-permute-start.23 = (bf16[128,16]{0,1:T(8,128)(2,1)S(1)}, bf16[128,16]{0,1:T(8,128)(2,1)S(1)}, u32[]{:S(2)}, u32[]{:S(2)}) collective-permute-start(bf16[128,16]{0,1:T(8,128)(2,1)S(1)} %convolution_convert_fusion), channel_id=1, source_target_pairs={{0,1},{1,0},{2,3},{3,2},{4,5},{5,4},{6,7},{7,6},{8,9},{9,8},{10,11... | collective-permute-start | bytes 12296 | tf_op jit(solution)/shard_map/ppermute | solution.py:196
  81.9 7.4 %collective-permute-done.15.rest_7_ = bf16[4,2,256,128]{3,2,1,0:T(8,128)(2,1)} collective-permute-done((bf16[4,2,256,128]{3,2,1,0:T(8,128)(2,1)}, bf16[4,2,256,128]{3,2,1,0:T(8,128)(2,1)}, u32[]{:S(2)}, u32[]{:S(2)}) %collective-permute-start.15) | collective-permute-done | bytes 524320 | tf_op jit(solution)/shard_map/ppermute | solution.py:192
  89.4 2.7 %collective-permute-done.12.rest_3_ = bf16[4,2,256,128]{3,2,1,0:T(8,128)(2,1)S(1)} collective-permute-done((bf16[4,2,256,128]{3,2,1,0:T(8,128)(2,1)}, bf16[4,2,256,128]{3,2,1,0:T(8,128)(2,1)S(1)}, u32[]{:S(2)}, u32[]{:S(2)}) %collective-permute-start.12) | collective-permute-done | bytes 524320 | tf_op jit(solution)/shard_map/ppermute | solution.py:192
  92.0 0.8 copy-done.19
  92.8 1.0 copy-done.2
  93.9 1.0 copy-done.4
  94.9 1.0 copy-done.6
  96.0 1.0 copy-done.8
  97.0 1.0 copy-done.12
  98.1 1.0 copy-done.14
  99.1 1.0 copy-done.16
  100.1 1.0 copy-done.18
  101.2 1.0 copy-done.20
  102.2 51.3 %attend.1 = (bf16[128,8192]{1,0:T(8,128)(2,1)}, bf16[128,4096]{1,0:T(8,128)(2,1)S(1)}, bf16[128,4096]{1,0:T(8,128)(2,1)S(1)}, bf16[128,4096]{1,0:T(8,128)(2,1)S(1)}) custom-call(s32[768]{0:T(1024)S(1)} %reshape.19.lists, s32[32]{0:T(128)S(1)} %dynamic_slice.46.live, s32[2]{0:T(128)S(1)} %pad_add_fusion.1.off, bf16[128,8192]{1,0:T(8,128)(2,1)} %copy-done.21, ...), custom_call_target="tpu_custom_call" | custom-call | flops 8589934592 | bytes 16777216 | tf_op jit(solution)/shard_map/attend/pallas_call | solution.py:163
  154.0 9.3 %collective-permute-start.24 = (f32[128,16]{0,1:T(8,128)S(1)}, f32[128,16]{0,1:T(8,128)S(1)}, u32[]{:S(2)}, u32[]{:S(2)}) collective-permute-start(f32[128,16]{0,1:T(8,128)S(1)} %fusion.21), channel_id=1, source_target_pairs={{0,1},{1,0},{2,3},{3,2},{4,5},{5,4},{6,7},{7,6},{8,9},{9,8},{10,11... | collective-permute-start | bytes 24584 | tf_op jit(solution)/shard_map/ppermute | solution.py:196
  163.2 1.0 fusion.41
  164.2 1.6 fusion.5
  165.8 1.0 dynamic-slice_convert_fusion
  167.0 1.2 fusion.2
  168.2 1.1 convert_add_fusion
  170.0 1.5 collective-permute-start.27
  171.4 1.2 collective-permute-start.28
  172.7 4.0 %collective-permute-done.26 = bf16[32,1024]{1,0:T(8,128)(2,1)} collective-permute-done((bf16[32,1024]{1,0:T(8,128)(2,1)}, bf16[32,1024]{1,0:T(8,128)(2,1)}, u32[]{:S(2)}, u32[]{:S(2)}) %collective-permute-start.26) | collective-permute-done | bytes 65568 | tf_op jit(solution)/shard_map/ppermute | solution.py:192
  176.7 1.0 fusion.16
  177.8 1.0 collective-permute-start.30
  178.8 1.7 collective-permute-start.31
  180.5 2.0 collective-permute-done.29
  182.9 2.8 %collective-permute-start.32 = (bf16[32,1024]{1,0:T(8,128)(2,1)S(1)}, bf16[32,1024]{1,0:T(8,128)(2,1)S(1)}, u32[]{:S(2)}, u32[]{:S(2)}) collective-permute-start(bf16[32,1024]{1,0:T(8,128)(2,1)S(1)} %add_convert_fusion.1), channel_id=1, source_target_pairs={{0,64},{32,96},{64,0},{96,32},{1,65},{33,97},{65,1},{97,33},{2,66}... | collective-permute-start | bytes 196616 | tf_op jit(solution)/shard_map/ppermute | solution.py:192
  186.1 2.4 %collective-permute-start.34 = (bf16[32,1024]{1,0:T(8,128)(2,1)S(1)}, bf16[32,1024]{1,0:T(8,128)(2,1)S(1)}, u32[]{:S(2)}, u32[]{:S(2)}) collective-permute-start(bf16[32,1024]{1,0:T(8,128)(2,1)S(1)} %add_convert_fusion.1), channel_id=1, source_target_pairs={{0,96},{32,0},{64,32},{96,64},{1,97},{33,1},{65,33},{97,65},{2,98}... | collective-permute-start | bytes 196616 | tf_op jit(solution)/shard_map/ppermute | solution.py:192
  188.4 2.3 %collective-permute-done.33 = bf16[32,1024]{1,0:T(8,128)(2,1)S(1)} collective-permute-done((bf16[32,1024]{1,0:T(8,128)(2,1)S(1)}, bf16[32,1024]{1,0:T(8,128)(2,1)S(1)}, u32[]{:S(2)}, u32[]{:S(2)}) %collective-permute-start.33) | collective-permute-done | bytes 65568 | tf_op jit(solution)/shard_map/ppermute | solution.py:192
  191.6 2.7 %collective-permute-start.36 = (bf16[32,1024]{1,0:T(8,128)(2,1)S(1)}, bf16[32,1024]{1,0:T(8,128)(2,1)S(1)}, u32[]{:S(2)}, u32[]{:S(2)}) collective-permute-start(bf16[32,1024]{1,0:T(8,128)(2,1)S(1)} %add_convert_fusion), channel_id=1, source_target_pairs={{0,2},{2,4},{4,6},{6,0},{1,3},{3,5},{5,7},{7,1},{8,10},{10,12},{12... | collective-permute-start | bytes 196616 | tf_op jit(solution)/shard_map/ppermute | solution.py:192
  194.3 1.3 collective-permute-done.35
  196.3 1.1 collective-permute-done.37
  197.6 4.3 %collective-permute-start.38 = (bf16[32,4096]{1,0:T(8,128)(2,1)S(1)}, bf16[32,4096]{1,0:T(8,128)(2,1)S(1)}, u32[]{:S(2)}, u32[]{:S(2)}) collective-permute-start(bf16[32,4096]{1,0:T(8,128)(2,1)S(1)} %pad_maximum_fusion.8), channel_id=1, source_target_pairs={{0,1},{1,0},{2,3},{3,2},{4,5},{5,4},{6,7},{7,6},{8,9},{9,8},{10,11... | collective-permute-start | bytes 786440 | tf_op jit(solution)/shard_map/ppermute | solution.py:196
  202.0 1.1 collective-permute-done.38
  203.3 0.8 fusion.6
  204.1 0.8 fusion.8
  205.2 1.3 copy-done.30
  (136 shorter events, 9.3 us)
Async XLA Ops:
  0.6 25.3 %copy-start = (bf16[1,128,8192]{2,1,0:T(8,128)(2,1)S(1)}, bf16[1,128,8192]{2,1,0:T(8,128)(2,1)}, u32[]{:S(2)}) copy-start(bf16[1,128,8192]{2,1,0:T(8,128)(2,1)} %param.12) | copy-start | bytes 6291460
  2.0 2.6 %collective-permute-start = (bf16[2,128,512]{2,1,0:T(8,128)(2,1)S(1)}, bf16[2,128,512]{2,1,0:T(8,128)(2,1)S(1)}, u32[]{:S(2)}, u32[]{:S(2)}) collective-permute-start(bf16[2,128,512]{2,1,0:T(8,128)(2,1)S(1)} %pad_maximum_fusion.7), channel_id=1, source_target_pairs={{0,1},{1,0},{2,3},{3,2},{4,5},{5,4},{6,7},{7,6},{8,9},{9,8},{10,11... | collective-permute-start | bytes 786440 | tf_op jit(solution)/shard_map/ppermute | solution.py:196
  4.9 8.2 %collective-permute-start.6 = (bf16[2,2,256,128]{3,2,1,0:T(8,128)(2,1)S(1)}, bf16[2,2,256,128]{3,2,1,0:T(8,128)(2,1)S(1)}, u32[]{:S(2)}, u32[]{:S(2)}) collective-permute-start(bf16[2,2,256,128]{3,2,1,0:T(8,128)(2,1)S(1)} %pad_maximum_fusion.5), channel_id=1, source_target_pairs={{0,24},{8,0},{16,8},{24,16},{1,25},{9,1},{17,9},{25,17},{2,26},{10... | collective-permute-start | bytes 786440 | tf_op jit(solution)/shard_map/ppermute | solution.py:192
  7.9 8.8 %collective-permute-start.5 = (bf16[2,2,256,128]{3,2,1,0:T(8,128)(2,1)S(1)}, bf16[2,2,256,128]{3,2,1,0:T(8,128)(2,1)S(1)}, u32[]{:S(2)}, u32[]{:S(2)}) collective-permute-start(bf16[2,2,256,128]{3,2,1,0:T(8,128)(2,1)S(1)} %pad_maximum_fusion.5), channel_id=1, source_target_pairs={{0,8},{8,16},{16,24},{24,0},{1,9},{9,17},{17,25},{25,1},{2,10},{10... | collective-permute-start | bytes 786440 | tf_op jit(solution)/shard_map/ppermute | solution.py:192
  8.0 8.8 %collective-permute-start.2 = (bf16[2,2,256,128]{3,2,1,0:T(8,128)(2,1)S(1)}, bf16[2,2,256,128]{3,2,1,0:T(8,128)(2,1)S(1)}, u32[]{:S(2)}, u32[]{:S(2)}) collective-permute-start(bf16[2,2,256,128]{3,2,1,0:T(8,128)(2,1)S(1)} %copy.32), channel_id=1, source_target_pairs={{0,6},{2,0},{4,2},{6,4},{1,7},{3,1},{5,3},{7,5},{8,14},{10,8},{12,... | collective-permute-start | bytes 786440 | tf_op jit(solution)/shard_map/ppermute | solution.py:192
  11.8 8.9 %collective-permute-start.1 = (bf16[2,2,256,128]{3,2,1,0:T(8,128)(2,1)S(1)}, bf16[2,2,256,128]{3,2,1,0:T(8,128)(2,1)S(1)}, u32[]{:S(2)}, u32[]{:S(2)}) collective-permute-start(bf16[2,2,256,128]{3,2,1,0:T(8,128)(2,1)S(1)} %copy.32), channel_id=1, source_target_pairs={{0,2},{2,4},{4,6},{6,0},{1,3},{3,5},{5,7},{7,1},{8,10},{10,12},{12... | collective-permute-start | bytes 786440 | tf_op jit(solution)/shard_map/ppermute | solution.py:192
  13.2 7.6 %collective-permute-start.8 = (bf16[2,256,128]{2,1,0:T(8,128)(2,1)S(1)}, bf16[2,256,128]{2,1,0:T(8,128)(2,1)S(1)}, u32[]{:S(2)}, u32[]{:S(2)}) collective-permute-start(bf16[2,256,128]{2,1,0:T(8,128)(2,1)S(1)} %get-tuple-element.40), channel_id=1, source_target_pairs={{0,24},{8,0},{16,8},{24,16},{1,25},{9,1},{17,9},{25,17},{2,26},{10... | collective-permute-start | bytes 393224 | tf_op jit(solution)/shard_map/ppermute | solution.py:192
  16.7 6.0 %collective-permute-start.7 = (bf16[2,256,128]{2,1,0:T(8,128)(2,1)S(1)}, bf16[2,256,128]{2,1,0:T(8,128)(2,1)S(1)}, u32[]{:S(2)}, u32[]{:S(2)}) collective-permute-start(bf16[2,256,128]{2,1,0:T(8,128)(2,1)S(1)} %get-tuple-element.37), channel_id=1, source_target_pairs={{0,8},{8,16},{16,24},{24,0},{1,9},{9,17},{17,25},{25,1},{2,10},{10... | collective-permute-start | bytes 393224 | tf_op jit(solution)/shard_map/ppermute | solution.py:192
  16.9 5.8 %collective-permute-start.4 = (bf16[2,256,128]{2,1,0:T(8,128)(2,1)S(1)}, bf16[2,256,128]{2,1,0:T(8,128)(2,1)S(1)}, u32[]{:S(2)}, u32[]{:S(2)}) collective-permute-start(bf16[2,256,128]{2,1,0:T(8,128)(2,1)S(1)} %get-tuple-element.46), channel_id=1, source_target_pairs={{0,6},{2,0},{4,2},{6,4},{1,7},{3,1},{5,3},{7,5},{8,14},{10,8},{12,... | collective-permute-start | bytes 393224 | tf_op jit(solution)/shard_map/ppermute | solution.py:192
  20.8 5.1 %collective-permute-start.3 = (bf16[2,256,128]{2,1,0:T(8,128)(2,1)S(1)}, bf16[2,256,128]{2,1,0:T(8,128)(2,1)S(1)}, u32[]{:S(2)}, u32[]{:S(2)}) collective-permute-start(bf16[2,256,128]{2,1,0:T(8,128)(2,1)S(1)} %get-tuple-element.43), channel_id=1, source_target_pairs={{0,2},{2,4},{4,6},{6,0},{1,3},{3,5},{5,7},{7,1},{8,10},{10,12},{12... | collective-permute-start | bytes 393224 | tf_op jit(solution)/shard_map/ppermute | solution.py:192
  20.9 15.1 %copy-start.1 = (bf16[4,2,256,128]{3,2,1,0:T(8,128)(2,1)}, bf16[4,2,256,128]{3,2,1,0:T(8,128)(2,1)S(1)}, u32[]{:S(2)}) copy-start(bf16[4,2,256,128]{3,2,1,0:T(8,128)(2,1)S(1)} %pad_maximum_fusion.4.rest_12_) | copy-start | bytes 1572868
  22.7 3.3 %copy-start.28 = (bf16[8192,16]{0,1:T(8,128)(2,1)S(1)}, bf16[8192,16]{0,1:T(8,128)(2,1)}, u32[]{:S(2)}) copy-start(bf16[8192,16]{0,1:T(8,128)(2,1)} %param.17) | copy-start | bytes 786436
  22.8 28.5 %copy-start.3 = (bf16[4,2,256,128]{3,2,1,0:T(8,128)(2,1)}, bf16[4,2,256,128]{3,2,1,0:T(8,128)(2,1)S(1)}, u32[]{:S(2)}) copy-start(bf16[4,2,256,128]{3,2,1,0:T(8,128)(2,1)S(1)} %copy.37.rest_4_) | copy-start | bytes 1572868
  22.8 3.8 %copy-start.23 = (bf16[1,128,8192]{2,1,0:T(8,128)(2,1)S(1)}, bf16[1,128,8192]{2,1,0:T(8,128)(2,1)}, u32[]{:S(2)}) copy-start(bf16[1,128,8192]{2,1,0:T(8,128)(2,1)} %param.13) | copy-start | bytes 6291460
  22.8 3.8 %copy-start.24 = (bf16[16,8192]{1,0:T(8,128)(2,1)S(1)}, bf16[16,8192]{1,0:T(8,128)(2,1)}, u32[]{:S(2)}) copy-start(bf16[16,8192]{1,0:T(8,128)(2,1)} %param.18) | copy-start | bytes 786436
  22.9 13.4 %copy-start.5 = (bf16[4,2,256,128]{3,2,1,0:T(8,128)(2,1)}, bf16[4,2,256,128]{3,2,1,0:T(8,128)(2,1)S(1)}, u32[]{:S(2)}) copy-start(bf16[4,2,256,128]{3,2,1,0:T(8,128)(2,1)S(1)} %pad_maximum_fusion.3.rest_8_) | copy-start | bytes 1572868
  25.9 35.8 %copy-start.7 = (bf16[4,2,256,128]{3,2,1,0:T(8,128)(2,1)}, bf16[4,2,256,128]{3,2,1,0:T(8,128)(2,1)S(1)}, u32[]{:S(2)}) copy-start(bf16[4,2,256,128]{3,2,1,0:T(8,128)(2,1)S(1)} %pad_maximum_fusion.1.rest_0_) | copy-start | bytes 1572868
  27.4 1.3 copy-start.21
  28.7 1.6 copy-start.27
  30.3 48.9 %copy-start.31 = (s32[64]{0:T(128)S(1)}, s32[64]{0:T(128)}, u32[]{:S(2)}) copy-start(s32[64]{0:T(128)} %param.22) | copy-start | bytes 772
  31.9 60.9 %collective-permute-start.9 = (bf16[2,128,4096]{2,1,0:T(8,128)(2,1)}, bf16[2,128,4096]{2,1,0:T(8,128)(2,1)}, u32[]{:S(2)}, u32[]{:S(2)}) collective-permute-start(bf16[2,128,4096]{2,1,0:T(8,128)(2,1)} %pad_maximum_fusion), channel_id=1, source_target_pairs={{0,1},{1,0},{2,3},{3,2},{4,5},{5,4},{6,7},{7,6},{8,9},{9,8},{10,11... | collective-permute-start | bytes 6291464 | tf_op jit(solution)/shard_map/ppermute | solution.py:196
  34.8 13.5 %collective-permute-start.20 = (bf16[4,2,256,128]{3,2,1,0:T(8,128)(2,1)S(1)}, bf16[4,2,256,128]{3,2,1,0:T(8,128)(2,1)S(1)}, u32[]{:S(2)}, u32[]{:S(2)}) collective-permute-start(bf16[4,2,256,128]{3,2,1,0:T(8,128)(2,1)S(1)} %pad_maximum_fusion.4.rest_12_), channel_id=1, source_target_pairs={{0,6},{2,0},{4,2},{6,4},{1,7},{3,1},{5,3},{7,5},{8,14},{10,8},{12,... | collective-permute-start | bytes 1572872 | tf_op jit(solution)/shard_map/ppermute | solution.py:192
  36.0 15.3 %collective-permute-start.19 = (bf16[4,2,256,128]{3,2,1,0:T(8,128)(2,1)S(1)}, bf16[4,2,256,128]{3,2,1,0:T(8,128)(2,1)S(1)}, u32[]{:S(2)}, u32[]{:S(2)}) collective-permute-start(bf16[4,2,256,128]{3,2,1,0:T(8,128)(2,1)S(1)} %pad_maximum_fusion.4.rest_12_), channel_id=1, source_target_pairs={{0,2},{2,4},{4,6},{6,0},{1,3},{3,5},{5,7},{7,1},{8,10},{10,12},{12... | collective-permute-start | bytes 1572872 | tf_op jit(solution)/shard_map/ppermute | solution.py:192
  36.3 25.4 %collective-permute-start.16 = (bf16[4,2,256,128]{3,2,1,0:T(8,128)(2,1)S(1)}, bf16[4,2,256,128]{3,2,1,0:T(8,128)(2,1)S(1)}, u32[]{:S(2)}, u32[]{:S(2)}) collective-permute-start(bf16[4,2,256,128]{3,2,1,0:T(8,128)(2,1)S(1)} %pad_maximum_fusion.3.rest_8_), channel_id=1, source_target_pairs={{0,2},{2,4},{4,6},{6,0},{1,3},{3,5},{5,7},{7,1},{8,10},{10,12},{12... | collective-permute-start | bytes 1572872 | tf_op jit(solution)/shard_map/ppermute | solution.py:192
  36.3 25.4 %collective-permute-start.17 = (bf16[4,2,256,128]{3,2,1,0:T(8,128)(2,1)S(1)}, bf16[4,2,256,128]{3,2,1,0:T(8,128)(2,1)S(1)}, u32[]{:S(2)}, u32[]{:S(2)}) collective-permute-start(bf16[4,2,256,128]{3,2,1,0:T(8,128)(2,1)S(1)} %pad_maximum_fusion.3.rest_8_), channel_id=1, source_target_pairs={{0,6},{2,0},{4,2},{6,4},{1,7},{3,1},{5,3},{7,5},{8,14},{10,8},{12,... | collective-permute-start | bytes 1572872 | tf_op jit(solution)/shard_map/ppermute | solution.py:192
  48.3 13.4 %copy-start.11 = (bf16[4,2,256,128]{3,2,1,0:T(8,128)(2,1)}, bf16[4,2,256,128]{3,2,1,0:T(8,128)(2,1)S(1)}, u32[]{:S(2)}) copy-start(bf16[4,2,256,128]{3,2,1,0:T(8,128)(2,1)S(1)} %collective-permute-done.20.rest_14_) | copy-start | bytes 1572868
  48.3 18.9 %collective-permute-start.14 = (bf16[4,2,256,128]{3,2,1,0:T(8,128)(2,1)S(1)}, bf16[4,2,256,128]{3,2,1,0:T(8,128)(2,1)}, u32[]{:S(2)}, u32[]{:S(2)}) collective-permute-start(bf16[4,2,256,128]{3,2,1,0:T(8,128)(2,1)S(1)} %copy.37.rest_4_), channel_id=1, source_target_pairs={{0,24},{8,0},{16,8},{24,16},{1,25},{9,1},{17,9},{25,17},{2,26},{10... | collective-permute-start | bytes 1572872 | tf_op jit(solution)/shard_map/ppermute | solution.py:192
  52.1 15.2 %collective-permute-start.13 = (bf16[4,2,256,128]{3,2,1,0:T(8,128)(2,1)S(1)}, bf16[4,2,256,128]{3,2,1,0:T(8,128)(2,1)}, u32[]{:S(2)}, u32[]{:S(2)}) collective-permute-start(bf16[4,2,256,128]{3,2,1,0:T(8,128)(2,1)S(1)} %copy.37.rest_4_), channel_id=1, source_target_pairs={{0,8},{8,16},{16,24},{24,0},{1,9},{9,17},{17,25},{25,1},{2,10},{10... | collective-permute-start | bytes 1572872 | tf_op jit(solution)/shard_map/ppermute | solution.py:192
  61.7 15.5 %collective-permute-start.10 = (bf16[4,2,256,128]{3,2,1,0:T(8,128)(2,1)S(1)}, bf16[4,2,256,128]{3,2,1,0:T(8,128)(2,1)}, u32[]{:S(2)}, u32[]{:S(2)}) collective-permute-start(bf16[4,2,256,128]{3,2,1,0:T(8,128)(2,1)S(1)} %pad_maximum_fusion.1.rest_0_), channel_id=1, source_target_pairs={{0,8},{8,16},{16,24},{24,0},{1,9},{9,17},{17,25},{25,1},{2,10},{10... | collective-permute-start | bytes 1572872 | tf_op jit(solution)/shard_map/ppermute | solution.py:192
  63.4 15.3 %collective-permute-start.11 = (bf16[4,2,256,128]{3,2,1,0:T(8,128)(2,1)S(1)}, bf16[4,2,256,128]{3,2,1,0:T(8,128)(2,1)}, u32[]{:S(2)}, u32[]{:S(2)}) collective-permute-start(bf16[4,2,256,128]{3,2,1,0:T(8,128)(2,1)S(1)} %pad_maximum_fusion.1.rest_0_), channel_id=1, source_target_pairs={{0,24},{8,0},{16,8},{24,16},{1,25},{9,1},{17,9},{25,17},{2,26},{10... | collective-permute-start | bytes 1572872 | tf_op jit(solution)/shard_map/ppermute | solution.py:192
  67.2 12.6 %collective-permute-start.21 = (bf16[4,2,256,128]{3,2,1,0:T(8,128)(2,1)}, bf16[4,2,256,128]{3,2,1,0:T(8,128)(2,1)}, u32[]{:S(2)}, u32[]{:S(2)}) collective-permute-start(bf16[4,2,256,128]{3,2,1,0:T(8,128)(2,1)} %copy-done.11), channel_id=1, source_target_pairs={{0,6},{2,0},{4,2},{6,4},{1,7},{3,1},{5,3},{7,5},{8,14},{10,8},{12,... | collective-permute-start | bytes 1572872 | tf_op jit(solution)/shard_map/ppermute | solution.py:192
  67.3 14.6 %collective-permute-start.18 = (bf16[4,2,256,128]{3,2,1,0:T(8,128)(2,1)}, bf16[4,2,256,128]{3,2,1,0:T(8,128)(2,1)}, u32[]{:S(2)}, u32[]{:S(2)}) collective-permute-start(bf16[4,2,256,128]{3,2,1,0:T(8,128)(2,1)} %copy-done.15), channel_id=1, source_target_pairs={{0,2},{2,4},{4,6},{6,0},{1,3},{3,5},{5,7},{7,1},{8,10},{10,12},{12... | collective-permute-start | bytes 1572872 | tf_op jit(solution)/shard_map/ppermute | solution.py:192
  77.2 12.1 %collective-permute-start.15 = (bf16[4,2,256,128]{3,2,1,0:T(8,128)(2,1)}, bf16[4,2,256,128]{3,2,1,0:T(8,128)(2,1)}, u32[]{:S(2)}, u32[]{:S(2)}) collective-permute-start(bf16[4,2,256,128]{3,2,1,0:T(8,128)(2,1)} %collective-permute-done.14.rest_6_), channel_id=1, source_target_pairs={{0,24},{8,0},{16,8},{24,16},{1,25},{9,1},{17,9},{25,17},{2,26},{10... | collective-permute-start | bytes 1572872 | tf_op jit(solution)/shard_map/ppermute | solution.py:192
  78.6 13.4 %collective-permute-start.12 = (bf16[4,2,256,128]{3,2,1,0:T(8,128)(2,1)}, bf16[4,2,256,128]{3,2,1,0:T(8,128)(2,1)S(1)}, u32[]{:S(2)}, u32[]{:S(2)}) collective-permute-start(bf16[4,2,256,128]{3,2,1,0:T(8,128)(2,1)} %collective-permute-done.10.rest_1_), channel_id=1, source_target_pairs={{0,8},{8,16},{16,24},{24,0},{1,9},{9,17},{17,25},{25,1},{2,10},{10... | collective-permute-start | bytes 1572872 | tf_op jit(solution)/shard_map/ppermute | solution.py:192
  79.7 83.5 %collective-permute-start.23 = (bf16[128,16]{0,1:T(8,128)(2,1)S(1)}, bf16[128,16]{0,1:T(8,128)(2,1)S(1)}, u32[]{:S(2)}, u32[]{:S(2)}) collective-permute-start(bf16[128,16]{0,1:T(8,128)(2,1)S(1)} %convolution_convert_fusion), channel_id=1, source_target_pairs={{0,1},{1,0},{2,3},{3,2},{4,5},{5,4},{6,7},{7,6},{8,9},{9,8},{10,11... | collective-permute-start | bytes 12296 | tf_op jit(solution)/shard_map/ppermute | solution.py:196
  92.8 1.0 copy-start.2
  93.9 1.0 copy-start.4
  94.9 1.0 copy-start.6
  96.0 1.0 copy-start.8
  97.0 1.0 copy-start.12
  98.1 1.0 copy-start.14
  153.6 10.6 %copy-start.9 = (bf16[128,4096]{1,0:T(8,128)(2,1)}, bf16[128,4096]{1,0:T(8,128)(2,1)S(1)}, u32[]{:S(2)}) copy-start(bf16[128,4096]{1,0:T(8,128)(2,1)S(1)} %get-tuple-element.14) | copy-start | bytes 3145732
  154.0 10.2 %collective-permute-start.24 = (f32[128,16]{0,1:T(8,128)S(1)}, f32[128,16]{0,1:T(8,128)S(1)}, u32[]{:S(2)}, u32[]{:S(2)}) collective-permute-start(f32[128,16]{0,1:T(8,128)S(1)} %fusion.21), channel_id=1, source_target_pairs={{0,1},{1,0},{2,3},{3,2},{4,5},{5,4},{6,7},{7,6},{8,9},{9,8},{10,11... | collective-permute-start | bytes 24584 | tf_op jit(solution)/shard_map/ppermute | solution.py:196
  166.7 1.5 collective-permute-start.25
  168.2 1.1 copy-start.22
  170.0 31.9 %copy-start.10 = (bf16[128,4096]{1,0:T(8,128)(2,1)S(1)}, bf16[128,4096]{1,0:T(8,128)(2,1)}, u32[]{:S(2)}) copy-start(bf16[128,4096]{1,0:T(8,128)(2,1)} %copy-done.9) | copy-start | bytes 3145732
  170.0 6.7 %collective-permute-start.26 = (bf16[32,1024]{1,0:T(8,128)(2,1)}, bf16[32,1024]{1,0:T(8,128)(2,1)}, u32[]{:S(2)}, u32[]{:S(2)}) collective-permute-start(bf16[32,1024]{1,0:T(8,128)(2,1)} %get-tuple-element.25), channel_id=1, source_target_pairs={{0,2},{2,4},{4,6},{6,0},{1,3},{3,5},{5,7},{7,1},{8,10},{10,12},{12... | collective-permute-start | bytes 196616 | tf_op jit(solution)/shard_map/ppermute | solution.py:192
  170.0 6.7 %collective-permute-start.27 = (bf16[32,1024]{1,0:T(8,128)(2,1)S(1)}, bf16[32,1024]{1,0:T(8,128)(2,1)}, u32[]{:S(2)}, u32[]{:S(2)}) collective-permute-start(bf16[32,1024]{1,0:T(8,128)(2,1)S(1)} %get-tuple-element.26), channel_id=1, source_target_pairs={{0,4},{2,6},{4,0},{6,2},{1,5},{3,7},{5,1},{7,3},{8,12},{10,14},{12... | collective-permute-start | bytes 196616 | tf_op jit(solution)/shard_map/ppermute | solution.py:192
  171.4 5.2 %collective-permute-start.28 = (bf16[32,1024]{1,0:T(8,128)(2,1)S(1)}, bf16[32,1024]{1,0:T(8,128)(2,1)}, u32[]{:S(2)}, u32[]{:S(2)}) collective-permute-start(bf16[32,1024]{1,0:T(8,128)(2,1)S(1)} %get-tuple-element.27), channel_id=1, source_target_pairs={{0,6},{2,0},{4,2},{6,4},{1,7},{3,1},{5,3},{7,5},{8,14},{10,8},{12,... | collective-permute-start | bytes 196616 | tf_op jit(solution)/shard_map/ppermute | solution.py:192
  177.7 4.8 %collective-permute-start.29 = (bf16[32,1024]{1,0:T(8,128)(2,1)S(1)}, bf16[32,1024]{1,0:T(8,128)(2,1)S(1)}, u32[]{:S(2)}, u32[]{:S(2)}) collective-permute-start(bf16[32,1024]{1,0:T(8,128)(2,1)S(1)} %fusion.16), channel_id=1, source_target_pairs={{0,16},{8,24},{16,0},{24,8},{1,17},{9,25},{17,1},{25,9},{2,18},{10... | collective-permute-start | bytes 196616 | tf_op jit(solution)/shard_map/ppermute | solution.py:192
  177.8 5.1 %collective-permute-start.30 = (bf16[32,1024]{1,0:T(8,128)(2,1)S(1)}, bf16[32,1024]{1,0:T(8,128)(2,1)S(1)}, u32[]{:S(2)}, u32[]{:S(2)}) collective-permute-start(bf16[32,1024]{1,0:T(8,128)(2,1)S(1)} %fusion.16), channel_id=1, source_target_pairs={{0,8},{8,16},{16,24},{24,0},{1,9},{9,17},{17,25},{25,1},{2,10},{10... | collective-permute-start | bytes 196616 | tf_op jit(solution)/shard_map/ppermute | solution.py:192
  178.8 4.1 %collective-permute-start.31 = (bf16[32,1024]{1,0:T(8,128)(2,1)S(1)}, bf16[32,1024]{1,0:T(8,128)(2,1)S(1)}, u32[]{:S(2)}, u32[]{:S(2)}) collective-permute-start(bf16[32,1024]{1,0:T(8,128)(2,1)S(1)} %fusion.16), channel_id=1, source_target_pairs={{0,24},{8,0},{16,8},{24,16},{1,25},{9,1},{17,9},{25,17},{2,26},{10... | collective-permute-start | bytes 196616 | tf_op jit(solution)/shard_map/ppermute | solution.py:192
  182.9 5.5 %collective-permute-start.32 = (bf16[32,1024]{1,0:T(8,128)(2,1)S(1)}, bf16[32,1024]{1,0:T(8,128)(2,1)S(1)}, u32[]{:S(2)}, u32[]{:S(2)}) collective-permute-start(bf16[32,1024]{1,0:T(8,128)(2,1)S(1)} %add_convert_fusion.1), channel_id=1, source_target_pairs={{0,64},{32,96},{64,0},{96,32},{1,65},{33,97},{65,1},{97,33},{2,66}... | collective-permute-start | bytes 196616 | tf_op jit(solution)/shard_map/ppermute | solution.py:192
  185.8 5.0 %collective-permute-start.33 = (bf16[32,1024]{1,0:T(8,128)(2,1)S(1)}, bf16[32,1024]{1,0:T(8,128)(2,1)S(1)}, u32[]{:S(2)}, u32[]{:S(2)}) collective-permute-start(bf16[32,1024]{1,0:T(8,128)(2,1)S(1)} %add_convert_fusion.1), channel_id=1, source_target_pairs={{0,32},{32,64},{64,96},{96,0},{1,33},{33,65},{65,97},{97,1},{2,34}... | collective-permute-start | bytes 196616 | tf_op jit(solution)/shard_map/ppermute | solution.py:192
  186.1 4.7 %collective-permute-start.34 = (bf16[32,1024]{1,0:T(8,128)(2,1)S(1)}, bf16[32,1024]{1,0:T(8,128)(2,1)S(1)}, u32[]{:S(2)}, u32[]{:S(2)}) collective-permute-start(bf16[32,1024]{1,0:T(8,128)(2,1)S(1)} %add_convert_fusion.1), channel_id=1, source_target_pairs={{0,96},{32,0},{64,32},{96,64},{1,97},{33,1},{65,33},{97,65},{2,98}... | collective-permute-start | bytes 196616 | tf_op jit(solution)/shard_map/ppermute | solution.py:192
  190.9 4.7 %collective-permute-start.35 = (bf16[32,1024]{1,0:T(8,128)(2,1)S(1)}, bf16[32,1024]{1,0:T(8,128)(2,1)S(1)}, u32[]{:S(2)}, u32[]{:S(2)}) collective-permute-start(bf16[32,1024]{1,0:T(8,128)(2,1)S(1)} %add_convert_fusion), channel_id=1, source_target_pairs={{0,4},{2,6},{4,0},{6,2},{1,5},{3,7},{5,1},{7,3},{8,12},{10,14},{12... | collective-permute-start | bytes 196616 | tf_op jit(solution)/shard_map/ppermute | solution.py:192
  191.6 4.7 %collective-permute-start.36 = (bf16[32,1024]{1,0:T(8,128)(2,1)S(1)}, bf16[32,1024]{1,0:T(8,128)(2,1)S(1)}, u32[]{:S(2)}, u32[]{:S(2)}) collective-permute-start(bf16[32,1024]{1,0:T(8,128)(2,1)S(1)} %add_convert_fusion), channel_id=1, source_target_pairs={{0,2},{2,4},{4,6},{6,0},{1,3},{3,5},{5,7},{7,1},{8,10},{10,12},{12... | collective-permute-start | bytes 196616 | tf_op jit(solution)/shard_map/ppermute | solution.py:192
  194.3 3.1 %collective-permute-start.37 = (bf16[32,1024]{1,0:T(8,128)(2,1)S(1)}, bf16[32,1024]{1,0:T(8,128)(2,1)S(1)}, u32[]{:S(2)}, u32[]{:S(2)}) collective-permute-start(bf16[32,1024]{1,0:T(8,128)(2,1)S(1)} %add_convert_fusion), channel_id=1, source_target_pairs={{0,6},{2,0},{4,2},{6,4},{1,7},{3,1},{5,3},{7,5},{8,14},{10,8},{12,... | collective-permute-start | bytes 196616 | tf_op jit(solution)/shard_map/ppermute | solution.py:192
  197.5 5.7 %copy-start.25 = (f32[16,8192]{1,0:T(8,128)S(1)}, f32[16,8192]{1,0:T(8,128)}, u32[]{:S(2)}) copy-start(f32[16,8192]{1,0:T(8,128)} %param.20) | copy-start | bytes 1572868
  197.6 5.4 %collective-permute-start.38 = (bf16[32,4096]{1,0:T(8,128)(2,1)S(1)}, bf16[32,4096]{1,0:T(8,128)(2,1)S(1)}, u32[]{:S(2)}, u32[]{:S(2)}) collective-permute-start(bf16[32,4096]{1,0:T(8,128)(2,1)S(1)} %pad_maximum_fusion.8), channel_id=1, source_target_pairs={{0,1},{1,0},{2,3},{3,2},{4,5},{5,4},{6,7},{7,6},{8,9},{9,8},{10,11... | collective-permute-start | bytes 786440 | tf_op jit(solution)/shard_map/ppermute | solution.py:196
  201.9 3.1 %collective-permute-start.22 = (bf16[128,4096]{1,0:T(8,128)(2,1)S(1)}, bf16[128,4096]{1,0:T(8,128)(2,1)S(1)}, u32[]{:S(2)}, u32[]{:S(2)}) collective-permute-start(bf16[128,4096]{1,0:T(8,128)(2,1)S(1)} %copy-done.10), channel_id=1, source_target_pairs={{0,1},{1,0},{2,3},{3,2},{4,5},{5,4},{6,7},{7,6},{8,9},{9,8},{10,11... | collective-permute-start | bytes 3145736 | tf_op jit(solution)/shard_map/ppermute | solution.py:196
  203.1 1.0 copy-start.26
  203.2 1.8 copy-start.29
  205.2 1.3 copy-start.30
  (7 other events, 6.3 us)
